TPU v7x, 32 devices: a whole 2x2x4 slice. The times are simulated.
32 devices in a mesh: head: 2 (over y), blk: 16 (over z, x, core).
Axes of the slice: x: 2, y: 2, z: 4, core: 2. Of those that a mesh axis runs over, the one named last changes fastest.
Arguments:
- tokens: bfloat16 [4, 1024, 768], P('head', 'blk'), may hold values from -6 to 6
- previous_layer_logits: float32 [4, 1024, 12], P('head', 'blk'), may hold values from -6 to 6
- lengths: int32 [4], replicated, may hold values from 256 to 1024, as said below
- routes: int32 [4, 1024, 2], P('head', 'blk'), may hold values from 0 to 11, all different within a row
- pair_order: int32 [4, 1024, 2], P('head', 'blk'), may hold values from 0 to 255, as said below
- gain_attn: bfloat16 [768], P('blk'), may hold values from 0.5 to 1.5
- w_qkv: bfloat16 [768, 3, 768], P('blk', None, 'head'), may hold values from -0.21875 to 0.21875
- w_out: bfloat16 [768, 768], P('blk', 'head'), may hold values from -1.75 to 1.75
- gain_ffn: bfloat16 [768], P('blk'), may hold values from 0.5 to 1.5
- w_router: bfloat16 [768, 12], P('blk'), may hold values from -0.109375 to 0.109375
- w_residual: float32 [12, 12], replicated, may hold values from -0.875 to 0.875
- w_const: bfloat16 [768, 4], P('blk'), may hold values from -0.21875 to 0.21875
- const_vec: bfloat16 [768, 2], P('blk'), may hold values from -6 to 6
- w_in: bfloat16 [768, 8, 2, 2048], P(None, 'head', None, 'blk'), may hold values from -0.21875 to 0.21875
- w_down: bfloat16 [2048, 8, 768], P('blk', 'head'), may hold values from -0.125 to 0.125
- cotangent: float32 [4, 1024, 768], P('head', 'blk'), may hold values from -6 to 6
Outputs:
- output: float32 [4, 1024, 768], P('head', 'blk')
- grad_tokens: float32 [4, 1024, 768], P('head', 'blk')
- grad_gain_attn: float32 [768], P('blk')
- grad_w_qkv: float32 [768, 3, 768], P('blk', None, 'head')
- grad_w_out: float32 [768, 768], P('blk', 'head')
- grad_gain_ffn: float32 [768], P('blk')
- grad_w_router: float32 [768, 12], P('blk')
- grad_w_residual: float32 [12, 12], replicated
- grad_w_const: float32 [768, 4], P('blk')
- grad_const_vec: float32 [768, 2], P('blk')
- grad_w_in: float32 [768, 8, 2, 2048], P(None, 'head', None, 'blk')
- grad_w_down: float32 [2048, 8, 768], P('blk', 'head')
Inputs may be any that keep to these rules, and one draw needn't show every extreme that they name: `lengths`: one sequence in every draw has all 1024 slots valid. `routes`: each token names two different experts: 0 to 7 feed-forward, 8 zero, 9 copy, 10 and 11 constant. `pair_order`: within each block (h, b) the values are a permutation of 0 to 255.
All inputs are finite; a program needn't handle non-finite values.
Results may differ from a plain program's by a relative error of at most 0.02.
Values may be sent and summed in bfloat16 or wider, within the bound.
No kernel may reach another device: no remote copies, remote signals or barrier semaphores. Data moves between devices by JAX's collectives and lax.ppermute only.
A program may use at most 256 MiB of HBM per device.

v0:
```python
import math

import jax
import jax.numpy as jnp
from jax import lax
from jax.sharding import PartitionSpec as P

HD = 64
NEXP = 8


EPS_NORM = 1e-05
NEG_BIG = -1e30


def rotate_half(values):
    half_width = values.shape[-1] // 2
    return jnp.concatenate([-values[..., half_width:], values[..., :half_width]], axis=-1)


def rotate_back(values):
    half_width = values.shape[-1] // 2
    return jnp.concatenate([values[..., half_width:], -values[..., :half_width]], axis=-1)


def rotary_tables(positions, head_dim):
    frequency = 10000.0 ** (-(2.0 * jnp.arange(head_dim // 2, dtype=jnp.float32)) / head_dim)
    angles = positions.astype(jnp.float32)[:, None] * frequency[None, :]
    angles = jnp.concatenate([angles, angles], axis=-1)
    return (jnp.cos(angles), jnp.sin(angles))


def apply_rotary(values, cosine, sine_tab):
    return values * cosine + rotate_half(values) * sine_tab


def place_pairs(route_pairs, order_pairs, valid_pairs, n_ffn, capacity):
    n_pairs = route_pairs.shape[0]
    eligible = valid_pairs & (route_pairs < n_ffn)
    inverse = (
        jnp.zeros((n_pairs,), jnp.int32).at[order_pairs].set(jnp.arange(n_pairs, dtype=jnp.int32))
    )
    sorted_route = route_pairs[inverse]
    sorted_elig = eligible[inverse]
    onehot = (
        (sorted_route[:, None] == jnp.arange(n_ffn, dtype=jnp.int32)[None, :])
        & sorted_elig[:, None]
    ).astype(jnp.int32)
    running = jnp.cumsum(onehot, axis=0, dtype=jnp.int32) - onehot
    rank_sorted = jnp.sum(running * onehot, axis=1, dtype=jnp.int32)
    rank_pos = rank_sorted[order_pairs]
    kept_pair = eligible & (rank_pos < capacity)
    slot_index = jnp.where(kept_pair, route_pairs * capacity + rank_pos, n_ffn * capacity)
    source = (
        jnp.full((n_ffn * capacity + 1,), n_pairs, jnp.int32)
        .at[slot_index]
        .set(jnp.arange(n_pairs, dtype=jnp.int32))
    )
    return (slot_index, source[: n_ffn * capacity])


def causal_mask(query_pos, key_pos, lengths):
    allowed = (key_pos[None, None, :] <= query_pos[None, :, None]) & (
        key_pos[None, None, :] < lengths[:, None, None]
    )
    return allowed[:, None]


def keep_state(state_in):
    return state_in


def gather_layer(w_qkv, w_out, gain_attn, gain_ffn, w_router, w_const, const_vec):
    return (
        lax.all_gather(w_qkv, "blk", axis=0, tiled=True),
        lax.all_gather(w_out, "blk", axis=0, tiled=True),
        lax.all_gather(gain_attn, "blk", axis=0, tiled=True),
        lax.all_gather(gain_ffn, "blk", axis=0, tiled=True),
        lax.all_gather(w_router, "blk", axis=0, tiled=True),
        lax.all_gather(w_const, "blk", axis=0, tiled=True),
        lax.all_gather(const_vec, "blk", axis=0, tiled=True),
    )


def gather_experts(w_in, w_down):
    return (
        lax.all_gather(w_in, "blk", axis=3, tiled=True),
        lax.all_gather(w_down, "blk", axis=0, tiled=True),
    )


def head_rows(rows_in):
    return lax.all_gather(rows_in, "head", axis=0, tiled=True)


def head_scatter(term_fn, row_count):
    return lax.psum_scatter(
        term_fn(jnp.int32(0), row_count * lax.axis_size("head")).astype(jnp.bfloat16),
        "head",
        scatter_dimension=0,
        tiled=True,
    ).astype(jnp.float32)


def to_experts(rows_in):
    return lax.all_to_all(rows_in, "head", split_axis=0, concat_axis=1, tiled=True)


def from_experts(rows_in):
    return lax.all_to_all(rows_in, "head", split_axis=1, concat_axis=0, tiled=True)


def sum_pair(first_term, second_term):
    return (
        lax.psum_scatter(first_term, "blk", scatter_dimension=0, tiled=True),
        lax.psum_scatter(second_term, "blk", scatter_dimension=0, tiled=True),
    )


def finish_experts(in_term, down_term):
    summed = sum_pair(in_term, down_term)
    return (jnp.transpose(summed[0], (1, 2, 3, 0)), summed[1])


def swiglu_back(grad_hidden, gate_part, up_part):
    sigmoid_g = jax.nn.sigmoid(gate_part)
    grad_gate_part = grad_hidden * up_part * sigmoid_g * (1.0 + gate_part * (1.0 - sigmoid_g))
    grad_up_part = grad_hidden * jax.nn.silu(gate_part)
    return jnp.stack([grad_gate_part, grad_up_part], axis=2).astype(jnp.bfloat16)


def per_device(
    tokens,
    previous_layer_logits,
    lengths,
    routes,
    pair_order,
    gain_attn,
    w_qkv,
    w_out,
    gain_ffn,
    w_router,
    w_residual,
    w_const,
    const_vec,
    w_in,
    w_down,
    cotangent,
):
    seq_dev, slot_dev, model_width = tokens.shape
    n_all = previous_layer_logits.shape[2]
    heads_here = w_qkv.shape[2] // HD
    tok_count = seq_dev * slot_dev
    capacity = 9 * 2 * tok_count // (8 * n_all)
    head_part = lax.axis_index("head")
    blk_part = lax.axis_index("blk")
    score_scale = 1.0 / math.sqrt(HD)
    layer_full = gather_layer(w_qkv, w_out, gain_attn, gain_ffn, w_router, w_const, const_vec)
    query_key_value_whole, out_full, gain_one, gain_two, router_full, const_full, vector_full = (
        layer_full
    )
    expert_full = gather_experts(w_in, w_down)
    token_broadcast = tokens.astype(jnp.float32)
    first_inverse_deviation = lax.rsqrt(
        jnp.mean(token_broadcast * token_broadcast, axis=-1, keepdims=True) + EPS_NORM
    )
    first_input_centered = token_broadcast * first_inverse_deviation
    first_normalized = (
        token_broadcast * first_inverse_deviation * gain_one.astype(jnp.float32)
    ).astype(jnp.bfloat16)
    normalized_every = head_rows(first_normalized)
    n_seq = normalized_every.shape[0]
    query_key_value_plain = jnp.einsum(
        "owj,jtm->owtm", normalized_every, query_key_value_whole, preferred_element_type=jnp.float32
    )
    qkv_heads = query_key_value_plain.reshape(n_seq, slot_dev, 3, heads_here, HD)
    positions = blk_part * slot_dev + jnp.arange(slot_dev, dtype=jnp.int32)
    first_pos = blk_part * slot_dev
    last_pos = first_pos + slot_dev - 1
    cosine, sine_tab = rotary_tables(positions, HD)
    cos_wide = cosine[None, :, None, :]
    sin_wide = sine_tab[None, :, None, :]
    query_rot = apply_rotary(qkv_heads[:, :, 0], cos_wide, sin_wide).astype(jnp.bfloat16)
    key_rot = apply_rotary(qkv_heads[:, :, 1], cos_wide, sin_wide).astype(jnp.bfloat16)
    value_low = qkv_heads[:, :, 2].astype(jnp.bfloat16)
    longest = jnp.max(lengths)
    start_state = (
        jnp.full((n_seq, heads_here, slot_dev), NEG_BIG, jnp.float32),
        jnp.zeros((n_seq, heads_here, slot_dev), jnp.float32),
        jnp.zeros((n_seq, heads_here, slot_dev, HD), jnp.float32),
    )
    key_blk = lax.all_gather(key_rot, "blk", axis=1, tiled=True)
    value_blk = lax.all_gather(value_low, "blk", axis=1, tiled=True)
    n_rows = key_blk.shape[1]
    sub_rows = math.gcd(n_rows, 512)

    def attend_one_step(step_idx, state_now):
        begin_row = step_idx * sub_rows
        key_pos = begin_row + jnp.arange(sub_rows, dtype=jnp.int32)

        def compute(state_in):
            run_max, run_sum, run_acc = state_in
            key_part = lax.dynamic_slice_in_dim(key_blk, step_idx * sub_rows, sub_rows, 1)
            value_part = lax.dynamic_slice_in_dim(value_blk, step_idx * sub_rows, sub_rows, 1)
            scores = (
                jnp.einsum(
                    "sqhd,skhd->shqk", query_rot, key_part, preferred_element_type=jnp.float32
                )
                * score_scale
            )
            allowed = causal_mask(positions, key_pos, lengths)
            scores = jnp.where(allowed, scores, NEG_BIG)
            new_max = jnp.maximum(run_max, jnp.max(scores, axis=-1))
            weights = jnp.where(allowed, jnp.exp(scores - new_max[..., None]), 0.0)
            factor = jnp.exp(run_max - new_max)
            run_sum = run_sum * factor + jnp.sum(weights, axis=-1)
            run_acc = run_acc * factor[..., None] + jnp.einsum(
                "shqk,skhd->shqd",
                weights.astype(jnp.bfloat16),
                value_part,
                preferred_element_type=jnp.float32,
            )
            return (new_max, run_sum, run_acc)

        skip_block = (begin_row > last_pos) | (begin_row >= longest)
        return lax.cond(skip_block, keep_state, compute, state_now)

    run_max, run_sum, run_acc = lax.fori_loop(0, n_rows // sub_rows, attend_one_step, start_state)
    attn_vec = jnp.transpose(run_acc / run_sum[..., None], (0, 2, 1, 3))
    log_sum = run_max + jnp.log(run_sum)
    attn_low = attn_vec.reshape(n_seq, slot_dev, heads_here * HD).astype(jnp.bfloat16)

    def out_rows(offset, amount):
        return jnp.einsum("slc,jc->slj", attn_low, out_full, preferred_element_type=jnp.float32)

    attn_out = head_scatter(out_rows, seq_dev)
    residual_flattened = (token_broadcast + attn_out).reshape(tok_count, model_width)
    second_inverse_deviation = lax.rsqrt(
        jnp.mean(residual_flattened * residual_flattened, axis=-1, keepdims=True) + EPS_NORM
    )
    second_input_centered = residual_flattened * second_inverse_deviation
    gain_two_wide = gain_two.astype(jnp.float32)
    normed_two = residual_flattened * second_inverse_deviation * gain_two_wide
    flat_low = normed_two.astype(jnp.bfloat16)
    flat_prev = previous_layer_logits.reshape(tok_count, n_all)
    route_flat = routes.reshape(tok_count, 2)
    router_scores = jnp.dot(flat_low, router_full, preferred_element_type=jnp.float32) + jnp.dot(
        flat_prev, w_residual, precision=lax.Precision.HIGHEST
    )
    chosen = jnp.take_along_axis(router_scores, route_flat, axis=1)
    gate_probs = jax.nn.softmax(chosen, axis=-1)
    constant_logits = jnp.dot(flat_low, const_full, preferred_element_type=jnp.float32).reshape(
        tok_count, 2, 2
    )
    alpha_mix = jax.nn.softmax(constant_logits, axis=-1)
    vector_wide = vector_full.astype(jnp.float32)
    const_zero = alpha_mix[:, 0, 0:1] * normed_two + alpha_mix[:, 0, 1:2] * vector_wide[:, 0]
    const_one = alpha_mix[:, 1, 0:1] * normed_two + alpha_mix[:, 1, 1:2] * vector_wide[:, 1]
    seq_lengths = lax.dynamic_slice_in_dim(lengths, head_part * seq_dev, seq_dev)
    valid_flat = (positions[None, :] < seq_lengths[:, None]).reshape(tok_count)
    slot_index, source = place_pairs(
        route_flat.reshape(2 * tok_count),
        pair_order.reshape(2 * tok_count),
        jnp.repeat(valid_flat, 2),
        NEXP,
        capacity,
    )
    zero_row = jnp.zeros((1, model_width), jnp.bfloat16)
    dispatch = jnp.concatenate([flat_low, zero_row], axis=0)[source // 2].reshape(
        NEXP, capacity, model_width
    )
    received = to_experts(dispatch)
    in_full, down_full = expert_full
    gate_up = jnp.einsum("ecd,degf->ecgf", received, in_full, preferred_element_type=jnp.float32)
    gate_part = gate_up[:, :, 0]
    up_part = gate_up[:, :, 1]
    hidden = (jax.nn.silu(gate_part) * up_part).astype(jnp.bfloat16)
    expert_out = jnp.einsum(
        "ecf,fed->ecd", hidden, down_full, preferred_element_type=jnp.float32
    ).astype(jnp.bfloat16)
    returned = from_experts(expert_out)
    ret_ext = jnp.concatenate([returned.reshape(NEXP * capacity, model_width), zero_row], axis=0)
    ffn_pairs = ret_ext[slot_index].astype(jnp.float32).reshape(tok_count, 2, model_width)
    route_wide = route_flat[..., None]
    pair_out = (
        jnp.where(route_wide < NEXP, ffn_pairs, 0.0)
        + jnp.where(route_wide == NEXP + 1, normed_two[:, None, :], 0.0)
        + jnp.where(route_wide == NEXP + 2, const_zero[:, None, :], 0.0)
        + jnp.where(route_wide == NEXP + 3, const_one[:, None, :], 0.0)
    )
    mixed_out = jnp.sum(gate_probs[..., None] * pair_out, axis=1)
    valid_col = valid_flat[:, None].astype(jnp.float32)
    output = (valid_col * (residual_flattened + mixed_out)).reshape(seq_dev, slot_dev, model_width)
    back_layer = gather_layer(w_qkv, w_out, gain_attn, gain_ffn, w_router, w_const, const_vec)
    back_experts = gather_experts(w_in, w_down)
    (
        query_key_value_backward,
        out_back,
        gain_one_b,
        gain_two_b,
        router_back,
        const_back,
        vector_back,
    ) = back_layer
    grad_out = valid_col * cotangent.reshape(tok_count, model_width)
    grad_gate = jnp.sum(grad_out[:, None, :] * pair_out, axis=-1)
    grad_pair = gate_probs[..., None] * grad_out[:, None, :]
    pair_ext = jnp.concatenate(
        [grad_pair.reshape(2 * tok_count, model_width).astype(jnp.bfloat16), zero_row], axis=0
    )
    grad_dispatch = pair_ext[source].reshape(NEXP, capacity, model_width)
    grad_recv = to_experts(grad_dispatch)
    in_back, down_back = back_experts
    grad_hidden = jnp.einsum(
        "ecd,fed->ecf", grad_recv, down_back, preferred_element_type=jnp.float32
    )
    grad_gate_up = swiglu_back(grad_hidden, gate_part, up_part)
    down_term = jnp.einsum("ecf,ecd->fed", hidden, grad_recv, preferred_element_type=jnp.float32)
    in_term = jnp.einsum(
        "ecd,ecgf->fdeg", received, grad_gate_up, preferred_element_type=jnp.float32
    )
    grad_rows_e = jnp.einsum(
        "ecgf,degf->ecd", grad_gate_up, in_back, preferred_element_type=jnp.float32
    ).astype(jnp.bfloat16)
    grad_back = from_experts(grad_rows_e)
    back_ext = jnp.concatenate([grad_back.reshape(NEXP * capacity, model_width), zero_row], axis=0)
    back_pairs = back_ext[slot_index].astype(jnp.float32).reshape(tok_count, 2, model_width)

    def routed(route_value):
        return jnp.sum(jnp.where(route_wide == route_value, grad_pair, 0.0), axis=1)

    vector_back_wide = vector_back.astype(jnp.float32)
    const_grads = [routed(NEXP + 2), routed(NEXP + 3)]
    alpha_rows = []
    vector_cols = []
    normalized_gradient = jnp.sum(back_pairs, axis=1) + routed(NEXP + 1)
    for const_idx in range(2):
        grad_const = const_grads[const_idx]
        alpha_rows.append(
            jnp.stack(
                [
                    jnp.sum(grad_const * normed_two, axis=-1),
                    jnp.sum(grad_const * vector_back_wide[:, const_idx], axis=-1),
                ],
                axis=-1,
            )
        )
        vector_cols.append(jnp.sum(alpha_mix[:, const_idx, 1:2] * grad_const, axis=0))
        normalized_gradient = normalized_gradient + alpha_mix[:, const_idx, 0:1] * grad_const
    alpha_grad = jnp.stack(alpha_rows, axis=1)
    vector_term = jnp.stack(vector_cols, axis=1)
    clog_grad = (
        (alpha_mix * (alpha_grad - jnp.sum(alpha_mix * alpha_grad, axis=-1, keepdims=True)))
        .reshape(tok_count, 4)
        .astype(jnp.bfloat16)
    )
    const_term = jnp.einsum("td,tc->dc", flat_low, clog_grad, preferred_element_type=jnp.float32)
    gate_sum = jnp.sum(gate_probs * grad_gate, axis=-1, keepdims=True)
    chosen_grad = gate_probs * (grad_gate - gate_sum)
    columns = jnp.arange(n_all, dtype=jnp.int32)
    logit_grad = jnp.sum(
        chosen_grad[..., None] * (route_flat[..., None] == columns).astype(jnp.float32), axis=1
    ).astype(jnp.bfloat16)
    router_term = jnp.einsum("td,te->de", flat_low, logit_grad, preferred_element_type=jnp.float32)
    resid_term = jnp.einsum(
        "te,tf->ef", flat_prev, logit_grad.astype(jnp.float32), precision=lax.Precision.HIGHEST
    )
    normalized_gradient = (
        normalized_gradient
        + jnp.einsum("tc,dc->td", clog_grad, const_back, preferred_element_type=jnp.float32)
        + jnp.einsum("te,de->td", logit_grad, router_back, preferred_element_type=jnp.float32)
    )
    second_gain_term = jnp.sum(normalized_gradient * second_input_centered, axis=0)
    second_centered = normalized_gradient * gain_two_b.astype(jnp.float32)
    grad_res = grad_out + second_inverse_deviation * (
        second_centered
        - second_input_centered
        * jnp.mean(second_centered * second_input_centered, axis=-1, keepdims=True)
    )
    grad_attn = grad_res.reshape(seq_dev, slot_dev, model_width).astype(jnp.bfloat16)
    grad_attn_all = head_rows(grad_attn)
    out_term = jnp.einsum(
        "slj,slc->jc", grad_attn_all, attn_low, preferred_element_type=jnp.float32
    )
    grad_vec = jnp.einsum(
        "slj,jc->slc", grad_attn_all, out_back, preferred_element_type=jnp.float32
    ).astype(jnp.bfloat16)
    dout_low = grad_vec.reshape(n_seq, slot_dev, heads_here, HD)
    delta_rows = jnp.sum(dout_low.astype(jnp.float32) * attn_vec, axis=-1)
    lse_rows = jnp.transpose(log_sum, (0, 2, 1))
    lse_full, delta_full = (
        lax.all_gather(lse_rows, "blk", axis=1, tiled=True),
        lax.all_gather(delta_rows, "blk", axis=1, tiled=True),
    )
    delta_here = jnp.transpose(delta_rows, (0, 2, 1))
    zero_grad = jnp.zeros((n_seq, slot_dev, heads_here, HD), jnp.float32)
    grad_key_blk = lax.all_gather(key_rot, "blk", axis=1, tiled=True)
    grad_value_blk = lax.all_gather(value_low, "blk", axis=1, tiled=True)
    query_blk = lax.all_gather(query_rot, "blk", axis=1, tiled=True)
    dout_blk = lax.all_gather(dout_low, "blk", axis=1, tiled=True)
    n_rows = grad_key_blk.shape[1]
    grad_sub_rows = math.gcd(n_rows, 512)

    def grad_one_step(step_idx, state_now):
        begin_row = step_idx * grad_sub_rows
        remote_pos = begin_row + jnp.arange(grad_sub_rows, dtype=jnp.int32)

        def take_part(array_in):
            return lax.dynamic_slice_in_dim(array_in, step_idx * grad_sub_rows, grad_sub_rows, 1)

        def local_queries(state_in):
            grad_query, grad_key, grad_value = state_in
            key_part = take_part(grad_key_blk)
            value_part = take_part(grad_value_blk)
            scores = (
                jnp.einsum(
                    "sqhd,skhd->shqk", query_rot, key_part, preferred_element_type=jnp.float32
                )
                * score_scale
            )
            allowed = causal_mask(positions, remote_pos, lengths)
            prob_rows = jnp.where(allowed, jnp.exp(scores - log_sum[..., None]), 0.0)
            grad_prob = jnp.einsum(
                "sqhd,skhd->shqk", dout_low, value_part, preferred_element_type=jnp.float32
            )
            grad_score = (prob_rows * (grad_prob - delta_here[..., None])).astype(jnp.bfloat16)
            grad_query = grad_query + score_scale * jnp.einsum(
                "shqk,skhd->sqhd", grad_score, key_part, preferred_element_type=jnp.float32
            )
            return (grad_query, grad_key, grad_value)

        def local_keys(state_in):
            grad_query, grad_key, grad_value = state_in
            query_part = take_part(query_blk)
            dout_part = take_part(dout_blk)
            lse_part = jnp.transpose(
                lax.dynamic_slice_in_dim(lse_full, begin_row, grad_sub_rows, 1), (0, 2, 1)
            )
            delta_part = jnp.transpose(
                lax.dynamic_slice_in_dim(delta_full, begin_row, grad_sub_rows, 1), (0, 2, 1)
            )
            scores = (
                jnp.einsum(
                    "sqhd,skhd->shqk", query_part, key_rot, preferred_element_type=jnp.float32
                )
                * score_scale
            )
            allowed = causal_mask(remote_pos, positions, lengths)
            prob_rows = jnp.where(allowed, jnp.exp(scores - lse_part[..., None]), 0.0)
            grad_prob = jnp.einsum(
                "sqhd,skhd->shqk", dout_part, value_low, preferred_element_type=jnp.float32
            )
            grad_score = (prob_rows * (grad_prob - delta_part[..., None])).astype(jnp.bfloat16)
            grad_value = grad_value + jnp.einsum(
                "shqk,sqhd->skhd",
                prob_rows.astype(jnp.bfloat16),
                dout_part,
                preferred_element_type=jnp.float32,
            )
            grad_key = grad_key + score_scale * jnp.einsum(
                "shqk,sqhd->skhd", grad_score, query_part, preferred_element_type=jnp.float32
            )
            return (grad_query, grad_key, grad_value)

        skip_first = (begin_row > last_pos) | (begin_row >= longest)
        state_now = lax.cond(skip_first, keep_state, local_queries, state_now)
        skip_second = (begin_row + grad_sub_rows - 1 < first_pos) | (first_pos >= longest)
        return lax.cond(skip_second, keep_state, local_keys, state_now)

    grad_query, grad_key, grad_value = lax.fori_loop(
        0, n_rows // grad_sub_rows, grad_one_step, (zero_grad, zero_grad, zero_grad)
    )
    grad_query = grad_query * cos_wide + rotate_back(grad_query * sin_wide)
    grad_key = grad_key * cos_wide + rotate_back(grad_key * sin_wide)
    query_key_value_gradient = (
        jnp.stack([grad_query, grad_key, grad_value], axis=2)
        .reshape(n_seq, slot_dev, 3, heads_here * HD)
        .astype(jnp.bfloat16)
    )
    query_key_value_term = jnp.einsum(
        "yzr,yzno->rno",
        normalized_every,
        query_key_value_gradient,
        preferred_element_type=jnp.float32,
    )

    def normed_grad(offset, amount):
        return jnp.einsum(
            "xwiu,hiu->xwh",
            query_key_value_gradient,
            query_key_value_backward,
            preferred_element_type=jnp.float32,
        )

    first_norm_gradient = head_scatter(normed_grad, seq_dev)
    first_gain_term = jnp.sum(first_norm_gradient * first_input_centered, axis=(0, 1))
    first_centered = first_norm_gradient * gain_one_b.astype(jnp.float32)
    grad_tokens = grad_res.reshape(seq_dev, slot_dev, model_width) + first_inverse_deviation * (
        first_centered
        - first_input_centered
        * jnp.mean(first_centered * first_input_centered, axis=-1, keepdims=True)
    )
    small_sums = lax.psum(
        (first_gain_term, second_gain_term, router_term, resid_term, const_term, vector_term),
        ("head", "blk"),
    )
    rows_here = gain_attn.shape[0]

    def own_rows(array_in):
        return lax.dynamic_slice_in_dim(array_in, blk_part * rows_here, rows_here, 0)

    in_sum, down_sum = finish_experts(in_term, down_term)
    qkv_sum, out_sum = sum_pair(query_key_value_term, out_term)
    return (
        output,
        grad_tokens,
        own_rows(small_sums[0]),
        qkv_sum,
        out_sum,
        own_rows(small_sums[1]),
        own_rows(small_sums[2]),
        small_sums[3],
        own_rows(small_sums[4]),
        own_rows(small_sums[5]),
        in_sum,
        down_sum,
    )


def solution(mesh):
    in_specs = (
        P("head", "blk", None),
        P("head", "blk", None),
        P(),
        P("head", "blk", None),
        P("head", "blk", None),
        P("blk"),
        P("blk", None, "head"),
        P("blk", "head"),
        P("blk"),
        P("blk", None),
        P(),
        P("blk", None),
        P("blk", None),
        P(None, "head", None, "blk"),
        P("blk", "head", None),
        P("head", "blk", None),
    )
    out_specs = (
        P("head", "blk", None),
        P("head", "blk", None),
        P("blk"),
        P("blk", None, "head"),
        P("blk", "head"),
        P("blk"),
        P("blk", None),
        P(),
        P("blk", None),
        P("blk", None),
        P(None, "head", None, "blk"),
        P("blk", "head", None),
    )
    return jax.shard_map(
        per_device, mesh=mesh, in_specs=in_specs, out_specs=out_specs, check_vma=False
    )
```

profile of v0, /device:TPU:0, one launch (start us, length us, event | category | flops | bytes accessed | tf_op | source)
XLA Modules:
  0.0 1623.8 jit_solution(8120592906695895179)
XLA Ops:
  11.6 35.7 %all-reduce.7 = (bf16[768]{0:T(1024)(128)(2,1)}, bf16[768]{0:T(1024)(128)(2,1)S(1)}) all-reduce(bf16[768]{0:T(1024)(128)(2,1)S(1)} %dynamic-update-slice.1, bf16[768]{0:T(1024)(128)(2,1)S(1)} %dynamic-update-slice), channel_id=1, replica_groups=mesh['head'=2,'blk'=16] {'blk'}, use_global_device_ids=true, to_apply=%add.5 | all-reduce | flops 1536 | bytes 6144
  67.4 22.2 %all_gather.67 = bf16[768,384]{1,0:T(8,128)(2,1)} all-gather(bf16[48,384]{1,0:T(8,128)(2,1)S(1)} %copy-done.60), channel_id=1, replica_groups=mesh['head'=2,'blk'=16] {'blk'}, dimensions={0}, use_global_device_ids=true | all-gather | bytes 626688 | tf_op jit(solution)/shard_map/all_gather | solution.py:76
  90.7 47.6 %all-gather.24.cloned.1.call-done = bf16[4,1024,1,6,64]{4,3,1,2,0:T(8,128)(2,1)} async-done(((bf16[4,64,1,6,64]{4,3,1,2,0:T(8,128)(2,1)}), bf16[4,1024,1,6,64]{4,3,1,2,0:T(8,128)(2,1)}) %all-gather.24.cloned.1.call-update) | async-done | bytes 3145744 | tf_op jit(solution)/shard_map/all_gather | solution.py:193
  147.4 66.2 %all-gather.14.cloned.1.call-done = bf16[4,1024,6,64]{3,2,1,0:T(8,128)(2,1)} async-done(((bf16[4,64,6,64]{3,2,1,0:T(8,128)(2,1)}), bf16[4,1024,6,64]{3,2,1,0:T(8,128)(2,1)}) %all-gather.14.cloned.1.call-update) | async-done | bytes 3145744 | tf_op jit(solution)/shard_map/all_gather | solution.py:192
  248.4 24.5 %all-gather.3 = bf16[16,48,2]{1,2,0:T(2,128)(2,1)S(1)} all-gather(bf16[1,48,2]{1,2,0:T(2,128)(2,1)} %bitcast.304), channel_id=1, replica_groups=mesh['head'=2,'blk'=16] {'blk'}, dimensions={0}, use_global_device_ids=true | all-gather | bytes 3264 | tf_op jit(solution)/shard_map/all_gather | solution.py:81
  273.6 17.7 %all-gather.2 = bf16[16,48,4]{1,2,0:T(4,128)(2,1)S(1)} all-gather(bf16[1,48,4]{1,2,0:T(4,128)(2,1)} %bitcast.303), channel_id=1, replica_groups=mesh['head'=2,'blk'=16] {'blk'}, dimensions={0}, use_global_device_ids=true | all-gather | bytes 6528 | tf_op jit(solution)/shard_map/all_gather | solution.py:80
  306.8 19.4 %all-gather.1 = bf16[16,48,12]{1,2,0:T(8,128)(2,1)S(1)} all-gather(bf16[1,48,12]{1,2,0:T(8,128)(2,1)S(1)} %bitcast.295), channel_id=1, replica_groups=mesh['head'=2,'blk'=16] {'blk'}, dimensions={0}, use_global_device_ids=true | all-gather | bytes 19584 | tf_op jit(solution)/shard_map/all_gather | solution.py:79
  376.9 21.5 %all-gather.16.cloned.1.call-done = bf16[768,4,2,2048]{3,0,2,1:T(8,128)(2,1)} async-done(((bf16[768,4,2,128]{3,0,2,1:T(8,128)(2,1)}), bf16[768,4,2,2048]{3,0,2,1:T(8,128)(2,1)}) %all-gather.16.cloned.1.call-update) | async-done | bytes 25165840 | tf_op jit(solution)/shard_map/all_gather | solution.py:87
  398.5 14.4 fusion.181
  412.9 87.7 %all-gather.18.cloned.1.call-done = bf16[2048,4,768]{2,0,1:T(8,128)(2,1)} async-done(((bf16[128,4,768]{2,0,1:T(8,128)(2,1)}), bf16[2048,4,768]{2,0,1:T(8,128)(2,1)}) %all-gather.18.cloned.1.call-update) | async-done | bytes 12582928 | tf_op jit(solution)/shard_map/all_gather | solution.py:88
  500.6 10.5 fusion.129
  522.4 13.4 fusion.110
  597.2 36.6 %all_gather.76 = f32[4,1024,6]{2,0,1:T(4,128)} all-gather(f32[4,64,6]{2,0,1:T(4,128)S(1)} %bitcast.276), channel_id=1, replica_groups=mesh['head'=2,'blk'=16] {'blk'}, dimensions={1}, use_global_device_ids=true | all-gather | bytes 104448 | tf_op jit(solution)/shard_map/all_gather | solution.py:392
  650.4 35.8 %all_gather.78 = f32[4,1024,6]{2,0,1:T(4,128)} all-gather(f32[4,64,6]{2,0,1:T(4,128)S(1)} %copy.281), channel_id=1, replica_groups=mesh['head'=2,'blk'=16] {'blk'}, dimensions={1}, use_global_device_ids=true | all-gather | bytes 104448 | tf_op jit(solution)/shard_map/all_gather | solution.py:393
  700.9 41.7 %while.45 = (s32[]{:T(128)}, f32[4,64,6,64]{1,3,2,0:T(8,128)}, f32[4,64,6,64]{1,3,2,0:T(8,128)}, f32[4,64,6,64]{1,3,2,0:T(8,128)}, s32[]{:T(128)}, /*index=5*/s3...) while((s32[]{:T(128)}, f32[4,64,6,64]{1,3,2,0:T(8,128)}, ...), condition=%wide.region_39.40_spmd.clone.clone, body=%wide.region_34.39_spmd.clone.clone.sunk | while | flops 718048064 | bytes 33079676 | solution.py:470
  710.0 15.9 conditional.13
  726.6 16.0 conditional.13
  751.7 10.3 convolution_bitcast_fusion.1
  763.5 27.3 %convolution_bitcast_fusion = f32[2048,768,4,2]{1,0,3,2:T(8,128)} fusion(bf16[4,48,768,1]{2,1,3,0:T(8,128)(2,1)S(1)} %bitcast.273, bf16[4,48,1,2048]{3,1,0,2:T(8,128)(2,1)S(1)} %copy-done.42, bf16[4,48,1,2048]{3,1,0,2:T(8,128)(2,1)S(1)} %copy-done.41), kind=kOutput, calls=%fused_computation.94 | convolution fusion | flops 1208745984 | bytes 52199424 | tf_op jit(solution)/shard_map/ecd,ecgf->fdeg/dot_general | solution.py:319
  799.1 45.1 %all-reduce.6 = (f32[768]{0:T(1024)S(1)}, f32[768]{0:T(1024)S(1)}, f32[768,12]{0,1:T(8,128)S(1)}, f32[12,12]{0,1:T(8,128)S(1)}, f32[768,4]{0,1:T(4,128)S(1)}, /*index=5*/f32[768,2]{0,1:T(2,128)S(1)}) all-reduce(f32[768]{0:T(1024)S(1)} %get-tuple-element.1369, ...), channel_id=1, replica_groups=mesh['head'=2,'blk'=16] {'head','blk'}, use_global_device_ids=true, to_apply=%region_43.44 | all-reduce | flops 15504 | bytes 124032 | tf_op jit(solution)/shard_map/psum | solution.py:503
  849.8 163.0 %reduce-scatter.17.cloned.1.call-done = f32[128,4,768]{0,2,1:T(8,128)} async-done(((f32[2048,4,768]{0,2,1:T(8,128)}), f32[128,4,768]{0,2,1:T(8,128)}) %reduce-scatter.17.cloned.1.call-update) | async-done | bytes 1572880 | tf_op jit(solution)/shard_map/reduce_scatter | solution.py:116
  1015.5 468.6 %reduce-scatter.15.cloned.1.call-done = f32[128,768,4,2]{1,0,3,2:T(8,128)} async-done(((f32[2048,768,4,2]{1,0,3,2:T(8,128)}), f32[128,768,4,2]{1,0,3,2:T(8,128)}) %reduce-scatter.15.cloned.1.call-update) | async-done | bytes 3145744 | tf_op jit(solution)/shard_map/reduce_scatter | solution.py:115
  1489.8 55.5 %reduce-scatter.13.cloned.1.call-done = f32[48,384]{1,0:T(8,128)} async-done(((f32[768,384]{1,0:T(8,128)}), f32[48,384]{1,0:T(8,128)}) %reduce-scatter.13.cloned.1.call-update) | async-done | bytes 73744 | tf_op jit(solution)/shard_map/reduce_scatter | solution.py:116
  1545.3 71.5 %reduce-scatter.11.cloned.1.call-done = f32[48,3,384]{2,0,1:T(8,128)} async-done(((f32[768,3,384]{2,0,1:T(8,128)}), f32[48,3,384]{2,0,1:T(8,128)}) %reduce-scatter.11.cloned.1.call-update) | async-done | bytes 221200 | tf_op jit(solution)/shard_map/reduce_scatter | solution.py:115
  (480 shorter events, 334.7 us)
Async XLA Ops:
  7.2 337.9 %copy-start = (f32[12,12]{1,0:T(8,128)S(1)}, f32[12,12]{1,0:T(8,128)}, u32[]{:S(2)}) copy-start(f32[12,12]{1,0:T(8,128)} %param.36) | copy-start | bytes 1732
  7.2 49.2 %all-gather.12.cloned.1.call-start = ((), (), s32[]{:S(2)}) async-start(), calls=%async_computation.10 | async-start | bytes 1880064 | tf_op jit(solution)/shard_map/all_gather | solution.py:75
  7.9 130.3 %all-gather.24.cloned.1.call-start = ((), (), s32[]{:S(2)}) async-start(), calls=%async_computation.22 | async-start | bytes 8912896 | tf_op jit(solution)/shard_map/all_gather | solution.py:193
  63.6 150.1 %all-gather.14.cloned.1.call-start = ((), (), s32[]{:S(2)}) async-start(), calls=%async_computation.11 | async-start | bytes 8912896 | tf_op jit(solution)/shard_map/all_gather | solution.py:192
  66.6 270.2 %reduce-scatter.7.cloned.1.call-start = ((), (), s32[]{:S(2)}) async-start(), calls=%async_computation.12 | async-start | bytes 589824 | tf_op jit(solution)/shard_map/reduce_scatter | solution.py:97
  241.8 156.7 %all-gather.16.cloned.1.call-start = ((), (), s32[]{:S(2)}) async-start(), calls=%async_computation.13 | async-start | bytes 26738688 | tf_op jit(solution)/shard_map/all_gather | solution.py:87
  244.6 256.0 %all-gather.18.cloned.1.call-start = ((), (), s32[]{:S(2)}) async-start(), calls=%async_computation.14 | async-start | bytes 13369344 | tf_op jit(solution)/shard_map/all_gather | solution.py:88
  246.8 60.0 %copy-start.83 = (bf16[48,12]{0,1:T(8,128)(2,1)S(1)}, bf16[48,12]{0,1:T(8,128)(2,1)}, u32[]{:S(2)}) copy-start(bf16[48,12]{0,1:T(8,128)(2,1)} %param.35) | copy-start | bytes 3460
  246.8 79.5 %copy-start.70 = (f32[2,64,12]{1,0,2:T(2,128)S(1)}, f32[2,64,12]{1,0,2:T(2,128)}, u32[]{:S(2)}) copy-start(f32[2,64,12]{1,0,2:T(2,128)} %param.27) | copy-start | bytes 18436
  246.8 389.6 %all-gather.20.cloned.1.call-start = ((), (), s32[]{:S(2)}) async-start(), calls=%async_computation.15 | async-start | bytes 8912896 | tf_op jit(solution)/shard_map/all_gather | solution.py:399
  248.1 78.1 %copy-start.84 = (f32[128]{0:T(128)}, f32[128]{0:T(128)S(1)}, u32[]{:S(2)}) copy-start(f32[128]{0:T(128)S(1)} %convert_element_type.201) | copy-start | bytes 1540
  248.4 120.2 %copy-start.69 = (s32[128,2]{0,1:T(2,128)}, s32[128,2]{0,1:T(2,128)S(1)}, u32[]{:S(2)}) copy-start(s32[128,2]{0,1:T(2,128)S(1)} %reshape.1021) | copy-start | bytes 3076
  336.1 206.0 %copy-start.73 = (s32[1024]{0:T(1024)}, s32[1024]{0:T(1024)S(1)}, u32[]{:S(2)}) copy-start(s32[1024]{0:T(1024)S(1)} %pad_clamp_fusion.1) | copy-start | bytes 12292
  350.9 13.2 all-to-all-start
  364.1 11.2 all-to-all-start.2
  518.9 18.7 %all-to-all-start.1 = ((bf16[4,48,768]{2,0,1:T(4,128)(2,1)}), bf16[4,48,768]{2,0,1:T(4,128)(2,1)S(1)}, u32[]{:S(2)}, u32[]{:S(2)}) async-start(bf16[4,48,768]{2,0,1:T(4,128)(2,1)} %copy.264), calls=%async_computation.2 | async-start | bytes 589824 | tf_op jit(solution)/shard_map/all_to_all | solution.py:110
  537.6 22.5 %all-to-all-start.3 = ((bf16[4,48,768]{2,0,1:T(4,128)(2,1)}), bf16[4,48,768]{2,0,1:T(4,128)(2,1)}, u32[]{:S(2)}, u32[]{:S(2)}) async-start(bf16[4,48,768]{2,0,1:T(4,128)(2,1)} %copy.275), calls=%async_computation.4 | async-start | bytes 589824 | tf_op jit(solution)/shard_map/all_to_all | solution.py:110
  541.8 146.9 %all-gather.22.cloned.1.call-start = ((), (), s32[]{:S(2)}) async-start(), calls=%async_computation.16 | async-start | bytes 8912896 | tf_op jit(solution)/shard_map/all_gather | solution.py:400
  591.4 206.3 %reduce-scatter.9.cloned.1.call-start = ((), (), s32[]{:S(2)}) async-start(), calls=%async_computation.17 | async-start | bytes 589824 | tf_op jit(solution)/shard_map/reduce_scatter | solution.py:97
  751.7 261.2 %reduce-scatter.17.cloned.1.call-start = ((), (), s32[]{:S(2)}) async-start(), calls=%async_computation.21 | async-start | bytes 26738688 | tf_op jit(solution)/shard_map/reduce_scatter | solution.py:116
  762.1 722.0 %reduce-scatter.15.cloned.1.call-start = ((), (), s32[]{:S(2)}) async-start(), calls=%async_computation.20 | async-start | bytes 53477376 | tf_op jit(solution)/shard_map/reduce_scatter | solution.py:115
  790.8 754.5 %reduce-scatter.13.cloned.1.call-start = ((), (), s32[]{:S(2)}) async-start(), calls=%async_computation.19 | async-start | bytes 1253376 | tf_op jit(solution)/shard_map/reduce_scatter | solution.py:116
  793.6 823.2 %reduce-scatter.11.cloned.1.call-start = ((), (), s32[]{:S(2)}) async-start(), calls=%async_computation.18 | async-start | bytes 3760128 | tf_op jit(solution)/shard_map/reduce_scatter | solution.py:115
  1484.1 132.7 %copy-start.1 = (f32[12,12]{1,0:T(8,128)S(1)}, f32[12,12]{1,0:T(8,128)}, u32[]{:S(2)}) copy-start(f32[12,12]{1,0:T(8,128)} %param.36) | copy-start | bytes 1732
  (82 other events, 628.8 us)
Sparse Core Ops, SparseCore 0:
  10.3 43.1 all-gather.11
  63.7 74.5 all-gather.23
  140.4 73.1 all-gather.13
  241.9 17.0 reduce-scatter.6
  261.0 137.4 all-gather.15
  400.9 99.6 all-gather.17
  503.0 73.0 all-gather.19
  591.6 91.6 all-gather.21
  751.8 12.6 reduce-scatter.8
  768.4 244.4 reduce-scatter.16
  1017.1 466.9 reduce-scatter.14
  1488.1 57.1 reduce-scatter.12
  1549.7 67.0 reduce-scatter.10
where the time goes:
time: 1640 us; the launch traced here: 1620 us
  waiting for transfers between devices  987 us (60%)
  blocking collectives  251 us (15%)
  local copies, waits for them, and re-layouts  155 us (9%)
  matrix products  139 us (8%)
  other arithmetic  54.8 us (3%)
  between operations  16.9 us (1%)
  starting transfers between devices  16.5 us (1%)
    reduce_scatter x2, waiting for transfers between devices, sum_pair(): lax.psum_scatter(first_term, 'blk', scatter_dimension=0, tiled=True)  540 us
    reduce_scatter x2, waiting for transfers between devices, sum_pair(): lax.psum_scatter(second_term, 'blk', scatter_dimension=0, tiled=True)  219 us
    all_gather x1, waiting for transfers between devices, gather_experts(): lax.all_gather(w_down, 'blk', axis=0, tiled=True)  87.7 us
    unnamed x185, local copies, waits for them, and re-layouts  74 us
    all_gather x1, waiting for transfers between devices, per_device(): key_blk = lax.all_gather(key_rot, 'blk', axis=1, tiled=True)  66.2 us
    all_gather x1, waiting for transfers between devices, per_device(): value_blk = lax.all_gather(value_low, 'blk', axis=1, tiled=True)  47.6 us
    psum x1, blocking collectives, per_device(): lax.psum((first_gain_term, second_gain_term, router_term, resid_term, con...  45.1 us
    all_gather x1, blocking collectives, per_device(): lax.all_gather(lse_rows, 'blk', axis=1, tiled=True)  36.6 us
  transfers between devices with their start and end apart: 17, of which 9 were waited for; matrix products, arithmetic and copies ran while one was open for 15% of the time, Pallas kernels for 0%

commit v1 on v0

v1 whole, which is shorter than its diff:
```python
import functools
import math

import jax
import jax.numpy as jnp
from jax import lax
from jax.experimental import pallas as pl
from jax.experimental.pallas import tpu as pltpu
from jax.sharding import PartitionSpec as P

HD = 64
NEXP = 8
EPS = 1e-05
NEG = -1e30
BF = jnp.bfloat16
F32 = jnp.float32
MIB = 1 << 20
ANY2 = (((1,), (1,)), ((), ()))
MM = (((1,), (0,)), ((), ()))
C_CONST, C_VEC, C_GAIN1, C_GAIN2 = 12, 16, 18, 19


def dot(a, b, dims=MM):
    return lax.dot_general(a, b, dims, preferred_element_type=F32)


def call(kernel, outs, args, smem=0, scratch=(), limit=40, flops=0, name=None):
    vm = pl.BlockSpec(memory_space=pltpu.VMEM)
    sm = pl.BlockSpec(memory_space=pltpu.SMEM)
    total = sum(math.prod(a.shape) * a.dtype.itemsize for a in list(args) + list(outs))
    return pl.pallas_call(
        kernel,
        out_shape=tuple(outs),
        in_specs=[sm] * smem + [vm] * (len(args) - smem),
        out_specs=tuple([vm] * len(outs)),
        scratch_shapes=list(scratch),
        compiler_params=pltpu.CompilerParams(vmem_limit_bytes=limit * MIB),
        cost_estimate=pl.CostEstimate(flops=flops, bytes_accessed=total, transcendentals=0),
        name=name,
    )(*args)


def sds(shape, dtype):
    return jax.ShapeDtypeStruct(shape, dtype)


def lower_lanes(shape):
    return (lax.broadcasted_iota(jnp.int32, shape, 1) & 63) < 32


def turned(values):
    return jnp.where(
        lower_lanes(values.shape), -pltpu.roll(values, 96, 1), pltpu.roll(values, 32, 1)
    )


def qkv_kernel(idx, mine, other, wpack, cos, sin, send, xn, small, xall):
    h = idx[0]
    rows = mine.shape[0]
    xall[pl.ds(h * rows, rows), :] = mine[...]
    xall[pl.ds((1 - h) * rows, rows), :] = other[...]
    width = mine.shape[1]
    small_t = jnp.transpose(wpack[:, wpack.shape[1] - 128 :].astype(F32))
    small[...] = small_t[: small.shape[0]]
    x = xall[...].astype(F32)
    rstd = lax.rsqrt(jnp.mean(x * x, axis=-1, keepdims=True) + EPS)
    normed = (x * rstd * small_t[C_GAIN1 : C_GAIN1 + 1]).astype(BF)
    xn[...] = normed
    part = (wpack.shape[1] - 128) // 4
    pairs = part // 128
    y = dot(normed, wpack[:, : 3 * part])
    slots = cos.shape[0]
    n_seq = xall.shape[0] // slots
    c = jnp.concatenate([cos[...]] * n_seq, axis=0)
    s = jnp.concatenate([sin[...]] * n_seq, axis=0)
    for p in range(pairs):
        for k in range(3):
            piece = y[:, k * part + p * 128 : k * part + (p + 1) * 128]
            if k < 2:
                piece = piece * c + turned(piece) * s
            if k == 0:
                piece = piece * (1.0 / math.sqrt(HD))
            piece = piece.astype(BF)
            for q in range(n_seq):
                send[p * n_seq + q, :, k * 128 : (k + 1) * 128] = piece[q * slots : (q + 1) * slots]
    used = pairs * n_seq
    if send.shape[0] > used:
        send[used:] = jnp.zeros((send.shape[0] - used,) + send.shape[1:], BF)


def head_mask(shape, which):
    lane = lax.broadcasted_iota(jnp.int32, shape, 1)
    return (lane >= 64) if which else (lane < 64)


def only(values, which):
    return jnp.where(head_mask(values.shape, which), values, jnp.zeros_like(values))


def scores_of(k_rows, q_head, first_query, limit_len):
    s = dot(k_rows, q_head, ANY2)
    key = lax.broadcasted_iota(jnp.int32, s.shape, 0)
    query = lax.broadcasted_iota(jnp.int32, (1, s.shape[1]), 1) + first_query
    last = jnp.minimum(query, limit_len - 1)
    return jnp.where(key <= last, s, NEG)


def each_block(total, block, fn):
    if total // block <= 4:
        for i in range(total // block):
            fn(i * block, (i + 1) * block)
    else:

        @pl.loop(0, total // block)
        def _(i):
            fn(pl.multiple_of(i * block, block), total)


def attend_kernel(idx, qkv, out, lse, vt):
    total = qkv.shape[0]
    block = 256
    limit_len = idx[1]
    vt[...] = jnp.transpose(qkv[:, 256:384])

    def step(start, n_keys):
        q = qkv[pl.ds(start, block), 0:128]
        parts = []
        for h in range(2):
            s = scores_of(qkv[0:n_keys, 128:256], only(q, h), start, limit_len)
            m = jnp.max(s, axis=0, keepdims=True)
            p = jnp.exp(s - m)
            total_p = jnp.sum(p, axis=0, keepdims=True)
            o = dot(vt[h * 64 : (h + 1) * 64, 0:n_keys], p.astype(BF))
            parts.append(o / total_p)
            lse[h : h + 1, pl.ds(start, block)] = m + jnp.log(total_p)
        out[pl.ds(start, block), :] = jnp.transpose(jnp.concatenate(parts, axis=0)).astype(BF)

    each_block(total, block, step)


def attend_back_kernel(idx, qkv, dout, out, lse, cos, sin, grad, kt, dk, dv):
    total = qkv.shape[0]
    block = 256
    limit_len = idx[1]
    kt[...] = jnp.transpose(qkv[:, 128:256])
    dk[...] = jnp.zeros_like(dk)
    dv[...] = jnp.zeros_like(dv)

    def unrotate(values, at, size):
        c, s = cos[pl.ds(at, size), :], sin[pl.ds(at, size), :]
        return values * c - turned(values) * s

    def step(start, n_keys):
        q = qkv[pl.ds(start, block), 0:128]
        do = dout[pl.ds(start, block), :]
        prod_t = jnp.transpose(do.astype(F32) * out[pl.ds(start, block), :].astype(F32))
        probs, ds, dq = [], [], []
        for h in range(2):
            q_head, do_head = only(q, h), only(do, h)
            s = scores_of(qkv[0:n_keys, 128:256], q_head, start, limit_len)
            p = jnp.exp(s - lse[h : h + 1, pl.ds(start, block)])
            delta = jnp.sum(prod_t[h * 64 : (h + 1) * 64], axis=0, keepdims=True)
            dp = dot(qkv[0:n_keys, 256:384], do_head, ANY2)
            d = (p * (dp - delta)).astype(BF)
            probs.append(p.astype(BF))
            ds.append(d)
            dq.append(dot(kt[h * 64 : (h + 1) * 64, 0:n_keys], d))
        both_q = jnp.concatenate([only(q, 0), only(q, 1)], axis=0)
        both_do = jnp.concatenate([only(do, 0), only(do, 1)], axis=0)
        dv[0:n_keys, :] += dot(jnp.concatenate(probs, axis=1), both_do)
        dk[0:n_keys, :] += dot(jnp.concatenate(ds, axis=1), both_q)
        gq = jnp.transpose(jnp.concatenate(dq, axis=0)) * (1.0 / math.sqrt(HD))
        grad[pl.ds(start, block), 0:128] = unrotate(gq, start, block).astype(BF)

    each_block(total, block, step)

    def finish(start, _):
        at = pl.ds(start, block)
        grad[at, 128:256] = unrotate(dk[at, :], start, block).astype(BF)
        grad[at, 256:384] = dv[at, :].astype(BF)

    each_block(total, block, finish)


def out_kernel(idx, recv, wpack, mine, other, attn, full):
    h = idx[0]
    part = attn.shape[1]
    n_seq = attn.shape[0] // recv.shape[1]
    for p in range(part // 128):
        rows = recv[p * n_seq : (p + 1) * n_seq].reshape(attn.shape[0], 128)
        attn[:, p * 128 : (p + 1) * 128] = rows
    full[...] = dot(attn[...], wpack[:, 3 * part : 4 * part], ANY2)
    rows = mine.shape[0]
    mine[...] = full[pl.ds(h * rows, rows), :]
    other[...] = full[pl.ds((1 - h) * rows, rows), :].astype(BF)


def onehot_rows(slots, n_rows):
    at = lax.broadcasted_iota(jnp.int32, (n_rows, slots.shape[1]), 0)
    return jnp.where((at == slots[0:1]) | (at == slots[1:2]), 1.0, 0.0).astype(BF)


def spread(rows, send):
    per = send.shape[1]
    copies = send.shape[0] * per // rows.shape[0]
    for i in range(send.shape[0]):
        at = (i // copies) * per
        send[i] = rows[at : at + per]


def send_grad_kernel(slots, cot, ints, send):
    g = (cot[...] * ints[:, 4:5].astype(F32)).astype(BF)
    n_rows = send.shape[1] * 2
    spread(dot(onehot_rows(slots[...], n_rows), g).astype(BF), send)


def norm_two(residual, gain):
    rstd = lax.rsqrt(jnp.mean(residual * residual, axis=-1, keepdims=True) + EPS)
    xhat = residual * rstd
    return rstd, xhat, xhat * gain


def route_kernel(tokens, mine, other, wpack, small, prev_logits, ints, slots, send, residual, aux):
    res = tokens[...].astype(F32) + mine[...] + other[...].astype(F32)
    residual[...] = res
    _, _, normed = norm_two(res, small[C_GAIN2 : C_GAIN2 + 1])
    low = normed.astype(BF)
    logits = dot(low, wpack[:, wpack.shape[1] - 128 :]) + prev_logits[...]
    lane = lax.broadcasted_iota(jnp.int32, logits.shape, 1)

    def pick(which):
        return jnp.sum(jnp.where(lane == which, logits, 0.0), axis=1, keepdims=True)

    def pair_softmax(a, b):
        top = jnp.maximum(a, b)
        ea, eb = jnp.exp(a - top), jnp.exp(b - top)
        return ea / (ea + eb), eb / (ea + eb)

    p0, p1 = pair_softmax(pick(ints[:, 0:1]), pick(ints[:, 1:2]))
    a00, a01 = pair_softmax(pick(C_CONST), pick(C_CONST + 1))
    a10, a11 = pair_softmax(pick(C_CONST + 2), pick(C_CONST + 3))
    info = jnp.zeros_like(logits)
    for i, v in enumerate((p0, p1, a00, a01, a10, a11)):
        info = jnp.where(lane == i, v, info)
    aux[...] = info
    n_rows = send.shape[1] * 2
    tok = slots.shape[1]
    at = lax.broadcasted_iota(jnp.int32, (n_rows, tok), 0)
    first = jnp.where(at == slots[0:1], 1.0, 0.0).astype(BF)
    second = jnp.where(at == slots[1:2], 1.0, 0.0).astype(BF)

    def split(v, base):
        high = v.astype(BF).astype(F32)
        return jnp.where(lane == 0, high, jnp.where(lane == 1, v - high, base))

    extra = dot(first, split(p0, 0.0).astype(BF)) + dot(second, split(p1, 0.0).astype(BF))
    rows = jnp.concatenate([dot(first + second, low), extra], axis=1)
    spread(rows.astype(BF), send)


def expert_kernel(n_pieces, x_ref, g_ref, *refs):
    wi, wd = refs[:n_pieces], refs[n_pieces : 2 * n_pieces]
    rest = refs[2 * n_pieces :]
    back = rest[0]
    gi, gd = rest[1 : 1 + n_pieces], rest[1 + n_pieces : 1 + 2 * n_pieces]
    acc_i, acc_d, wd_all = rest[1 + 2 * n_pieces :]
    step = pl.program_id(0)
    width = g_ref.shape[1]
    unit = wd[0].shape[0]

    @pl.when(step == 0)
    def _():
        acc_i[...] = jnp.zeros_like(acc_i)
        acc_d[...] = jnp.zeros_like(acc_d)
        for d in range(n_pieces):
            wd_all[d * unit : (d + 1) * unit, :] = wd[d][...]

    x = x_ref[:, :width]
    g = g_ref[...]
    prob = jnp.sum(x_ref[:, width:].astype(F32), axis=1, keepdims=True)
    xt = jnp.transpose(x)
    up_grad = dot(g, wd_all[...], ANY2) * prob
    hiddens = []
    grad_in = jnp.zeros((x.shape[0], width), F32)
    for d in range(n_pieces):
        both = dot(x, wi[d][...])
        gate, up = both[:, :unit], both[:, unit:]
        sig = 1.0 / (1.0 + jnp.exp(-gate))
        act = gate * sig
        hiddens.append((act * up).astype(BF))
        gh = up_grad[:, d * unit : (d + 1) * unit]
        g_gate = gh * up * sig * (1.0 + gate * (1.0 - sig))
        g_both = jnp.concatenate([g_gate, gh * act], axis=1).astype(BF)
        grad_in += dot(g_both, wi[d][...], ANY2)
        acc_i[d] += dot(xt, g_both)
    hidden = jnp.concatenate(hiddens, axis=1)
    back[:, :width] = dot(hidden, wd_all[...]).astype(BF)
    back[:, width:] = grad_in.astype(BF)
    g_scaled = (g.astype(F32) * prob).astype(BF)
    acc_d[...] += dot(jnp.transpose(hidden), g_scaled)

    @pl.when(step == pl.num_programs(0) - 1)
    def _():
        for d in range(n_pieces):
            gi[d][...] = acc_i[d].astype(BF)
            gd[d][...] = acc_d[d * unit : (d + 1) * unit, :].astype(BF)


def experts(x_rows, g_rows, w_in_pieces, w_down_pieces):
    n = len(w_in_pieces)
    rows, wide = x_rows.shape
    width = g_rows.shape[1]
    unit = w_down_pieces[0].shape[0]
    block = 256 if rows % 256 == 0 else rows
    whole = lambda a: pl.BlockSpec(a.shape, lambda i: (0,) * len(a.shape))
    outs = (
        [sds((rows, 2 * width), BF)]
        + [sds((width, 2 * unit), BF)] * n
        + [sds((unit, width), BF)] * n
    )
    flops = 18 * rows * width * unit * n
    return pl.pallas_call(
        functools.partial(expert_kernel, n),
        grid=(rows // block,),
        in_specs=[
            pl.BlockSpec((block, wide), lambda i: (i, 0)),
            pl.BlockSpec((block, width), lambda i: (i, 0)),
        ]
        + [whole(a) for a in w_in_pieces]
        + [whole(a) for a in w_down_pieces],
        out_specs=tuple(
            [pl.BlockSpec((block, 2 * width), lambda i: (i, 0))] + [whole(o) for o in outs[1:]]
        ),
        out_shape=tuple(outs),
        scratch_shapes=[
            pltpu.VMEM((n, width, 2 * unit), F32),
            pltpu.VMEM((n * unit, width), F32),
            pltpu.VMEM((n * unit, width), BF),
        ],
        compiler_params=pltpu.CompilerParams(vmem_limit_bytes=48 * MIB),
        cost_estimate=pl.CostEstimate(
            flops=flops, bytes_accessed=8 * rows * width + 12 * width * unit * n, transcendentals=0
        ),
        name="experts",
    )(x_rows, g_rows, *w_in_pieces, *w_down_pieces)


def combine_kernel(recv, residual, cot, small, wpack, ints, aux, prev, out, grad_res, grad_low, sums, resid):
    res = residual[...]
    gain = small[C_GAIN2 : C_GAIN2 + 1]
    rstd, xhat, normed = norm_two(res, gain)
    low = normed.astype(BF)
    width = res.shape[1]
    heads = 2
    copies = recv.shape[0] // heads
    groups = []
    for h in range(heads):
        total = recv[h * copies].astype(F32)
        for r in range(1, copies):
            total = total + recv[h * copies + r].astype(F32)
        groups.append(total.astype(BF))
    rows = jnp.concatenate(groups, axis=0)
    valid = ints[:, 4:5].astype(F32)
    go = cot[...] * valid
    lane = lax.broadcasted_iota(jnp.int32, (res.shape[0], rows.shape[0]), 1)
    first = jnp.where(lane == ints[:, 2:3], 1.0, 0.0).astype(BF)
    second = jnp.where(lane == ints[:, 3:4], 1.0, 0.0).astype(BF)
    eo0 = dot(first, rows[:, :width])
    eo1 = dot(second, rows[:, :width])
    gin = dot(first + second, rows[:, width:])
    info = aux[...]
    p0, p1 = info[:, 0:1], info[:, 1:2]
    alpha = ((info[:, 2:3], info[:, 3:4]), (info[:, 4:5], info[:, 5:6]))
    r0, r1 = ints[:, 0:1], ints[:, 1:2]

    def at(route, which):
        return jnp.where(route == which, 1.0, 0.0)

    vec = (small[C_VEC : C_VEC + 1], small[C_VEC + 1 : C_VEC + 2])
    share0 = at(r0, NEXP + 1) + at(r0, NEXP + 2) * alpha[0][0] + at(r0, NEXP + 3) * alpha[1][0]
    share1 = at(r1, NEXP + 1) + at(r1, NEXP + 2) * alpha[0][0] + at(r1, NEXP + 3) * alpha[1][0]
    weight = [p0 * at(r0, NEXP + 2 + j) + p1 * at(r1, NEXP + 2 + j) for j in range(2)]
    mixed = (
        p0 * eo0
        + p1 * eo1
        + (p0 * share0 + p1 * share1) * normed
        + (weight[0] * alpha[0][1]) * vec[0]
        + (weight[1] * alpha[1][1]) * vec[1]
    )
    out[...] = valid * (res + mixed)

    def rowsum(v):
        return jnp.sum(v, axis=1, keepdims=True)

    s_norm = rowsum(go * normed)
    s_vec = [rowsum(go * vec[j]) for j in range(2)]
    gg0 = rowsum(go * eo0) + share0 * s_norm
    gg1 = rowsum(go * eo1) + share1 * s_norm
    for j in range(2):
        gg0 = gg0 + at(r0, NEXP + 2 + j) * alpha[j][1] * s_vec[j]
        gg1 = gg1 + at(r1, NEXP + 2 + j) * alpha[j][1] * s_vec[j]
    gsum = p0 * gg0 + p1 * gg1
    c0, c1 = p0 * (gg0 - gsum), p1 * (gg1 - gsum)
    wide = lax.broadcasted_iota(jnp.int32, (res.shape[0], 128), 1)
    dl = jnp.where(wide == r0, c0, 0.0) + jnp.where(wide == r1, c1, 0.0)
    coef = p0 * at(r0, NEXP + 1) + p1 * at(r1, NEXP + 1)
    vec_rows = []
    for j in range(2):
        ga0, ga1 = weight[j] * s_norm, weight[j] * s_vec[j]
        mean = alpha[j][0] * ga0 + alpha[j][1] * ga1
        dl = jnp.where(wide == C_CONST + 2 * j, alpha[j][0] * (ga0 - mean), dl)
        dl = jnp.where(wide == C_CONST + 2 * j + 1, alpha[j][1] * (ga1 - mean), dl)
        coef = coef + alpha[j][0] * weight[j]
        vec_rows.append(jnp.sum((alpha[j][1] * weight[j]) * go, axis=0, keepdims=True))
    dl = dl.astype(BF)
    dlt = jnp.transpose(dl)
    proj = dot(dlt, low)
    resid[...] = dot(jnp.transpose(prev[...]), dl.astype(F32), MM) if False else lax.dot_general(
        jnp.transpose(prev[...]), dl.astype(F32), MM, precision=lax.Precision.HIGHEST,
        preferred_element_type=F32,
    )
    gn = gin + coef * go + dot(dl, wpack[:, wpack.shape[1] - 128 :], ANY2)
    gain_row = jnp.sum(gn * xhat, axis=0, keepdims=True)
    row = lax.broadcasted_iota(jnp.int32, (sums.shape[0], 1), 0)
    table = jnp.where(row < C_VEC, proj[: sums.shape[0]], 0.0)
    table = jnp.where(row == C_VEC, vec_rows[0], table)
    table = jnp.where(row == C_VEC + 1, vec_rows[1], table)
    sums[...] = jnp.where(row == C_GAIN2, gain_row, table)
    ghat = gn * gain
    grad = go + rstd * (ghat - xhat * jnp.mean(ghat * xhat, axis=-1, keepdims=True))
    grad_res[...] = grad
    grad_low[...] = grad.astype(BF)


def grad_vec_kernel(idx, mine, other, attn, wpack, send, dw, both):
    h = idx[0]
    rows = mine.shape[0]
    both[pl.ds(h * rows, rows), :] = mine[...]
    both[pl.ds((1 - h) * rows, rows), :] = other[...]
    part = attn.shape[1]
    g = both[...]
    gv = dot(g, wpack[:, 3 * part : 4 * part]).astype(BF)
    slots = send.shape[1]
    n_seq = g.shape[0] // slots
    for p in range(part // 128):
        for s in range(n_seq):
            send[p * n_seq + s] = gv[s * slots : (s + 1) * slots, p * 128 : (p + 1) * 128]
    used = part // 128 * n_seq
    if send.shape[0] > used:
        send[used:] = jnp.zeros((send.shape[0] - used,) + send.shape[1:], BF)
    dw[...] = dot(jnp.transpose(g), attn[...]).astype(BF)


def grad_qkv_kernel(idx, recv, xn, wpack, mine, other, dw, both, full):
    h = idx[0]
    part = both.shape[1] // 3
    n_seq = both.shape[0] // recv.shape[1]
    for p in range(part // 128):
        rows = recv[p * n_seq : (p + 1) * n_seq].reshape(both.shape[0], 384)
        for k in range(3):
            at = k * part + p * 128
            both[:, at : at + 128] = rows[:, k * 128 : (k + 1) * 128]
    g = both[...]
    full[...] = dot(g, wpack[:, : 3 * part], ANY2)
    rows = mine.shape[0]
    mine[...] = full[pl.ds(h * rows, rows), :]
    other[...] = full[pl.ds((1 - h) * rows, rows), :].astype(BF)
    dw[...] = dot(jnp.transpose(xn[...]), g).astype(BF)


def final_kernel(tokens, mine, other, grad_res, small, grad, gain_row):
    x = tokens[...].astype(F32)
    rstd = lax.rsqrt(jnp.mean(x * x, axis=-1, keepdims=True) + EPS)
    xhat = x * rstd
    gn = mine[...] + other[...].astype(F32)
    gain_row[...] = jnp.broadcast_to(jnp.sum(gn * xhat, axis=0, keepdims=True), gain_row.shape)
    ghat = gn * small[C_GAIN1 : C_GAIN1 + 1]
    grad[...] = grad_res[...] + rstd * (
        ghat - xhat * jnp.mean(ghat * xhat, axis=-1, keepdims=True)
    )


def per_device(
    tokens, previous_layer_logits, lengths, routes, pair_order, gain_attn, w_qkv, w_out, gain_ffn,
    w_router, w_residual, w_const, const_vec, w_in, w_down, cotangent,
):
    seq_dev, slot_dev, width = tokens.shape
    n_all = previous_layer_logits.shape[2]
    tok = seq_dev * slot_dev
    heads = lax.axis_size("head")
    n_blk = lax.axis_size("blk")
    n_seq = seq_dev * heads
    n_slots = slot_dev * n_blk
    e_loc = w_in.shape[1]
    n_share = n_blk // e_loc
    unit = w_in.shape[3]
    rows_here = gain_attn.shape[0]
    part = w_qkv.shape[2]
    capacity = 9 * 2 * tok // (8 * n_all)
    h = lax.axis_index("head")
    b = lax.axis_index("blk")
    q = b % e_loc
    swap = [(0, 1), (1, 0)]
    everyone = ("head", "blk")

    def across(x):
        return lax.ppermute(x, "head", swap)

    def hop(x, d):
        return lax.ppermute(x, "blk", [(i, i ^ d) for i in range(n_blk)]) if d else x

    small_cols = jnp.concatenate(
        [w_router, w_const, const_vec, gain_attn[:, None], gain_ffn[:, None],
         jnp.zeros((rows_here, 128 - 20), BF)], axis=1)
    packed = jnp.concatenate([w_qkv.reshape(rows_here, 3 * part), w_out, small_cols], axis=1)
    wpack = lax.all_gather(packed, "blk", axis=0, tiled=True)
    flat_tokens = tokens.reshape(tok, width)
    other_tokens = across(flat_tokens)

    positions = b * slot_dev + jnp.arange(slot_dev, dtype=jnp.int32)
    own_len = lax.dynamic_slice_in_dim(lengths, h * seq_dev, seq_dev)
    valid = (positions[None, :] < own_len[:, None]).reshape(tok)
    route_rows = jnp.transpose(routes.reshape(tok, 2))
    order = jnp.transpose(pair_order.reshape(tok, 2)).reshape(2 * tok)
    route = route_rows.reshape(2 * tok)
    eligible = jnp.concatenate([valid, valid]) & (route < NEXP)
    before = (
        (route[:, None] == route[None, :]) & (order[None, :] < order[:, None]) & eligible[None, :]
    )
    rank = jnp.sum(before.astype(jnp.int32), axis=1)
    slot = jnp.where(eligible & (rank < capacity), route * capacity + rank, NEXP * capacity)
    slot = slot.reshape(2, tok)
    slot_rows = jnp.concatenate([slot, jnp.zeros((6, tok), jnp.int32)], axis=0)
    ints = jnp.concatenate(
        [routes.reshape(tok, 2), jnp.transpose(slot), valid[:, None].astype(jnp.int32),
         jnp.zeros((tok, 3), jnp.int32)], axis=1)

    cot = cotangent.reshape(tok, width)
    per_send = e_loc * capacity
    (send_g,) = call(
        send_grad_kernel, [sds((heads * n_share, per_send, width), BF)], [slot_rows, cot, ints],
        name="send_grad")

    def to_experts(rows):
        flat = rows.reshape(heads * n_blk * capacity, rows.shape[-1])
        return lax.all_to_all(flat, everyone, 0, 0, tiled=True)

    g_rows = to_experts(send_g)

    in_by_expert = jnp.transpose(w_in, (1, 0, 2, 3)).reshape(e_loc, width, 2 * unit)
    down_by_expert = jnp.transpose(w_down, (1, 0, 2))
    in_pieces = [
        hop(lax.dynamic_index_in_dim(in_by_expert, q ^ d, 0, keepdims=False), d) for d in range(e_loc)]
    down_pieces = [
        hop(lax.dynamic_index_in_dim(down_by_expert, q ^ d, 0, keepdims=False), d) for d in range(e_loc)]
    joined = unit % 128 != 0
    if joined:
        cube = [p.reshape(width, 2, unit) for p in in_pieces]
        in_pieces = [jnp.concatenate(cube, axis=2).reshape(width, 2 * unit * e_loc)]
        down_pieces = [jnp.concatenate(down_pieces, axis=0)]

    frequency = 10000.0 ** (-(2.0 * jnp.arange(HD // 2, dtype=F32)) / HD)
    angles = jnp.arange(n_slots, dtype=jnp.int32).astype(F32)[:, None] * frequency[None, :]
    cos_all = jnp.concatenate([jnp.cos(angles)] * 4, axis=1)
    sin_all = jnp.concatenate([jnp.sin(angles)] * 4, axis=1)
    cos_here = lax.dynamic_slice_in_dim(cos_all, b * slot_dev, slot_dev)
    sin_here = lax.dynamic_slice_in_dim(sin_all, b * slot_dev, slot_dev)
    idx = jnp.stack([h, lax.dynamic_index_in_dim(lengths, b % n_seq, 0, keepdims=False)])
    prev = previous_layer_logits.reshape(tok, n_all)
    prev_wide = jnp.pad(prev, ((0, 0), (0, 128 - n_all)))
    prev_logits = jnp.pad(
        jnp.dot(prev, w_residual, precision=lax.Precision.HIGHEST), ((0, 0), (0, 128 - n_all)))

    send_qkv, xn, small = call(
        qkv_kernel,
        [sds((n_blk, slot_dev, 384), BF), sds((n_seq * slot_dev, width), BF), sds((24, width), F32)],
        [idx, flat_tokens, other_tokens, wpack, cos_here, sin_here], smem=1,
        scratch=[pltpu.VMEM((n_seq * slot_dev, width), BF)],
        flops=2 * n_seq * slot_dev * width * 3 * part, name="qkv")

    def exchange(x):
        flat = x.reshape(n_blk * slot_dev, x.shape[-1])
        return lax.all_to_all(flat, "blk", 0, 0, tiled=True)

    qkv = exchange(send_qkv)
    attn_unit, lse = call(
        attend_kernel, [sds((n_slots, 128), BF), sds((8, n_slots), F32)], [idx, qkv], smem=1,
        scratch=[pltpu.VMEM((128, n_slots), BF)], flops=2 * n_slots * n_slots * 512, name="attend")
    attn_recv = exchange(attn_unit).reshape(n_blk, slot_dev, 128)
    mine, other, attn_low = call(
        out_kernel,
        [sds((tok, width), F32), sds((tok, width), BF), sds((n_seq * slot_dev, part), BF)],
        [idx, attn_recv, wpack], smem=1, scratch=[pltpu.VMEM((n_seq * slot_dev, width), F32)],
        flops=2 * n_seq * slot_dev * width * part, name="out")
    send_x, residual, aux = call(
        route_kernel,
        [sds((heads * n_share, per_send, width + 128), BF), sds((tok, width), F32), sds((tok, 128), F32)],
        [flat_tokens, mine, across(other), wpack, small, prev_logits, ints, slot_rows],
        flops=tok * width * 1000, name="route")
    x_rows = to_experts(send_x)
    n = 1 if joined else e_loc
    results = experts(x_rows, g_rows, in_pieces, down_pieces)
    back_rows, grad_in_pieces, grad_down_pieces = results[0], results[1 : 1 + n], results[1 + n :]
    recv = to_experts(back_rows).reshape(heads * n_share, per_send, 2 * width)

    if joined:
        cube = grad_in_pieces[0].reshape(width, 2, e_loc, unit)
        grad_in_pieces = [cube[:, :, d].reshape(width, 2 * unit) for d in range(e_loc)]
        grad_down_pieces = [grad_down_pieces[0][d * unit : (d + 1) * unit] for d in range(e_loc)]
    came_in = [hop(grad_in_pieces[d], d) for d in range(e_loc)]
    came_down = [hop(grad_down_pieces[d], d) for d in range(e_loc)]

    output, grad_res, grad_low, sums, resid = call(
        combine_kernel,
        [sds((tok, width), F32), sds((tok, width), F32), sds((tok, width), BF), sds((24, width), F32),
         sds((128, 128), F32)],
        [recv, residual, cot, small, wpack, ints, aux, prev_wide], flops=tok * width * 2000,
        name="combine")

    send_gv, dw_out = call(
        grad_vec_kernel, [sds((n_blk, slot_dev, 128), BF), sds((width, part), BF)],
        [idx, grad_low, across(grad_low), attn_low, wpack], smem=1,
        scratch=[pltpu.VMEM((n_seq * slot_dev, width), BF)],
        flops=4 * n_seq * slot_dev * width * part, name="grad_vec")
    dout = exchange(send_gv)
    (grad_unit,) = call(
        attend_back_kernel, [sds((n_slots, 384), BF)],
        [idx, qkv, dout, attn_unit, lse, cos_all, sin_all], smem=1,
        scratch=[pltpu.VMEM((128, n_slots), BF), pltpu.VMEM((n_slots, 128), F32),
                 pltpu.VMEM((n_slots, 128), F32)],
        flops=5 * n_slots * n_slots * 256, name="attend_back")
    grad_recv = exchange(grad_unit).reshape(n_blk, slot_dev, 384)
    gn_mine, gn_other, dw_qkv = call(
        grad_qkv_kernel,
        [sds((tok, width), F32), sds((tok, width), BF), sds((width, 3 * part), BF)],
        [idx, grad_recv, xn, wpack], smem=1,
        scratch=[pltpu.VMEM((n_seq * slot_dev, 3 * part), BF),
                 pltpu.VMEM((n_seq * slot_dev, width), F32)],
        flops=4 * n_seq * slot_dev * width * 3 * part, name="grad_qkv")
    grad_tokens, gain_row = call(
        final_kernel, [sds((tok, width), F32), sds((8, width), F32)],
        [flat_tokens, gn_mine, across(gn_other), grad_res, small], name="final")

    def own_rows_sum(partial):
        return lax.psum_scatter(partial, "blk", scatter_dimension=0, tiled=True).astype(F32)

    out_sum = own_rows_sum(dw_out)
    qkv_sum = own_rows_sum(dw_qkv).reshape(rows_here, 3, part)
    table = jnp.concatenate(
        [sums[:C_GAIN1], gain_row[:1], sums[C_GAIN2 : C_GAIN2 + 1]], axis=0)
    by_owner = jnp.transpose(table.reshape(20, n_blk, rows_here), (1, 0, 2)).reshape(n_blk, -1)
    extra = jnp.broadcast_to(resid[:n_all, :n_all].reshape(1, -1), (n_blk, n_all * n_all))
    chunk = jnp.concatenate([by_owner, extra], axis=1)
    chunk = jnp.concatenate([chunk] * heads, axis=0)
    total = jnp.sum(lax.all_to_all(chunk, everyone, 0, 0, tiled=True), axis=0)
    owned = total[: 20 * rows_here].reshape(20, rows_here)
    resid_sum = total[20 * rows_here :].reshape(n_all, n_all)

    def by_source(pieces):
        chosen = []
        for e in range(e_loc):
            value = pieces[e_loc - 1]
            for d in range(e_loc - 1):
                value = jnp.where((q ^ d) == e, pieces[d], value)
            chosen.append(value.astype(F32))
        return chosen

    in_sum = jnp.stack([v.reshape(width, 2, unit) for v in by_source(came_in)], axis=1)
    down_sum = jnp.stack(by_source(came_down), axis=1)
    return (
        output.reshape(tokens.shape),
        grad_tokens.reshape(tokens.shape),
        owned[C_GAIN1],
        qkv_sum,
        out_sum,
        owned[C_GAIN2],
        jnp.transpose(owned[:n_all]),
        resid_sum,
        jnp.transpose(owned[C_CONST:C_VEC]),
        jnp.transpose(owned[C_VEC : C_VEC + 2]),
        in_sum,
        down_sum,
    )


def solution(mesh):
    in_specs = (
        P("head", "blk", None),
        P("head", "blk", None),
        P(),
        P("head", "blk", None),
        P("head", "blk", None),
        P("blk"),
        P("blk", None, "head"),
        P("blk", "head"),
        P("blk"),
        P("blk", None),
        P(),
        P("blk", None),
        P("blk", None),
        P(None, "head", None, "blk"),
        P("blk", "head", None),
        P("head", "blk", None),
    )
    out_specs = (
        P("head", "blk", None),
        P("head", "blk", None),
        P("blk"),
        P("blk", None, "head"),
        P("blk", "head"),
        P("blk"),
        P("blk", None),
        P(),
        P("blk", None),
        P("blk", None),
        P(None, "head", None, "blk"),
        P("blk", "head", None),
    )
    return jax.shard_map(
        per_device, mesh=mesh, in_specs=in_specs, out_specs=out_specs, check_vma=False
    )
```

time: 1640 us -> 450 us (0.27)
  waiting for transfers between devices: 987 us -> 266 us
  blocking collectives: 251 us -> 12.6 us
  matrix products: 139 us -> 0.19 us
  local copies, waits for them, and re-layouts: 155 us -> 65.4 us
  other arithmetic: 54.8 us -> 10.9 us
  Pallas kernels: 0 us -> 33.8 us
  starting transfers between devices: 16.5 us -> 44.6 us
    reduce_scatter x6 -> x2, waiting for transfers between devices: 759 us -> 48.9 us  [own_rows_sum(): lax.psum_scatter(partial, 'blk', scatter_dimension=0, tiled=True)]
    all_gather x7 -> x1, waiting for transfers between devices: 223 us -> 36.4 us  [per_device(): wpack = lax.all_gather(packed, 'blk', axis=0, tiled=True)]
    all_gather x8 -> x0, blocking collectives: 170 us -> none  [the longest x1 36.6 us: per_device(): lax.all_gather(lse_rows, 'blk', axis=1, tiled=True)]
    dot_general x29 -> x1, matrix products: 138 us -> 0.19 us  [per_device(): jnp.dot(prev, w_residual, precision=lax.Precision.HIGHEST)]
    all_to_all x4 -> x7, waiting for transfers between devices: 4.86 us -> 114 us  [the longest x3 67.1 us: to_experts(): return lax.all_to_all(flat, everyone, 0, 0, tiled=True)]
    ppermute x0 -> x16, waiting for transfers between devices: none -> 65.9 us  [the longest x12 49.7 us: hop(): lax.ppermute(x, 'blk', [(i, i ^ d) for i in range(n_blk)])]
    psum x1 -> x0, blocking collectives: 45.1 us -> none  [per_device(): lax.psum((first_gain_term, second_gain_term, router_term, resid_term, con...]
    unnamed x1 -> x0, blocking collectives: 35.7 us -> none
  transfers between devices with their start and end apart: 17 -> 26, of which waited for: 9 -> 16; matrix products, arithmetic and copies ran while one was open for 15% -> 8% of each run, Pallas kernels for 0% -> 1%
where the time goes in v1:
time: 450 us; the launch traced here: 448 us
  waiting for transfers between devices  266 us (59%)
  local copies, waits for them, and re-layouts  65.4 us (15%)
  starting transfers between devices  44.6 us (10%)
  Pallas kernels  33.8 us (8%)
  between operations  14.5 us (3%)
  blocking collectives  12.6 us (3%)
  other arithmetic  10.9 us (2%)
    all_to_all x3, waiting for transfers between devices, to_experts(): return lax.all_to_all(flat, everyone, 0, 0, tiled=True)  67.1 us
    ppermute x12, waiting for transfers between devices, hop(): lax.ppermute(x, 'blk', [(i, i ^ d) for i in range(n_blk)])  49.7 us
    reduce_scatter x2, waiting for transfers between devices, own_rows_sum(): lax.psum_scatter(partial, 'blk', scatter_dimension=0, tiled=True)  48.9 us
    all_to_all x3, waiting for transfers between devices, exchange(): return lax.all_to_all(flat, 'blk', 0, 0, tiled=True)  43.2 us
    unnamed x170, local copies, waits for them, and re-layouts  40.2 us
    all_gather x1, waiting for transfers between devices, per_device(): wpack = lax.all_gather(packed, 'blk', axis=0, tiled=True)  36.4 us
    pallas_call x10, Pallas kernels, call(): pl.pallas_call(kernel, out_shape=tuple(outs), in_specs=[sm] * smem + [vm]...  23.1 us
    ppermute x4, waiting for transfers between devices, across(): return lax.ppermute(x, 'head', swap)  16.1 us
  transfers between devices with their start and end apart: 26, of which 16 were waited for; matrix products, arithmetic and copies ran while one was open for 8% of the time, Pallas kernels for 1%

profile of v1, /device:TPU:0, one launch (start us, length us, event | category | flops | bytes accessed | tf_op | source)
XLA Modules:
  0.0 447.9 jit_solution(14263095373058343514)
XLA Ops:
  23.0 36.4 %all-gather.2.cloned.1.call-done.wpack = bf16[768,1664]{1,0:T(8,128)(2,1)} async-done(((bf16[48,1664]{1,0:T(8,128)(2,1)}), bf16[768,1664]{1,0:T(8,128)(2,1)}) %all-gather.2.cloned.1.call-update) | async-done | bytes 2555920 | tf_op jit(solution)/shard_map/all_gather | solution.py:516
  68.9 17.6 %all-to-all-done = bf16[16,64,384]{2,1,0:T(8,128)(2,1)S(1)} async-done(((bf16[16,64,384]{2,1,0:T(8,128)(2,1)}), bf16[16,64,384]{2,1,0:T(8,128)(2,1)S(1)}, u32[]{:S(2)}, u32[]{:S(2)}) %all-to-all-start) | async-done | bytes 786464 | tf_op jit(solution)/shard_map/all_to_all | solution.py:583
  86.6 5.5 %attend.1 = (bf16[1024,128]{1,0:T(8,128)(2,1)}, f32[8,1024]{1,0:T(8,128)S(1)}) custom-call(s32[2]{0:T(128)S(1)} %pad_add_fusion.idx, bf16[1024,384]{1,0:T(8,128)(2,1)S(1)} %bitcast.116), custom_call_target="tpu_custom_call" | custom-call | flops 1073741824 | bytes 1081352 | tf_op jit(solution)/shard_map/attend/pallas_call | solution.py:31
  92.1 5.4 %all-to-all-start.1 = ((bf16[16,64,128]{2,1,0:T(8,128)(2,1)}), bf16[16,64,128]{2,1,0:T(8,128)(2,1)S(1)}, u32[]{:S(2)}, u32[]{:S(2)}) async-start(bf16[16,64,128]{2,1,0:T(8,128)(2,1)} %bitcast.5), calls=%async_computation.1 | async-start | bytes 524288 | tf_op jit(solution)/shard_map/all_to_all | solution.py:583
  99.9 7.7 %all-to-all-done.1.recv = bf16[16,64,128]{2,1,0:T(8,128)(2,1)S(1)} async-done(((bf16[16,64,128]{2,1,0:T(8,128)(2,1)}), bf16[16,64,128]{2,1,0:T(8,128)(2,1)S(1)}, u32[]{:S(2)}, u32[]{:S(2)}) %all-to-all-start.1) | async-done | bytes 262176 | tf_op jit(solution)/shard_map/all_to_all | solution.py:583
  115.9 10.6 %collective-permute-done.1.other = bf16[128,768]{1,0:T(8,128)(2,1)S(1)} collective-permute-done((bf16[128,768]{1,0:T(8,128)(2,1)S(1)}, bf16[128,768]{1,0:T(8,128)(2,1)S(1)}, u32[]{:S(2)}, u32[]{:S(2)}) %collective-permute-start.1) | collective-permute-done | bytes 196640 | tf_op jit(solution)/shard_map/ppermute | solution.py:507
  129.1 11.8 %all-to-all-done.3 = bf16[32,24,768]{2,1,0:T(8,128)(2,1)} async-done(((bf16[32,24,768]{2,1,0:T(8,128)(2,1)}), bf16[32,24,768]{2,1,0:T(8,128)(2,1)}, u32[]{:S(2)}, u32[]{:S(2)}) %all-to-all-start.3) | async-done | bytes 1179680 | tf_op jit(solution)/shard_map/all_to_all | solution.py:546
  148.3 6.5 %constant_dynamic-slice_fusion.4 = (bf16[1,768,256]{2,0,1:T(2,128)(2,1)S(1)}, bf16[1,768,256]{2,0,1:T(2,128)(2,1)S(1)}, bf16[1,768,256]{2,0,1:T(2,128)(2,1)S(1)}, bf16[1,768,256]{2,0,1:T(2,128)(2,1)S(1)}) fusion(bf16[4,768,256]{2,0,1:T(4,128)(2,1)} %reshape.235, s32[]{:T(128)S(6)} %select_n.196, s32[]{:T(128)S(6)} %select_n.195, s32[]{:T(128)S(6)} %select_n.194, ...), kind=kLoop, calls=%fused_computation.34 | loop fusion | bytes 3145744 | tf_op jit(solution)/shard_map/jit(dynamic_index_in_dim)/dynamic_slice | solution.py:553
  162.5 24.5 %collective-permute-done.6.refs_6_ = bf16[128,768]{1,0:T(8,128)(2,1)S(1)} collective-permute-done((bf16[128,768]{1,0:T(8,128)(2,1)S(1)}, bf16[128,768]{1,0:T(8,128)(2,1)S(1)}, u32[]{:S(2)}, u32[]{:S(2)}) %collective-permute-start.6) | collective-permute-done | bytes 196640 | tf_op jit(solution)/shard_map/ppermute | solution.py:510
  200.1 10.6 %experts.1 = (bf16[768,1536]{1,0:T(8,128)(2,1)}, bf16[768,256]{1,0:T(8,128)(2,1)S(1)}, bf16[768,256]{1,0:T(8,128)(2,1)S(1)}, bf16[768,256]{1,0:T(8,128)(2,1)S(1)...) custom-call(bf16[768,896]{1,0:T(8,128)(2,1)} %bitcast.17.x_ref, ...), custom_call_target="tpu_custom_call" | custom-call | flops 5435817984 | bytes 9437184 | tf_op jit(solution)/shard_map/experts/pallas_call | solution.py:322
  216.5 5.6 %all-to-all-start.4 = ((bf16[32,24,1536]{2,1,0:T(8,128)(2,1)}), bf16[32,24,1536]{2,1,0:T(8,128)(2,1)}, u32[]{:S(2)}, u32[]{:S(2)}) async-start(bf16[32,24,1536]{2,1,0:T(8,128)(2,1)} %bitcast.123), calls=%async_computation.4 | async-start | bytes 4718592 | tf_op jit(solution)/shard_map/all_to_all | solution.py:546
  222.1 55.3 %all-to-all-done.4 = bf16[32,24,1536]{2,1,0:T(8,128)(2,1)} async-done(((bf16[32,24,1536]{2,1,0:T(8,128)(2,1)}), bf16[32,24,1536]{2,1,0:T(8,128)(2,1)}, u32[]{:S(2)}, u32[]{:S(2)}) %all-to-all-start.4) | async-done | bytes 2359328 | tf_op jit(solution)/shard_map/all_to_all | solution.py:546
  279.3 3.8 combine.1
  285.3 5.5 %collective-permute-done.8.other = bf16[128,768]{1,0:T(8,128)(2,1)S(1)} collective-permute-done((bf16[128,768]{1,0:T(8,128)(2,1)S(1)}, bf16[128,768]{1,0:T(8,128)(2,1)S(1)}, u32[]{:S(2)}, u32[]{:S(2)}) %collective-permute-start.8) | collective-permute-done | bytes 196640 | tf_op jit(solution)/shard_map/ppermute | solution.py:507
  292.0 12.6 %all_to_all.74 = bf16[16,64,128]{2,1,0:T(8,128)(2,1)S(1)} all-to-all(bf16[16,64,128]{2,1,0:T(8,128)(2,1)S(1)} %get-tuple-element.56), channel_id=1, replica_groups=mesh['head'=2,'blk'=16] {'blk'}, dimensions={0} | all-to-all | bytes 524288 | tf_op jit(solution)/shard_map/all_to_all | solution.py:583
  304.6 5.5 %attend_back.1 = bf16[1024,384]{1,0:T(8,128)(2,1)S(1)} custom-call(s32[2]{0:T(128)S(1)} %copy-done.41, bf16[1024,384]{1,0:T(8,128)(2,1)S(1)} %bitcast.117, bf16[1024,128]{1,0:T(8,128)(2,1)S(1)} %bitcast.120, bf16[1024,128]{1,0:T(8,128)(2,1)} %get-tuple-element.45.out, f32[8,1024]{1,0:T(8,128)S(1)} %copy-done.70, f32[1024,128]{1,0:T(8,128)S(1)} %copy-done.14, ...), custom_call_target="tpu_custom_call" | custom-call | flops 1342177280 | bytes 3178504 | tf_op jit(solution)/shard_map/attend_back/pallas_call | solution.py:31
  311.0 3.7 all-to-all-start.6
  315.6 17.9 %all-to-all-done.6.recv = bf16[16,64,384]{2,1,0:T(8,128)(2,1)S(1)} async-done(((bf16[16,64,384]{2,1,0:T(8,128)(2,1)}), bf16[16,64,384]{2,1,0:T(8,128)(2,1)S(1)}, u32[]{:S(2)}, u32[]{:S(2)}) %all-to-all-start.6) | async-done | bytes 786464 | tf_op jit(solution)/shard_map/all_to_all | solution.py:583
  342.5 4.5 %collective-permute-done.13 = bf16[128,768]{1,0:T(8,128)(2,1)S(1)} collective-permute-done((bf16[128,768]{1,0:T(8,128)(2,1)}, bf16[128,768]{1,0:T(8,128)(2,1)S(1)}, u32[]{:S(2)}, u32[]{:S(2)}) %collective-permute-start.13) | collective-permute-done | bytes 196640 | tf_op jit(solution)/shard_map/ppermute | solution.py:510
  347.4 4.0 collective-permute-done.15
  354.6 6.6 %collective-permute-done.10 = bf16[768,256]{1,0:T(8,128)(2,1)S(1)} collective-permute-done((bf16[768,256]{1,0:T(8,128)(2,1)S(1)}, bf16[768,256]{1,0:T(8,128)(2,1)S(1)}, u32[]{:S(2)}, u32[]{:S(2)}) %collective-permute-start.10) | collective-permute-done | bytes 393248 | tf_op jit(solution)/shard_map/ppermute | solution.py:510
  361.2 7.4 %collective-permute-done.12 = bf16[768,256]{1,0:T(8,128)(2,1)S(1)} collective-permute-done((bf16[768,256]{1,0:T(8,128)(2,1)S(1)}, bf16[768,256]{1,0:T(8,128)(2,1)S(1)}, u32[]{:S(2)}, u32[]{:S(2)}) %collective-permute-start.12) | collective-permute-done | bytes 393248 | tf_op jit(solution)/shard_map/ppermute | solution.py:510
  374.0 4.8 %all-to-all-start.7 = ((f32[32,1,1104]{2,1,0:T(1,128)}), f32[32,1,1104]{2,1,0:T(1,128)S(1)}, u32[]{:S(2)}, u32[]{:S(2)}) async-start(f32[32,1,1104]{2,1,0:T(1,128)} %copy.133), calls=%async_computation.7 | async-start | bytes 294912 | tf_op jit(solution)/shard_map/all_to_all | solution.py:655
  390.8 48.9 %reduce-scatter.3.cloned.1.call-done = bf16[48,1152]{1,0:T(8,128)(2,1)} async-done(((bf16[768,1152]{1,0:T(8,128)(2,1)}), bf16[48,1152]{1,0:T(8,128)(2,1)}) %reduce-scatter.3.cloned.1.call-update) | async-done | bytes 110608 | tf_op jit(solution)/shard_map/reduce_scatter | solution.py:645
  (283 shorter events, 110.4 us)
Async XLA Ops:
  7.2 52.2 %all-gather.2.cloned.1.call-start = ((), (), s32[]{:S(2)}) async-start(), calls=%async_computation.10 | async-start | bytes 2715648 | tf_op jit(solution)/shard_map/all_gather | solution.py:516
  13.6 9.4 %collective-permute-start = (bf16[128,768]{1,0:T(8,128)(2,1)}, bf16[128,768]{1,0:T(8,128)(2,1)S(1)}, u32[]{:S(2)}, u32[]{:S(2)}) collective-permute-start(bf16[128,768]{1,0:T(8,128)(2,1)} %bitcast.109), channel_id=1, source_target_pairs={{0,16},{16,0},{1,17},{17,1},{2,18},{18,2},{3,19},{19,3},{4,20},{20... | collective-permute-start | bytes 589832 | tf_op jit(solution)/shard_map/ppermute | solution.py:507
  64.3 22.3 %all-to-all-start = ((bf16[16,64,384]{2,1,0:T(8,128)(2,1)}), bf16[16,64,384]{2,1,0:T(8,128)(2,1)S(1)}, u32[]{:S(2)}, u32[]{:S(2)}) async-start(bf16[16,64,384]{2,1,0:T(8,128)(2,1)} %get-tuple-element.44), calls=%async_computation | async-start | bytes 1572864 | tf_op jit(solution)/shard_map/all_to_all | solution.py:583
  92.1 15.5 %all-to-all-start.1 = ((bf16[16,64,128]{2,1,0:T(8,128)(2,1)}), bf16[16,64,128]{2,1,0:T(8,128)(2,1)S(1)}, u32[]{:S(2)}, u32[]{:S(2)}) async-start(bf16[16,64,128]{2,1,0:T(8,128)(2,1)} %bitcast.5), calls=%async_computation.1 | async-start | bytes 524288 | tf_op jit(solution)/shard_map/all_to_all | solution.py:583
  107.6 33.4 %all-to-all-start.3 = ((bf16[32,24,768]{2,1,0:T(8,128)(2,1)}), bf16[32,24,768]{2,1,0:T(8,128)(2,1)}, u32[]{:S(2)}, u32[]{:S(2)}) async-start(bf16[32,24,768]{2,1,0:T(8,128)(2,1)} %bitcast.108), calls=%async_computation.3 | async-start | bytes 2359296 | tf_op jit(solution)/shard_map/all_to_all | solution.py:546
  114.1 12.5 %collective-permute-start.1 = (bf16[128,768]{1,0:T(8,128)(2,1)S(1)}, bf16[128,768]{1,0:T(8,128)(2,1)S(1)}, u32[]{:S(2)}, u32[]{:S(2)}) collective-permute-start(bf16[128,768]{1,0:T(8,128)(2,1)S(1)} %get-tuple-element.47), channel_id=1, source_target_pairs={{0,16},{16,0},{1,17},{17,1},{2,18},{18,2},{3,19},{19,3},{4,20},{20... | collective-permute-start | bytes 589832 | tf_op jit(solution)/shard_map/ppermute | solution.py:507
  141.0 52.3 %all-to-all-start.2 = ((bf16[32,24,896]{2,1,0:T(8,128)(2,1)}), bf16[32,24,896]{2,1,0:T(8,128)(2,1)}, u32[]{:S(2)}, u32[]{:S(2)}) async-start(bf16[32,24,896]{2,1,0:T(8,128)(2,1)} %bitcast.115), calls=%async_computation.2 | async-start | bytes 2752512 | tf_op jit(solution)/shard_map/all_to_all | solution.py:546
  154.9 36.2 %collective-permute-start.2 = (bf16[768,256]{1,0:T(8,128)(2,1)S(1)}, bf16[768,256]{1,0:T(8,128)(2,1)S(1)}, u32[]{:S(2)}, u32[]{:S(2)}) collective-permute-start(bf16[768,256]{1,0:T(8,128)(2,1)S(1)} %bitcast.134), channel_id=1, source_target_pairs={{0,1},{1,0},{2,3},{3,2},{4,5},{5,4},{6,7},{7,6},{8,9},{9,8},{10,11... | collective-permute-start | bytes 1179656 | tf_op jit(solution)/shard_map/ppermute | solution.py:510
  157.7 34.1 %collective-permute-start.3 = (bf16[768,256]{1,0:T(8,128)(2,1)S(1)}, bf16[768,256]{1,0:T(8,128)(2,1)S(1)}, u32[]{:S(2)}, u32[]{:S(2)}) collective-permute-start(bf16[768,256]{1,0:T(8,128)(2,1)S(1)} %bitcast.135), channel_id=1, source_target_pairs={{0,2},{1,3},{2,0},{3,1},{4,6},{5,7},{6,4},{7,5},{8,10},{9,11},{10,... | collective-permute-start | bytes 1179656 | tf_op jit(solution)/shard_map/ppermute | solution.py:510
  159.4 33.1 %collective-permute-start.4 = (bf16[768,256]{1,0:T(8,128)(2,1)S(1)}, bf16[768,256]{1,0:T(8,128)(2,1)S(1)}, u32[]{:S(2)}, u32[]{:S(2)}) collective-permute-start(bf16[768,256]{1,0:T(8,128)(2,1)S(1)} %bitcast.136), channel_id=1, source_target_pairs={{0,3},{1,2},{2,1},{3,0},{4,7},{5,6},{6,5},{7,4},{8,11},{9,10},{10,... | collective-permute-start | bytes 1179656 | tf_op jit(solution)/shard_map/ppermute | solution.py:510
  159.8 27.2 %collective-permute-start.6 = (bf16[128,768]{1,0:T(8,128)(2,1)S(1)}, bf16[128,768]{1,0:T(8,128)(2,1)S(1)}, u32[]{:S(2)}, u32[]{:S(2)}) collective-permute-start(bf16[128,768]{1,0:T(8,128)(2,1)S(1)} %bitcast.139), channel_id=1, source_target_pairs={{0,2},{1,3},{2,0},{3,1},{4,6},{5,7},{6,4},{7,5},{8,10},{9,11},{10,... | collective-permute-start | bytes 589832 | tf_op jit(solution)/shard_map/ppermute | solution.py:510
  161.3 29.0 %collective-permute-start.7 = (bf16[128,768]{1,0:T(8,128)(2,1)S(1)}, bf16[128,768]{1,0:T(8,128)(2,1)S(1)}, u32[]{:S(2)}, u32[]{:S(2)}) collective-permute-start(bf16[128,768]{1,0:T(8,128)(2,1)S(1)} %bitcast.140), channel_id=1, source_target_pairs={{0,3},{1,2},{2,1},{3,0},{4,7},{5,6},{6,5},{7,4},{8,11},{9,10},{10,... | collective-permute-start | bytes 589832 | tf_op jit(solution)/shard_map/ppermute | solution.py:510
  216.5 61.0 %all-to-all-start.4 = ((bf16[32,24,1536]{2,1,0:T(8,128)(2,1)}), bf16[32,24,1536]{2,1,0:T(8,128)(2,1)}, u32[]{:S(2)}, u32[]{:S(2)}) async-start(bf16[32,24,1536]{2,1,0:T(8,128)(2,1)} %bitcast.123), calls=%async_computation.4 | async-start | bytes 4718592 | tf_op jit(solution)/shard_map/all_to_all | solution.py:546
  311.0 22.4 %all-to-all-start.6 = ((bf16[16,64,384]{2,1,0:T(8,128)(2,1)}), bf16[16,64,384]{2,1,0:T(8,128)(2,1)S(1)}, u32[]{:S(2)}, u32[]{:S(2)}) async-start(bf16[16,64,384]{2,1,0:T(8,128)(2,1)} %bitcast.118), calls=%async_computation.6 | async-start | bytes 1572864 | tf_op jit(solution)/shard_map/all_to_all | solution.py:583
  314.8 67.5 %reduce-scatter.5.cloned.1.call-start = ((), (), s32[]{:S(2)}) async-start(), calls=%async_computation.12 | async-start | bytes 626688 | tf_op jit(solution)/shard_map/reduce_scatter | solution.py:645
  315.5 124.2 %reduce-scatter.3.cloned.1.call-start = ((), (), s32[]{:S(2)}) async-start(), calls=%async_computation.11 | async-start | bytes 1880064 | tf_op jit(solution)/shard_map/reduce_scatter | solution.py:645
  339.0 8.0 %collective-permute-start.13 = (bf16[128,768]{1,0:T(8,128)(2,1)}, bf16[128,768]{1,0:T(8,128)(2,1)S(1)}, u32[]{:S(2)}, u32[]{:S(2)}) collective-permute-start(bf16[128,768]{1,0:T(8,128)(2,1)} %copy-done.60), channel_id=1, source_target_pairs={{0,2},{1,3},{2,0},{3,1},{4,6},{5,7},{6,4},{7,5},{8,10},{9,11},{10,... | collective-permute-start | bytes 589832 | tf_op jit(solution)/shard_map/ppermute | solution.py:510
  340.1 7.3 %collective-permute-start.14 = (bf16[128,768]{1,0:T(8,128)(2,1)S(1)}, bf16[128,768]{1,0:T(8,128)(2,1)S(1)}, u32[]{:S(2)}, u32[]{:S(2)}) collective-permute-start(bf16[128,768]{1,0:T(8,128)(2,1)S(1)} %copy-done.59), channel_id=1, source_target_pairs={{0,1},{1,0},{2,3},{3,2},{4,5},{5,4},{6,7},{7,6},{8,9},{9,8},{10,11... | collective-permute-start | bytes 589832 | tf_op jit(solution)/shard_map/ppermute | solution.py:510
  340.6 10.8 %collective-permute-start.15 = (bf16[128,768]{1,0:T(8,128)(2,1)S(1)}, bf16[128,768]{1,0:T(8,128)(2,1)S(1)}, u32[]{:S(2)}, u32[]{:S(2)}) collective-permute-start(bf16[128,768]{1,0:T(8,128)(2,1)S(1)} %copy-done.57), channel_id=1, source_target_pairs={{0,3},{1,2},{2,1},{3,0},{4,7},{5,6},{6,5},{7,4},{8,11},{9,10},{10,... | collective-permute-start | bytes 589832 | tf_op jit(solution)/shard_map/ppermute | solution.py:510
  341.4 19.8 %collective-permute-start.10 = (bf16[768,256]{1,0:T(8,128)(2,1)S(1)}, bf16[768,256]{1,0:T(8,128)(2,1)S(1)}, u32[]{:S(2)}, u32[]{:S(2)}) collective-permute-start(bf16[768,256]{1,0:T(8,128)(2,1)S(1)} %copy-done.49), channel_id=1, source_target_pairs={{0,2},{1,3},{2,0},{3,1},{4,6},{5,7},{6,4},{7,5},{8,10},{9,11},{10,... | collective-permute-start | bytes 1179656 | tf_op jit(solution)/shard_map/ppermute | solution.py:510
  342.3 18.9 %collective-permute-start.11 = (bf16[768,256]{1,0:T(8,128)(2,1)S(1)}, bf16[768,256]{1,0:T(8,128)(2,1)S(1)}, u32[]{:S(2)}, u32[]{:S(2)}) collective-permute-start(bf16[768,256]{1,0:T(8,128)(2,1)S(1)} %copy-done.47), channel_id=1, source_target_pairs={{0,1},{1,0},{2,3},{3,2},{4,5},{5,4},{6,7},{7,6},{8,9},{9,8},{10,11... | collective-permute-start | bytes 1179656 | tf_op jit(solution)/shard_map/ppermute | solution.py:510
  347.0 21.6 %collective-permute-start.12 = (bf16[768,256]{1,0:T(8,128)(2,1)S(1)}, bf16[768,256]{1,0:T(8,128)(2,1)S(1)}, u32[]{:S(2)}, u32[]{:S(2)}) collective-permute-start(bf16[768,256]{1,0:T(8,128)(2,1)S(1)} %copy-done.45), channel_id=1, source_target_pairs={{0,3},{1,2},{2,1},{3,0},{4,7},{5,6},{6,5},{7,4},{8,11},{9,10},{10,... | collective-permute-start | bytes 1179656 | tf_op jit(solution)/shard_map/ppermute | solution.py:510
  353.8 18.0 %collective-permute-start.9 = (bf16[128,768]{1,0:T(8,128)(2,1)S(1)}, bf16[128,768]{1,0:T(8,128)(2,1)S(1)}, u32[]{:S(2)}, u32[]{:S(2)}) collective-permute-start(bf16[128,768]{1,0:T(8,128)(2,1)S(1)} %copy-done.62), channel_id=1, source_target_pairs={{0,16},{16,0},{1,17},{17,1},{2,18},{18,2},{3,19},{19,3},{4,20},{20... | collective-permute-start | bytes 589832 | tf_op jit(solution)/shard_map/ppermute | solution.py:507
  374.0 13.2 %all-to-all-start.7 = ((f32[32,1,1104]{2,1,0:T(1,128)}), f32[32,1,1104]{2,1,0:T(1,128)S(1)}, u32[]{:S(2)}, u32[]{:S(2)}) async-start(f32[32,1,1104]{2,1,0:T(1,128)} %copy.133), calls=%async_computation.7 | async-start | bytes 294912 | tf_op jit(solution)/shard_map/all_to_all | solution.py:655
  (79 other events, 878.1 us)
Sparse Core Ops, SparseCore 0:
  13.7 45.6 all-gather.1
  319.2 56.9 reduce-scatter.4
  380.4 59.2 reduce-scatter.2

commit v2 on v1

--- a/solution.py
+++ b/solution.py
@@ -6,6 +6,7 @@
 from jax import lax
 from jax.experimental import pallas as pl
 from jax.experimental.pallas import tpu as pltpu
+from jax.sharding import Mesh
 from jax.sharding import PartitionSpec as P
 
 HD = 64
@@ -18,23 +19,46 @@
 ANY2 = (((1,), (1,)), ((), ()))
 MM = (((1,), (0,)), ((), ()))
 C_CONST, C_VEC, C_GAIN1, C_GAIN2 = 12, 16, 18, 19
+RESID = 32
 
 
 def dot(a, b, dims=MM):
     return lax.dot_general(a, b, dims, preferred_element_type=F32)
 
 
-def call(kernel, outs, args, smem=0, scratch=(), limit=40, flops=0, name=None):
-    vm = pl.BlockSpec(memory_space=pltpu.VMEM)
+def whole_block(shape):
+    return pl.BlockSpec(shape, lambda i: (0,) * len(shape), pipeline_mode=pl.Buffered(1))
+
+
+def far(x):
+    return pltpu.with_memory_space_constraint(x, pltpu.HBM)
+
+
+class Columns:
+    def __init__(self, array, count, at):
+        self.array, self.at, self.window = array, (0, at // count), (array.shape[0], count)
+        self.shape, self.dtype = self.window, array.dtype
+
+
+def call(kernel, outs, args, smem=0, scratch=(), room=12, flops=0, name=None,
+         far_in=(), far_out=()):
     sm = pl.BlockSpec(memory_space=pltpu.SMEM)
     total = sum(math.prod(a.shape) * a.dtype.itemsize for a in list(args) + list(outs))
+    limit = total + sum(math.prod(a.shape) * a.dtype.itemsize for a in scratch) + room * MIB
+    specs = [
+        pl.BlockSpec(a.window, functools.partial(lambda at, i: at, a.at), pipeline_mode=pl.Buffered(1))
+        if isinstance(a, Columns) else whole_block(a.shape) for a in args[smem:]]
+    args = [a.array if isinstance(a, Columns) else a for a in args]
+    args = [far(a) if i in far_in else a for i, a in enumerate(args)]
+    shapes = tuple(pltpu.HBM(o.shape, o.dtype) if i in far_out else o for i, o in enumerate(outs))
     return pl.pallas_call(
         kernel,
-        out_shape=tuple(outs),
-        in_specs=[sm] * smem + [vm] * (len(args) - smem),
-        out_specs=tuple([vm] * len(outs)),
+        grid=(1,),
+        out_shape=shapes,
+        in_specs=[sm] * smem + specs,
+        out_specs=tuple(whole_block(o.shape) for o in outs),
         scratch_shapes=list(scratch),
-        compiler_params=pltpu.CompilerParams(vmem_limit_bytes=limit * MIB),
+        compiler_params=pltpu.CompilerParams(vmem_limit_bytes=min(limit, 60 * MIB)),
         cost_estimate=pl.CostEstimate(flops=flops, bytes_accessed=total, transcendentals=0),
         name=name,
     )(*args)
@@ -54,21 +78,21 @@
     )
 
 
-def qkv_kernel(idx, mine, other, wpack, cos, sin, send, xn, small, xall):
+def qkv_kernel(idx, mine, other, wq, wsmall, cos, sin, send, xn, small, xall):
     h = idx[0]
     rows = mine.shape[0]
     xall[pl.ds(h * rows, rows), :] = mine[...]
     xall[pl.ds((1 - h) * rows, rows), :] = other[...]
     width = mine.shape[1]
-    small_t = jnp.transpose(wpack[:, wpack.shape[1] - 128 :].astype(F32))
+    small_t = jnp.transpose(wsmall[...].astype(F32))
     small[...] = small_t[: small.shape[0]]
     x = xall[...].astype(F32)
     rstd = lax.rsqrt(jnp.mean(x * x, axis=-1, keepdims=True) + EPS)
     normed = (x * rstd * small_t[C_GAIN1 : C_GAIN1 + 1]).astype(BF)
     xn[...] = normed
-    part = (wpack.shape[1] - 128) // 4
+    part = wq.shape[1] // 3
     pairs = part // 128
-    y = dot(normed, wpack[:, : 3 * part])
+    y = dot(normed, wq[...])
     slots = cos.shape[0]
     n_seq = xall.shape[0] // slots
     c = jnp.concatenate([cos[...]] * n_seq, axis=0)
@@ -189,7 +213,7 @@
     for p in range(part // 128):
         rows = recv[p * n_seq : (p + 1) * n_seq].reshape(attn.shape[0], 128)
         attn[:, p * 128 : (p + 1) * 128] = rows
-    full[...] = dot(attn[...], wpack[:, 3 * part : 4 * part], ANY2)
+    full[...] = dot(attn[...], wpack[...], ANY2)
     rows = mine.shape[0]
     mine[...] = full[pl.ds(h * rows, rows), :]
     other[...] = full[pl.ds((1 - h) * rows, rows), :].astype(BF)
@@ -225,7 +249,7 @@
     residual[...] = res
     _, _, normed = norm_two(res, small[C_GAIN2 : C_GAIN2 + 1])
     low = normed.astype(BF)
-    logits = dot(low, wpack[:, wpack.shape[1] - 128 :]) + prev_logits[...]
+    logits = dot(low, wpack[...]) + prev_logits[...]
     lane = lax.broadcasted_iota(jnp.int32, logits.shape, 1)
 
     def pick(which):
@@ -258,91 +282,103 @@
     spread(rows.astype(BF), send)
 
 
-def expert_kernel(n_pieces, x_ref, g_ref, *refs):
-    wi, wd = refs[:n_pieces], refs[n_pieces : 2 * n_pieces]
-    rest = refs[2 * n_pieces :]
-    back = rest[0]
-    gi, gd = rest[1 : 1 + n_pieces], rest[1 + n_pieces : 1 + 2 * n_pieces]
-    acc_i, acc_d, wd_all = rest[1 + 2 * n_pieces :]
+def expert_kernel(n_pieces, n_steps, x_ref, g_ref, *refs):
+    w, back, grads = refs[:n_pieces], refs[n_pieces], refs[n_pieces + 1 : 2 * n_pieces + 1]
+    wd_all = refs[2 * n_pieces + 1]
+    acc = refs[2 * n_pieces + 2] if n_steps > 1 else None
     step = pl.program_id(0)
     width = g_ref.shape[1]
-    unit = wd[0].shape[0]
+    two = w[0].shape[1]
+    unit = two // 2
+    strips = width // two
 
     @pl.when(step == 0)
     def _():
-        acc_i[...] = jnp.zeros_like(acc_i)
-        acc_d[...] = jnp.zeros_like(acc_d)
         for d in range(n_pieces):
-            wd_all[d * unit : (d + 1) * unit, :] = wd[d][...]
+            for j in range(strips):
+                at = width + j * unit
+                wd_all[d * unit : (d + 1) * unit, j * two : (j + 1) * two] = w[d][at : at + unit, :]
 
     x = x_ref[:, :width]
     g = g_ref[...]
     prob = jnp.sum(x_ref[:, width:].astype(F32), axis=1, keepdims=True)
     xt = jnp.transpose(x)
+    g_scaled = (g.astype(F32) * prob).astype(BF)
     up_grad = dot(g, wd_all[...], ANY2) * prob
     hiddens = []
     grad_in = jnp.zeros((x.shape[0], width), F32)
+
+    def keep(d, start, value):
+        at = slice(start, start + value.shape[0])
+        if n_steps == 1:
+            grads[d][at, :] = value.astype(BF)
+            return
+
+        @pl.when(step == 0)
+        def _():
+            acc[d, at, :] = value
+
+        @pl.when(step > 0)
+        def _():
+            acc[d, at, :] += value
+
+        @pl.when(step == n_steps - 1)
+        def _():
+            grads[d][at, :] = acc[d, at, :].astype(BF)
+
     for d in range(n_pieces):
-        both = dot(x, wi[d][...])
+        both = dot(x, w[d][:width, :])
         gate, up = both[:, :unit], both[:, unit:]
         sig = 1.0 / (1.0 + jnp.exp(-gate))
         act = gate * sig
-        hiddens.append((act * up).astype(BF))
+        hidden = (act * up).astype(BF)
+        hiddens.append(hidden)
         gh = up_grad[:, d * unit : (d + 1) * unit]
         g_gate = gh * up * sig * (1.0 + gate * (1.0 - sig))
         g_both = jnp.concatenate([g_gate, gh * act], axis=1).astype(BF)
-        grad_in += dot(g_both, wi[d][...], ANY2)
-        acc_i[d] += dot(xt, g_both)
-    hidden = jnp.concatenate(hiddens, axis=1)
-    back[:, :width] = dot(hidden, wd_all[...]).astype(BF)
+        grad_in += dot(g_both, w[d][:width, :], ANY2)
+        keep(d, 0, dot(xt, g_both))
+        gd = dot(jnp.transpose(hidden), g_scaled)
+        for j in range(strips):
+            keep(d, width + j * unit, gd[:, j * two : (j + 1) * two])
+    back[:, :width] = dot(jnp.concatenate(hiddens, axis=1), wd_all[...]).astype(BF)
     back[:, width:] = grad_in.astype(BF)
-    g_scaled = (g.astype(F32) * prob).astype(BF)
-    acc_d[...] += dot(jnp.transpose(hidden), g_scaled)
-
-    @pl.when(step == pl.num_programs(0) - 1)
-    def _():
-        for d in range(n_pieces):
-            gi[d][...] = acc_i[d].astype(BF)
-            gd[d][...] = acc_d[d * unit : (d + 1) * unit, :].astype(BF)
-
-
-def experts(x_rows, g_rows, w_in_pieces, w_down_pieces):
-    n = len(w_in_pieces)
+
+
+def experts(x_rows, g_rows, pieces):
+    n = len(pieces)
     rows, wide = x_rows.shape
     width = g_rows.shape[1]
-    unit = w_down_pieces[0].shape[0]
-    block = 256 if rows % 256 == 0 else rows
-    whole = lambda a: pl.BlockSpec(a.shape, lambda i: (0,) * len(a.shape))
-    outs = (
-        [sds((rows, 2 * width), BF)]
-        + [sds((width, 2 * unit), BF)] * n
-        + [sds((unit, width), BF)] * n
-    )
-    flops = 18 * rows * width * unit * n
+    deep, two = pieces[0].shape
+    unit = two // 2
+    block = 384 if rows % 384 == 0 else rows
+    steps = rows // block
+    outs = [sds((rows, 2 * width), BF)] + [sds((deep, two), BF)] * n
+    scratch = [pltpu.VMEM((n * unit, width), BF)]
+    if steps > 1:
+        scratch.append(pltpu.VMEM((n, deep, two), F32))
     return pl.pallas_call(
-        functools.partial(expert_kernel, n),
-        grid=(rows // block,),
+        functools.partial(expert_kernel, n, steps),
+        grid=(steps,),
         in_specs=[
             pl.BlockSpec((block, wide), lambda i: (i, 0)),
             pl.BlockSpec((block, width), lambda i: (i, 0)),
         ]
-        + [whole(a) for a in w_in_pieces]
-        + [whole(a) for a in w_down_pieces],
+        + [whole_block(a.shape) for a in pieces],
         out_specs=tuple(
-            [pl.BlockSpec((block, 2 * width), lambda i: (i, 0))] + [whole(o) for o in outs[1:]]
+            [pl.BlockSpec((block, 2 * width), lambda i: (i, 0))]
+            + [whole_block(o.shape) for o in outs[1:]]
         ),
-        out_shape=tuple(outs),
-        scratch_shapes=[
-            pltpu.VMEM((n, width, 2 * unit), F32),
-            pltpu.VMEM((n * unit, width), F32),
-            pltpu.VMEM((n * unit, width), BF),
-        ],
-        compiler_params=pltpu.CompilerParams(vmem_limit_bytes=48 * MIB),
+        out_shape=tuple(outs[:1] + [pltpu.HBM(o.shape, o.dtype) for o in outs[1:]]),
+        scratch_shapes=scratch,
+        compiler_params=pltpu.CompilerParams(vmem_limit_bytes=(30 if steps == 1 else 48) * MIB),
         cost_estimate=pl.CostEstimate(
-            flops=flops, bytes_accessed=8 * rows * width + 12 * width * unit * n, transcendentals=0
+            flops=18 * rows * width * unit * n,
+            bytes_accessed=8 * rows * width + 12 * width * unit * n,
+            transcendentals=0,
         ),
         name="experts",
-    )(x_rows, g_rows, *w_in_pieces, *w_down_pieces)
+    )(x_rows, far(g_rows), *[far(p) for p in pieces])
 
 
 def combine_kernel(recv, residual, cot, small, wpack, ints, aux, prev, out, grad_res, grad_low, sums, resid):
@@ -415,11 +451,11 @@
     dl = dl.astype(BF)
     dlt = jnp.transpose(dl)
     proj = dot(dlt, low)
-    resid[...] = dot(jnp.transpose(prev[...]), dl.astype(F32), MM) if False else lax.dot_general(
-        jnp.transpose(prev[...]), dl.astype(F32), MM, precision=lax.Precision.HIGHEST,
-        preferred_element_type=F32,
+    resid[...] = lax.dot_general(
+        jnp.transpose(prev[...]), jnp.where(wide < C_CONST, dl.astype(F32), 0.0), MM,
+        precision=lax.Precision.HIGHEST, preferred_element_type=F32,
     )
-    gn = gin + coef * go + dot(dl, wpack[:, wpack.shape[1] - 128 :], ANY2)
+    gn = gin + coef * go + dot(dl, wpack[...], ANY2)
     gain_row = jnp.sum(gn * xhat, axis=0, keepdims=True)
     row = lax.broadcasted_iota(jnp.int32, (sums.shape[0], 1), 0)
     table = jnp.where(row < C_VEC, proj[: sums.shape[0]], 0.0)
@@ -439,7 +475,7 @@
     both[pl.ds((1 - h) * rows, rows), :] = other[...]
     part = attn.shape[1]
     g = both[...]
-    gv = dot(g, wpack[:, 3 * part : 4 * part]).astype(BF)
+    gv = dot(g, wpack[...]).astype(BF)
     slots = send.shape[1]
     n_seq = g.shape[0] // slots
     for p in range(part // 128):
@@ -448,11 +484,12 @@
     used = part // 128 * n_seq
     if send.shape[0] > used:
         send[used:] = jnp.zeros((send.shape[0] - used,) + send.shape[1:], BF)
-    dw[...] = dot(jnp.transpose(g), attn[...]).astype(BF)
-
-
-def grad_qkv_kernel(idx, recv, xn, wpack, mine, other, dw, both, full):
-    h = idx[0]
+    dw[...] = dot(jnp.transpose(g), attn[...])
+
+
+def grad_qkv_kernel(idx, recv, xn, mine_tok, other_tok, wpack, sums, resid, dw_out, mine, other, keep, give,
+                    both, full, pay, xall):
+    h, c = idx[0], idx[2]
     part = both.shape[1] // 3
     n_seq = both.shape[0] // recv.shape[1]
     for p in range(part // 128):
@@ -461,19 +498,102 @@
             at = k * part + p * 128
             both[:, at : at + 128] = rows[:, k * 128 : (k + 1) * 128]
     g = both[...]
-    full[...] = dot(g, wpack[:, : 3 * part], ANY2)
+    gn = dot(g, wpack[...], ANY2)
+    full[...] = gn
     rows = mine.shape[0]
     mine[...] = full[pl.ds(h * rows, rows), :]
     other[...] = full[pl.ds((1 - h) * rows, rows), :].astype(BF)
-    dw[...] = dot(jnp.transpose(xn[...]), g).astype(BF)
-
-
-def final_kernel(tokens, mine, other, grad_res, small, grad, gain_row):
+    xall[pl.ds(h * rows, rows), :] = mine_tok[...]
+    xall[pl.ds((1 - h) * rows, rows), :] = other_tok[...]
+    x = xall[...].astype(F32)
+    rstd = lax.rsqrt(jnp.mean(x * x, axis=-1, keepdims=True) + EPS)
+    gain_row = jnp.sum(gn * (x * rstd), axis=0, keepdims=True)
+    row = lax.broadcasted_iota(jnp.int32, (sums.shape[0], 1), 0)
+    table = jnp.where(row == C_GAIN1, gain_row, sums[...])
+    table = jnp.concatenate([table, jnp.zeros((128 - table.shape[0], table.shape[1]), F32)], axis=0)
+    columns = jnp.transpose(table)
+    dw = dot(jnp.transpose(xn[...]), g)
+    half, _, owned, _ = pay.shape
+    block = pltpu.roll(resid[:owned, :], RESID, 1)
+    for i in range(half):
+        for j in range(2):
+            at = (2 * i + j) * owned
+            pay[i, j, :, : 3 * part] = dw[at : at + owned]
+            pay[i, j, :, 3 * part : 4 * part] = dw_out[at : at + owned, :]
+            pay[i, j, :, 4 * part :] = columns[at : at + owned] + block
+    for i in range(half):
+        keep[i] = pay[i, c]
+        give[i] = pay[i, 1 - c].astype(BF)
+
+
+def add_kernel(a, b, out):
+    out[...] = (a[...] + b[...].astype(F32)).astype(BF)
+
+
+def total_kernel(recv, dw, dw_out, small):
+    total = recv[0].astype(F32)
+    for i in range(1, recv.shape[0]):
+        total = total + recv[i].astype(F32)
+    part = dw.shape[2]
+    for k in range(3):
+        dw[k] = total[:, k * part : (k + 1) * part]
+    dw_out[...] = total[:, 3 * part : 4 * part]
+    small[...] = total[:, 4 * part :]
+
+
+def small_kernel(n_all, mine, other, gain1, gain2, router, const, vec, resid):
+    total = mine[...] + other[...]
+    rows = jnp.transpose(total)
+    router[...] = rows[:n_all]
+    const[...] = rows[C_CONST:C_VEC]
+    vec[...] = rows[C_VEC : C_VEC + 2]
+    gain1[...] = rows[C_GAIN1 : C_GAIN1 + 1]
+    gain2[...] = rows[C_GAIN2 : C_GAIN2 + 1]
+    resid[...] = total[:n_all, RESID : RESID + n_all]
+
+
+def pair_add_kernel(n, *refs):
+    for i in range(n):
+        refs[2 * n + i][...] = (refs[i][...].astype(F32) + refs[n + i][...].astype(F32)).astype(BF)
+
+
+def place_kernel(e_loc, idx, *refs):
+    came, gin, gdown = refs[:e_loc], refs[e_loc], refs[e_loc + 1]
+    width = gin.shape[0] // (2 * e_loc)
+    strips = width // 256
+    per = strips * 2 * e_loc
+    for q in range(e_loc):
+
+        @pl.when(idx[3] == q)
+        def _():
+            for d in range(e_loc):
+                e = q ^ d
+                for i in range(2):
+                    lanes = slice(i * 128, (i + 1) * 128)
+                    rows = came[d][0:width, lanes].astype(F32)
+                    gin[pl.ds(2 * e + i, width, stride=2 * e_loc), :] = rows
+                    for j in range(strips):
+                        at = width + j * 128
+                        rows = came[d][at : at + 128, lanes].astype(F32)
+                        start = (2 * j + i) * e_loc + e
+                        gdown[pl.ds(start, 128, stride=per), :] = rows
+
+
+def pack_kernel(w_qkv, w_out, router, const, vec, gain1, gain2, out):
+    part = w_out.shape[1]
+    for k in range(3):
+        out[:, k * part : (k + 1) * part] = w_qkv[k]
+    out[:, 3 * part : 4 * part] = w_out[...]
+    rows = [r[...].astype(F32) for r in (router, const, vec, gain1, gain2)]
+    rows.append(jnp.zeros((128 - 20, out.shape[0]), F32))
+    out[:, 4 * part :] = jnp.transpose(jnp.concatenate(rows, axis=0)).astype(BF)
+
+
+def final_kernel(tokens, mine, other, grad_res, small, grad):
     x = tokens[...].astype(F32)
     rstd = lax.rsqrt(jnp.mean(x * x, axis=-1, keepdims=True) + EPS)
     xhat = x * rstd
     gn = mine[...] + other[...].astype(F32)
-    gain_row[...] = jnp.broadcast_to(jnp.sum(gn * xhat, axis=0, keepdims=True), gain_row.shape)
     ghat = gn * small[C_GAIN1 : C_GAIN1 + 1]
     grad[...] = grad_res[...] + rstd * (
         ghat - xhat * jnp.mean(ghat * xhat, axis=-1, keepdims=True)
@@ -488,34 +608,70 @@
     n_all = previous_layer_logits.shape[2]
     tok = seq_dev * slot_dev
     heads = lax.axis_size("head")
-    n_blk = lax.axis_size("blk")
+    ring = lax.axis_size("ring")
+    n_blk = 2 * ring
     n_seq = seq_dev * heads
     n_slots = slot_dev * n_blk
     e_loc = w_in.shape[1]
-    n_share = n_blk // e_loc
+    n_share = ring // e_loc
     unit = w_in.shape[3]
     rows_here = gain_attn.shape[0]
     part = w_qkv.shape[2]
     capacity = 9 * 2 * tok // (8 * n_all)
     h = lax.axis_index("head")
-    b = lax.axis_index("blk")
-    q = b % e_loc
+    ring_at = lax.axis_index("ring")
+    core = lax.axis_index("core")
+    b = ring_at * 2 + core
+    q = ring_at % e_loc
     swap = [(0, 1), (1, 0)]
-    everyone = ("head", "blk")
+    blk = ("ring", "core")
+    barrier = lax.optimization_barrier
 
     def across(x):
         return lax.ppermute(x, "head", swap)
 
+    def partner(x):
+        return lax.ppermute(x, "core", swap)
+
+    def join(parts):
+        total = unit * len(parts)
+        cube = jnp.concatenate([p[:width].reshape(width, 2, unit) for p in parts], axis=2)
+        down = [p[width:].reshape(strips, unit, 2 * unit) for p in parts]
+        down = [jnp.transpose(p, (1, 0, 2)).reshape(unit, -1, 2 * total) for p in down]
+        down = jnp.transpose(jnp.concatenate(down, axis=0), (1, 0, 2))
+        return jnp.concatenate(
+            [cube.reshape(width, 2 * total), down.reshape(-1, 2 * total)], axis=0)
+
+    def divide(full):
+        total = full.shape[1] // 2
+        cube = full[:width].reshape(width, 2, total // unit, unit)
+        down = jnp.transpose(full[width:].reshape(-1, total, 2 * total), (1, 0, 2))
+        down = down.reshape(total // unit, unit, strips, 2 * unit)
+        return [
+            jnp.concatenate(
+                [cube[:, :, d].reshape(width, 2 * unit),
+                 jnp.transpose(down[d], (1, 0, 2)).reshape(-1, 2 * unit)], axis=0)
+            for d in range(total // unit)]
+
     def hop(x, d):
-        return lax.ppermute(x, "blk", [(i, i ^ d) for i in range(n_blk)]) if d else x
-
-    small_cols = jnp.concatenate(
-        [w_router, w_const, const_vec, gain_attn[:, None], gain_ffn[:, None],
-         jnp.zeros((rows_here, 128 - 20), BF)], axis=1)
-    packed = jnp.concatenate([w_qkv.reshape(rows_here, 3 * part), w_out, small_cols], axis=1)
-    wpack = lax.all_gather(packed, "blk", axis=0, tiled=True)
+        return lax.ppermute(x, "ring", [(i, i ^ d) for i in range(ring)]) if d else x
+
+    (packed,) = call(
+        pack_kernel, [sds((rows_here, 4 * part + 128), BF)],
+        [jnp.transpose(w_qkv, (1, 0, 2)), w_out, jnp.transpose(w_router), jnp.transpose(w_const),
+         jnp.transpose(const_vec), gain_attn[None, :], gain_ffn[None, :]],
+        name="pack")
+    wpack = lax.all_gather(packed, blk, axis=0, tiled=True)
     flat_tokens = tokens.reshape(tok, width)
     other_tokens = across(flat_tokens)
+
+    strips = width // (2 * unit)
+    bundle = jnp.concatenate(
+        [jnp.transpose(w_in, (1, 0, 2, 3)).reshape(e_loc, width, 2 * unit),
+         jnp.transpose(w_down.reshape(unit, e_loc, strips, 2 * unit), (1, 2, 0, 3)).reshape(
+             e_loc, strips * unit, 2 * unit)], axis=1)
+
+    shares = [lax.dynamic_index_in_dim(bundle, q ^ d, 0, keepdims=False) for d in range(e_loc)]
 
     positions = b * slot_dev + jnp.arange(slot_dev, dtype=jnp.int32)
     own_len = lax.dynamic_slice_in_dim(lengths, h * seq_dev, seq_dev)
@@ -542,22 +698,12 @@
         name="send_grad")
 
     def to_experts(rows):
-        flat = rows.reshape(heads * n_blk * capacity, rows.shape[-1])
-        return lax.all_to_all(flat, everyone, 0, 0, tiled=True)
+        flat = rows.reshape(heads * ring * capacity, rows.shape[-1])
+        return lax.all_to_all(flat, ("head", "ring"), 0, 0, tiled=True)
 
     g_rows = to_experts(send_g)
-
-    in_by_expert = jnp.transpose(w_in, (1, 0, 2, 3)).reshape(e_loc, width, 2 * unit)
-    down_by_expert = jnp.transpose(w_down, (1, 0, 2))
-    in_pieces = [
-        hop(lax.dynamic_index_in_dim(in_by_expert, q ^ d, 0, keepdims=False), d) for d in range(e_loc)]
-    down_pieces = [
-        hop(lax.dynamic_index_in_dim(down_by_expert, q ^ d, 0, keepdims=False), d) for d in range(e_loc)]
-    joined = unit % 128 != 0
-    if joined:
-        cube = [p.reshape(width, 2, unit) for p in in_pieces]
-        in_pieces = [jnp.concatenate(cube, axis=2).reshape(width, 2 * unit * e_loc)]
-        down_pieces = [jnp.concatenate(down_pieces, axis=0)]
+    g_rows, shares = barrier((g_rows, shares))
+    pieces = [hop(shares[d], d) for d in range(e_loc)]
 
     frequency = 10000.0 ** (-(2.0 * jnp.arange(HD // 2, dtype=F32)) / HD)
     angles = jnp.arange(n_slots, dtype=jnp.int32).astype(F32)[:, None] * frequency[None, :]
@@ -565,157 +711,188 @@
     sin_all = jnp.concatenate([jnp.sin(angles)] * 4, axis=1)
     cos_here = lax.dynamic_slice_in_dim(cos_all, b * slot_dev, slot_dev)
     sin_here = lax.dynamic_slice_in_dim(sin_all, b * slot_dev, slot_dev)
-    idx = jnp.stack([h, lax.dynamic_index_in_dim(lengths, b % n_seq, 0, keepdims=False)])
+    idx = jnp.stack([h, lax.dynamic_index_in_dim(lengths, b % n_seq, 0, keepdims=False), core, q])
     prev = previous_layer_logits.reshape(tok, n_all)
     prev_wide = jnp.pad(prev, ((0, 0), (0, 128 - n_all)))
     prev_logits = jnp.pad(
         jnp.dot(prev, w_residual, precision=lax.Precision.HIGHEST), ((0, 0), (0, 128 - n_all)))
+    (wpack, g_rows, pieces[:-1], prev_wide, prev_logits, cos_all, sin_all, ints, slot_rows) = barrier(
+        (wpack, g_rows, pieces[:-1], prev_wide, prev_logits, cos_all, sin_all, ints, slot_rows))
+
+    w_qkv_all = Columns(wpack, 3 * part, 0)
+    w_out_all = Columns(wpack, part, 3 * part)
+    w_small_all = Columns(wpack, 128, 4 * part)
 
     send_qkv, xn, small = call(
         qkv_kernel,
         [sds((n_blk, slot_dev, 384), BF), sds((n_seq * slot_dev, width), BF), sds((24, width), F32)],
-        [idx, flat_tokens, other_tokens, wpack, cos_here, sin_here], smem=1,
+        [idx, flat_tokens, other_tokens, w_qkv_all, w_small_all, cos_here, sin_here], smem=1,
         scratch=[pltpu.VMEM((n_seq * slot_dev, width), BF)],
-        flops=2 * n_seq * slot_dev * width * 3 * part, name="qkv")
+        flops=2 * n_seq * slot_dev * width * 3 * part, name="qkv", far_in=(3, 4), far_out=(1, 2))
 
     def exchange(x):
         flat = x.reshape(n_blk * slot_dev, x.shape[-1])
-        return lax.all_to_all(flat, "blk", 0, 0, tiled=True)
+        return lax.all_to_all(flat, blk, 0, 0, tiled=True)
 
     qkv = exchange(send_qkv)
+    qkv, pieces[-1] = barrier((qkv, pieces[-1]))
     attn_unit, lse = call(
         attend_kernel, [sds((n_slots, 128), BF), sds((8, n_slots), F32)], [idx, qkv], smem=1,
-        scratch=[pltpu.VMEM((128, n_slots), BF)], flops=2 * n_slots * n_slots * 512, name="attend")
+        scratch=[pltpu.VMEM((128, n_slots), BF)], flops=2 * n_slots * n_slots * 512, name="attend", far_in=(1,), far_out=(0, 1))
     attn_recv = exchange(attn_unit).reshape(n_blk, slot_dev, 128)
+    pieces = pieces + [partner(p) for p in pieces]
     mine, other, attn_low = call(
         out_kernel,
         [sds((tok, width), F32), sds((tok, width), BF), sds((n_seq * slot_dev, part), BF)],
-        [idx, attn_recv, wpack], smem=1, scratch=[pltpu.VMEM((n_seq * slot_dev, width), F32)],
-        flops=2 * n_seq * slot_dev * width * part, name="out")
+        [idx, attn_recv, w_out_all], smem=1, scratch=[pltpu.VMEM((n_seq * slot_dev, width), F32)],
+        flops=2 * n_seq * slot_dev * width * part, name="out", far_in=(2,), far_out=(2,))
     send_x, residual, aux = call(
         route_kernel,
         [sds((heads * n_share, per_send, width + 128), BF), sds((tok, width), F32), sds((tok, 128), F32)],
-        [flat_tokens, mine, across(other), wpack, small, prev_logits, ints, slot_rows],
-        flops=tok * width * 1000, name="route")
+        [flat_tokens, mine, across(other), w_small_all, small, prev_logits, ints, slot_rows],
+        flops=tok * width * 1000, name="route", far_in=(3, 4, 5), far_out=(1, 2))
     x_rows = to_experts(send_x)
-    n = 1 if joined else e_loc
-    results = experts(x_rows, g_rows, in_pieces, down_pieces)
-    back_rows, grad_in_pieces, grad_down_pieces = results[0], results[1 : 1 + n], results[1 + n :]
-    recv = to_experts(back_rows).reshape(heads * n_share, per_send, 2 * width)
-
-    if joined:
-        cube = grad_in_pieces[0].reshape(width, 2, e_loc, unit)
-        grad_in_pieces = [cube[:, :, d].reshape(width, 2 * unit) for d in range(e_loc)]
-        grad_down_pieces = [grad_down_pieces[0][d * unit : (d + 1) * unit] for d in range(e_loc)]
-    came_in = [hop(grad_in_pieces[d], d) for d in range(e_loc)]
-    came_down = [hop(grad_down_pieces[d], d) for d in range(e_loc)]
-
+    x_rows, pieces = barrier((x_rows, pieces))
+    group = max(1, 128 // unit)
+    if group > 1:
+        pieces = [join(pieces[i : i + group]) for i in range(0, len(pieces), group)]
+    back_rows, *grad_pieces = experts(x_rows, g_rows, pieces)
+    back_recv = to_experts(back_rows)
+
+    if group > 1:
+        grad_pieces = [part_of for full in grad_pieces for part_of in divide(full)]
+    ours = list(grad_pieces[:e_loc])
+    theirs = [partner(p) for p in grad_pieces[e_loc:]]
+    recv = back_recv.reshape(heads * n_share, per_send, 2 * width)
+    added = call(
+        functools.partial(pair_add_kernel, e_loc), [sds(p.shape, BF) for p in ours], ours + theirs,
+        name="pair_add", far_in=range(2 * e_loc), far_out=range(e_loc))
+
+    recv, added = barrier((recv, added))
     output, grad_res, grad_low, sums, resid = call(
         combine_kernel,
         [sds((tok, width), F32), sds((tok, width), F32), sds((tok, width), BF), sds((24, width), F32),
          sds((128, 128), F32)],
-        [recv, residual, cot, small, wpack, ints, aux, prev_wide], flops=tok * width * 2000,
-        name="combine")
-
+        [recv, residual, cot, small, w_small_all, ints, aux, prev_wide], flops=tok * width * 2000,
+        name="combine", far_in=(1, 2, 3, 4, 5, 6, 7), far_out=(0, 1, 3, 4))
+
+    came = [hop(added[d], d) for d in range(e_loc)]
     send_gv, dw_out = call(
-        grad_vec_kernel, [sds((n_blk, slot_dev, 128), BF), sds((width, part), BF)],
-        [idx, grad_low, across(grad_low), attn_low, wpack], smem=1,
+        grad_vec_kernel, [sds((n_blk, slot_dev, 128), BF), sds((width, part), F32)],
+        [idx, grad_low, across(grad_low), attn_low, w_out_all], smem=1,
         scratch=[pltpu.VMEM((n_seq * slot_dev, width), BF)],
-        flops=4 * n_seq * slot_dev * width * part, name="grad_vec")
+        flops=4 * n_seq * slot_dev * width * part, name="grad_vec", far_in=(3, 4), far_out=(1,))
     dout = exchange(send_gv)
+    dout, came = barrier((dout, came))
     (grad_unit,) = call(
         attend_back_kernel, [sds((n_slots, 384), BF)],
         [idx, qkv, dout, attn_unit, lse, cos_all, sin_all], smem=1,
         scratch=[pltpu.VMEM((128, n_slots), BF), pltpu.VMEM((n_slots, 128), F32),
                  pltpu.VMEM((n_slots, 128), F32)],
-        flops=5 * n_slots * n_slots * 256, name="attend_back")
+        flops=5 * n_slots * n_slots * 256, name="attend_back", far_in=(1, 3, 4, 5, 6), far_out=())
     grad_recv = exchange(grad_unit).reshape(n_blk, slot_dev, 384)
-    gn_mine, gn_other, dw_qkv = call(
-        grad_qkv_kernel,
-        [sds((tok, width), F32), sds((tok, width), BF), sds((width, 3 * part), BF)],
-        [idx, grad_recv, xn, wpack], smem=1,
-        scratch=[pltpu.VMEM((n_seq * slot_dev, 3 * part), BF),
-                 pltpu.VMEM((n_seq * slot_dev, width), F32)],
-        flops=4 * n_seq * slot_dev * width * 3 * part, name="grad_qkv")
-    grad_tokens, gain_row = call(
-        final_kernel, [sds((tok, width), F32), sds((8, width), F32)],
-        [flat_tokens, gn_mine, across(gn_other), grad_res, small], name="final")
-
-    def own_rows_sum(partial):
-        return lax.psum_scatter(partial, "blk", scatter_dimension=0, tiled=True).astype(F32)
-
-    out_sum = own_rows_sum(dw_out)
-    qkv_sum = own_rows_sum(dw_qkv).reshape(rows_here, 3, part)
-    table = jnp.concatenate(
-        [sums[:C_GAIN1], gain_row[:1], sums[C_GAIN2 : C_GAIN2 + 1]], axis=0)
-    by_owner = jnp.transpose(table.reshape(20, n_blk, rows_here), (1, 0, 2)).reshape(n_blk, -1)
-    extra = jnp.broadcast_to(resid[:n_all, :n_all].reshape(1, -1), (n_blk, n_all * n_all))
-    chunk = jnp.concatenate([by_owner, extra], axis=1)
-    chunk = jnp.concatenate([chunk] * heads, axis=0)
-    total = jnp.sum(lax.all_to_all(chunk, everyone, 0, 0, tiled=True), axis=0)
-    owned = total[: 20 * rows_here].reshape(20, rows_here)
-    resid_sum = total[20 * rows_here :].reshape(n_all, n_all)
-
-    def by_source(pieces):
+    def by_source(parts):
         chosen = []
         for e in range(e_loc):
-            value = pieces[e_loc - 1]
+            value = parts[e_loc - 1]
             for d in range(e_loc - 1):
-                value = jnp.where((q ^ d) == e, pieces[d], value)
+                value = jnp.where((q ^ d) == e, parts[d], value)
             chosen.append(value.astype(F32))
         return chosen
 
-    in_sum = jnp.stack([v.reshape(width, 2, unit) for v in by_source(came_in)], axis=1)
-    down_sum = jnp.stack(by_source(came_down), axis=1)
+    if group == 1:
+        in_sum, down_sum = call(
+            functools.partial(place_kernel, e_loc),
+            [sds((width * e_loc * 2, 128), F32), sds((width // 128 * e_loc * unit, 128), F32)],
+            [idx, *came], smem=1, name="place", far_in=range(1, e_loc + 1), far_out=(0, 1))
+        in_sum = in_sum.reshape(width, e_loc, 2, unit)
+        down_sum = jnp.transpose(down_sum.reshape(unit, -1, e_loc, 128), (0, 2, 1, 3))
+        down_sum = down_sum.reshape(unit, e_loc, width)
+    else:
+        in_sum = jnp.stack(by_source([p[:width].reshape(width, 2, unit) for p in came]), axis=1)
+        down_sum = by_source([p[width:].reshape(strips, unit, 2 * unit) for p in came])
+        down_sum = jnp.transpose(jnp.stack(down_sum, axis=0), (2, 0, 1, 3))
+        down_sum = down_sum.reshape(unit, e_loc, width)
+    grad_recv, in_sum, down_sum = barrier((grad_recv, in_sum, down_sum))
+    pay = (ring, rows_here, 4 * part + 128)
+    gn_mine, gn_other, keep, give = call(
+        grad_qkv_kernel,
+        [sds((tok, width), F32), sds((tok, width), BF), sds(pay, F32), sds(pay, BF)],
+        [idx, grad_recv, xn, flat_tokens, other_tokens, w_qkv_all, sums, resid, dw_out], smem=1,
+        scratch=[pltpu.VMEM((n_seq * slot_dev, 3 * part), BF),
+                 pltpu.VMEM((n_seq * slot_dev, width), F32),
+                 pltpu.VMEM((ring, 2, rows_here, 4 * part + 128), F32),
+                 pltpu.VMEM((n_seq * slot_dev, width), BF)],
+        flops=4 * n_seq * slot_dev * width * 3 * part, name="grad_qkv", far_in=(2, 3, 4, 5, 6, 7, 8), far_out=(0,))
+    gn_came = across(gn_other)
+    (pair_sum,) = call(add_kernel, [sds(pay, BF)], [keep, partner(give)], name="add")
+    ring_recv = lax.all_to_all(pair_sum, "ring", 0, 0, tiled=True)
+    (grad_tokens,) = call(
+        final_kernel, [sds((tok, width), F32)],
+        [flat_tokens, gn_mine, gn_came, grad_res, small], name="final", far_in=(0, 1, 3, 4), far_out=(0,))
+    ring_recv, grad_tokens = barrier((ring_recv, grad_tokens))
+    qkv_sum, out_sum, small_sum = call(
+        total_kernel,
+        [sds((3, rows_here, part), F32), sds((rows_here, part), F32), sds((rows_here, 128), F32)],
+        [ring_recv], name="total")
+    gain1_sum, gain2_sum, router_sum, const_sum, vec_sum, resid_sum = call(
+        functools.partial(small_kernel, n_all),
+        [sds((1, rows_here), F32), sds((1, rows_here), F32), sds((n_all, rows_here), F32),
+         sds((4, rows_here), F32), sds((2, rows_here), F32), sds((n_all, n_all), F32)],
+        [small_sum, across(small_sum)], name="small")
+
     return (
         output.reshape(tokens.shape),
         grad_tokens.reshape(tokens.shape),
-        owned[C_GAIN1],
-        qkv_sum,
+        gain1_sum.reshape(rows_here),
+        jnp.transpose(qkv_sum, (1, 0, 2)),
         out_sum,
-        owned[C_GAIN2],
-        jnp.transpose(owned[:n_all]),
+        gain2_sum.reshape(rows_here),
+        jnp.transpose(router_sum),
         resid_sum,
-        jnp.transpose(owned[C_CONST:C_VEC]),
-        jnp.transpose(owned[C_VEC : C_VEC + 2]),
+        jnp.transpose(const_sum),
+        jnp.transpose(vec_sum),
         in_sum,
         down_sum,
     )
 
 
 def solution(mesh):
+    heads, blocks = mesh.devices.shape
+    split = Mesh(mesh.devices.reshape(heads, blocks // 2, 2), ("head", "ring", "core"))
+    blk = ("ring", "core")
     in_specs = (
-        P("head", "blk", None),
-        P("head", "blk", None),
+        P("head", blk, None),
+        P("head", blk, None),
         P(),
-        P("head", "blk", None),
-        P("head", "blk", None),
-        P("blk"),
-        P("blk", None, "head"),
-        P("blk", "head"),
-        P("blk"),
-        P("blk", None),
+        P("head", blk, None),
+        P("head", blk, None),
+        P(blk),
+        P(blk, None, "head"),
+        P(blk, "head"),
+        P(blk),
+        P(blk, None),
         P(),
-        P("blk", None),
-        P("blk", None),
-        P(None, "head", None, "blk"),
-        P("blk", "head", None),
-        P("head", "blk", None),
+        P(blk, None),
+        P(blk, None),
+        P(None, "head", None, blk),
+        P(blk, "head", None),
+        P("head", blk, None),
     )
     out_specs = (
-        P("head", "blk", None),
-        P("head", "blk", None),
-        P("blk"),
-        P("blk", None, "head"),
-        P("blk", "head"),
-        P("blk"),
-        P("blk", None),
+        P("head", blk, None),
+        P("head", blk, None),
+        P(blk),
+        P(blk, None, "head"),
+        P(blk, "head"),
+        P(blk),
+        P(blk, None),
         P(),
-        P("blk", None),
-        P("blk", None),
-        P(None, "head", None, "blk"),
-        P("blk", "head", None),
+        P(blk, None),
+        P(blk, None),
+        P(None, "head", None, blk),
+        P(blk, "head", None),
     )
     return jax.shard_map(
-        per_device, mesh=mesh, in_specs=in_specs, out_specs=out_specs, check_vma=False
+        per_device, mesh=split, in_specs=in_specs, out_specs=out_specs, check_vma=False
     )

time: 450 us -> 332 us (0.74)
  waiting for transfers between devices: 266 us -> 159 us
  local copies, waits for them, and re-layouts: 65.4 us -> 21.3 us
  Pallas kernels: 33.8 us -> 58.7 us
  starting transfers between devices: 44.6 us -> 53.3 us
    reduce_scatter x2 -> x0, waiting for transfers between devices: 48.9 us -> none  [own_rows_sum(): lax.psum_scatter(partial, 'blk', scatter_dimension=0, tiled=True)]
    all_to_all x7, waiting for transfers between devices: 114 us -> 76 us  [the longest x3 39.7 us: to_experts(): return lax.all_to_all(flat, ('head', 'ring'), 0, 0, tiled=True)]
    all_gather x1, waiting for transfers between devices: 36.4 us -> 0.01 us  [per_device(): wpack = lax.all_gather(packed, blk, axis=0, tiled=True)]
    unnamed x170 -> x90, local copies, waits for them, and re-layouts: 40.2 us -> 13.8 us
    pallas_call x11 -> x17, Pallas kernels: 33.8 us -> 58.7 us  [the longest x16 47.2 us: call(): pl.pallas_call(kernel, grid=(1,), out_shape=shapes, in_specs=[sm] * smem...]
    ppermute x12 -> x15, waiting for transfers between devices: 49.7 us -> 71.4 us  [the longest x6 61.5 us: hop(): lax.ppermute(x, 'ring', [(i, i ^ d) for i in range(ring)])]
    dynamic_slice x1 -> x0, local copies, waits for them, and re-layouts: 6.46 us -> none  [per_device(): lax.dynamic_index_in_dim(in_by_expert, q ^ d, 0, keepdims=False)]
    ppermute x4 -> x5, waiting for transfers between devices: 16.1 us -> 12.1 us  [across(): return lax.ppermute(x, 'head', swap)]
  transfers between devices with their start and end apart: 26 -> 28, of which waited for: 16 -> 24; matrix products, arithmetic and copies ran while one was open for 8% -> 6% of each run, Pallas kernels for 1% -> 5%
where the time goes in v2:
time: 332 us; the launch traced here: 331 us
  waiting for transfers between devices  159 us (48%)
  Pallas kernels  58.7 us (18%)
  starting transfers between devices  53.3 us (16%)
  local copies, waits for them, and re-layouts  21.3 us (6%)
  blocking collectives  15 us (5%)
  between operations  14.5 us (4%)
  other arithmetic  8.33 us (3%)
    ppermute x6, waiting for transfers between devices, hop(): lax.ppermute(x, 'ring', [(i, i ^ d) for i in range(ring)])  61.5 us
    pallas_call x16, Pallas kernels, call(): pl.pallas_call(kernel, grid=(1,), out_shape=shapes, in_specs=[sm] * smem...  47.2 us
    all_to_all x3, waiting for transfers between devices, to_experts(): return lax.all_to_all(flat, ('head', 'ring'), 0, 0, tiled=True)  39.7 us
    all_to_all x1, waiting for transfers between devices, per_device(): ring_recv = lax.all_to_all(pair_sum, 'ring', 0, 0, tiled=True)  22.1 us
    all_to_all x3, starting transfers between devices, to_experts(): return lax.all_to_all(flat, ('head', 'ring'), 0, 0, tiled=True)  16.9 us
    all_to_all x1, blocking collectives, exchange(): return lax.all_to_all(flat, blk, 0, 0, tiled=True)  15 us
    all_to_all x3, waiting for transfers between devices, exchange(): return lax.all_to_all(flat, blk, 0, 0, tiled=True)  14.2 us
    unnamed x90, local copies, waits for them, and re-layouts  13.8 us
  transfers between devices with their start and end apart: 28, of which 24 were waited for; matrix products, arithmetic and copies ran while one was open for 6% of the time, Pallas kernels for 5%

profile of v2, /device:TPU:0, one launch (start us, length us, event | category | flops | bytes accessed | tf_op | source)
XLA Modules:
  0.0 330.7 jit_solution(12458414900921183643)
XLA Ops:
  18.6 8.4 %all-to-all-start = ((bf16[16,24,768]{2,1,0:T(8,128)(2,1)}), bf16[16,24,768]{2,1,0:T(8,128)(2,1)}, u32[]{:S(2)}, u32[]{:S(2)}) async-start(bf16[16,24,768]{2,1,0:T(8,128)(2,1)} %bitcast.20), calls=%async_computation | async-start | bytes 1179648 | tf_op jit(solution)/shard_map/all_to_all | solution.py:702
  37.3 9.5 %all-to-all-done = bf16[16,24,768]{2,1,0:T(8,128)(2,1)} async-done(((bf16[16,24,768]{2,1,0:T(8,128)(2,1)}), bf16[16,24,768]{2,1,0:T(8,128)(2,1)}, u32[]{:S(2)}, u32[]{:S(2)}) %all-to-all-start) | async-done | bytes 589856 | tf_op jit(solution)/shard_map/all_to_all | solution.py:702
  54.0 12.5 %collective-permute-done.1.refs_1_ = bf16[1152,256]{1,0:T(8,128)(2,1)S(1)} collective-permute-done((bf16[1152,256]{1,0:T(8,128)(2,1)}, bf16[1152,256]{1,0:T(8,128)(2,1)S(1)}, u32[]{:S(2)}, u32[]{:S(2)}) %collective-permute-start.1) | collective-permute-done | bytes 589856 | tf_op jit(solution)/shard_map/ppermute | solution.py:657
  73.5 4.9 %all-to-all-start.1 = ((bf16[16,64,384]{2,1,0:T(8,128)(2,1)}), bf16[16,64,384]{2,1,0:T(8,128)(2,1)S(1)}, u32[]{:S(2)}, u32[]{:S(2)}) async-start(bf16[16,64,384]{2,1,0:T(8,128)(2,1)} %get-tuple-element.105), calls=%async_computation.1 | async-start | bytes 1572864 | tf_op jit(solution)/shard_map/all_to_all | solution.py:735
  81.3 26.4 %collective-permute-done.3.refs_3_ = bf16[1152,256]{1,0:T(8,128)(2,1)S(1)} collective-permute-done((bf16[1152,256]{1,0:T(8,128)(2,1)S(1)}, bf16[1152,256]{1,0:T(8,128)(2,1)S(1)}, u32[]{:S(2)}, u32[]{:S(2)}) %collective-permute-start.3) | collective-permute-done | bytes 589856 | tf_op jit(solution)/shard_map/ppermute | solution.py:657
  108.6 6.1 %attend.1 = (bf16[1024,128]{1,0:T(8,128)(2,1)}, f32[8,1024]{1,0:T(8,128)}) custom-call(s32[4]{0:T(128)S(1)} %pad_add_fusion.idx, bf16[1024,384]{1,0:T(8,128)(2,1)} %bitcast.107), custom_call_target="tpu_custom_call" | custom-call | flops 1073741824 | bytes 1081360 | tf_op jit(solution)/shard_map/attend/pallas_call | solution.py:54
  114.7 15.0 %all_to_all.74.recv = bf16[16,64,128]{2,1,0:T(8,128)(2,1)S(1)} all-to-all(bf16[16,64,128]{2,1,0:T(8,128)(2,1)} %bitcast.112), channel_id=1, replica_groups=mesh['head'=2,'ring'=8,'core'=2] {'ring','core'}, dimensions={0} | all-to-all | bytes 524288 | tf_op jit(solution)/shard_map/all_to_all | solution.py:735
  134.0 4.8 %collective-permute-done.4.other = bf16[128,768]{1,0:T(8,128)(2,1)S(1)} collective-permute-done((bf16[128,768]{1,0:T(8,128)(2,1)S(1)}, bf16[128,768]{1,0:T(8,128)(2,1)S(1)}, u32[]{:S(2)}, u32[]{:S(2)}) %collective-permute-start.4) | collective-permute-done | bytes 196640 | tf_op jit(solution)/shard_map/ppermute | solution.py:631
  141.3 4.6 %all-to-all-start.3 = ((bf16[16,24,896]{2,1,0:T(8,128)(2,1)}), bf16[16,24,896]{2,1,0:T(8,128)(2,1)S(1)}, u32[]{:S(2)}, u32[]{:S(2)}) async-start(bf16[16,24,896]{2,1,0:T(8,128)(2,1)} %bitcast.33), calls=%async_computation.3 | async-start | bytes 1376256 | tf_op jit(solution)/shard_map/all_to_all | solution.py:702
  152.2 11.6 %all-to-all-done.3 = bf16[16,24,896]{2,1,0:T(8,128)(2,1)S(1)} async-done(((bf16[16,24,896]{2,1,0:T(8,128)(2,1)}), bf16[16,24,896]{2,1,0:T(8,128)(2,1)S(1)}, u32[]{:S(2)}, u32[]{:S(2)}) %all-to-all-start.3) | async-done | bytes 688160 | tf_op jit(solution)/shard_map/all_to_all | solution.py:702
  163.8 11.5 %experts.1 = (bf16[384,1536]{1,0:T(8,128)(2,1)}, bf16[1152,256]{1,0:T(8,128)(2,1)}, bf16[1152,256]{1,0:T(8,128)(2,1)}, bf16[1152,256]{1,0:T(8,128)(2,1)}, bf16[1...) custom-call(bf16[384,896]{1,0:T(8,128)(2,1)S(1)} %bitcast.94, ...), custom_call_target="tpu_custom_call" | custom-call | flops 5435817984 | bytes 11796480 | tf_op jit(solution)/shard_map/experts/pallas_call | solution.py:360
  175.4 3.9 %all-to-all-start.4 = ((bf16[16,24,1536]{2,1,0:T(8,128)(2,1)}), bf16[16,24,1536]{2,1,0:T(8,128)(2,1)S(1)}, u32[]{:S(2)}, u32[]{:S(2)}) async-start(bf16[16,24,1536]{2,1,0:T(8,128)(2,1)} %bitcast.35), calls=%async_computation.4 | async-start | bytes 2359296 | tf_op jit(solution)/shard_map/all_to_all | solution.py:702
  184.7 3.8 %pair_add.1 = (bf16[1152,256]{1,0:T(8,128)(2,1)}, bf16[1152,256]{1,0:T(8,128)(2,1)}, bf16[1152,256]{1,0:T(8,128)(2,1)}, bf16[1152,256]{1,0:T(8,128)(2,1)}) custom-call(bf16[1152,256]{1,0:T(8,128)(2,1)} %get-tuple-element.131.refs_0_, bf16[1152,256]{1,0:T(8,128)(2,1)} %get-tuple-element.132.refs_1_, bf16[1152,256]{1,0:T(8,128)(2,1)} %get-tuple-element.133.refs_2_, ...), custom_call_target="tpu_custom_call" | custom-call | bytes 7077888 | tf_op jit(solution)/shard_map/pair_add/pallas_call | solution.py:54
  188.5 18.6 %all-to-all-done.4 = bf16[16,24,1536]{2,1,0:T(8,128)(2,1)S(1)} async-done(((bf16[16,24,1536]{2,1,0:T(8,128)(2,1)}), bf16[16,24,1536]{2,1,0:T(8,128)(2,1)S(1)}, u32[]{:S(2)}, u32[]{:S(2)}) %all-to-all-start.4) | async-done | bytes 1179680 | tf_op jit(solution)/shard_map/all_to_all | solution.py:702
  207.2 3.8 %combine.1 = (f32[128,768]{1,0:T(8,128)}, f32[128,768]{1,0:T(8,128)}, bf16[128,768]{1,0:T(8,128)(2,1)S(1)}, f32[24,768]{1,0:T(8,128)}, f32[128,128]{1,0:T(8,128)}) custom-call(bf16[4,96,1536]{2,1,0:T(8,128)(2,1)S(1)} %bitcast.86, f32[128,768]{1,0:T(8,128)} %get-tuple-element.144.residual, f32[128,768]{1,0:T(8,128)} %bitcast.92, ...), custom_call_target="tpu_custom_call" | custom-call | flops 196608000 | bytes 3493888 | tf_op jit(solution)/shard_map/combine/pallas_call | solution.py:54
  223.2 4.7 %collective-permute-done.14.refs_1_ = bf16[1152,256]{1,0:T(8,128)(2,1)S(1)} collective-permute-done((bf16[1152,256]{1,0:T(8,128)(2,1)}, bf16[1152,256]{1,0:T(8,128)(2,1)S(1)}, u32[]{:S(2)}, u32[]{:S(2)}) %collective-permute-start.14) | collective-permute-done | bytes 589856 | tf_op jit(solution)/shard_map/ppermute | solution.py:657
  230.9 11.3 %collective-permute-done.16.refs_3_ = bf16[1152,256]{1,0:T(8,128)(2,1)S(1)} collective-permute-done((bf16[1152,256]{1,0:T(8,128)(2,1)S(1)}, bf16[1152,256]{1,0:T(8,128)(2,1)S(1)}, u32[]{:S(2)}, u32[]{:S(2)}) %collective-permute-start.16) | collective-permute-done | bytes 589856 | tf_op jit(solution)/shard_map/ppermute | solution.py:657
  244.5 7.0 %attend_back.1 = bf16[1024,384]{1,0:T(8,128)(2,1)} custom-call(s32[4]{0:T(128)S(1)} %pad_add_fusion.idx, bf16[1024,384]{1,0:T(8,128)(2,1)} %bitcast.108, bf16[1024,128]{1,0:T(8,128)(2,1)S(1)} %bitcast.95, bf16[1024,128]{1,0:T(8,128)(2,1)} %get-tuple-element.108.out, f32[8,1024]{1,0:T(8,128)} %get-tuple-element.156.lse, f32[1024,128]{1,0:T(8,128)} %copy-done.16, ...), custom_call_target="tpu_custom_call" | custom-call | flops 1342177280 | bytes 3178512 | tf_op jit(solution)/shard_map/attend_back/pallas_call | solution.py:54
  255.1 5.0 %place.1 = (f32[6144,128]{1,0:T(8,128)}, f32[3072,128]{1,0:T(8,128)}) custom-call(s32[4]{0:T(128)S(1)} %pad_add_fusion.idx, bf16[1152,256]{1,0:T(8,128)(2,1)} %get-tuple-element.159.refs_0_, bf16[1152,256]{1,0:T(8,128)(2,1)} %copy-done.22, bf16[1152,256]{1,0:T(8,128)(2,1)} %copy-done.23, bf16[1152,256]{1,0:T(8,128)(2,1)} %copy-done.24), custom_call_target="tpu_custom_call" | custom-call | bytes 7077904 | tf_op jit(solution)/shard_map/place/pallas_call | solution.py:54
  261.9 11.9 %all-to-all-done.6.recv = bf16[16,64,384]{2,1,0:T(8,128)(2,1)S(1)} async-done(((bf16[16,64,384]{2,1,0:T(8,128)(2,1)}), bf16[16,64,384]{2,1,0:T(8,128)(2,1)S(1)}, u32[]{:S(2)}, u32[]{:S(2)}) %all-to-all-start.6) | async-done | bytes 786464 | tf_op jit(solution)/shard_map/all_to_all | solution.py:735
  273.8 3.9 %grad_qkv.1 = (f32[128,768]{1,0:T(8,128)}, bf16[128,768]{1,0:T(8,128)(2,1)S(1)}, f32[8,48,1664]{2,1,0:T(8,128)S(1)}, bf16[8,48,1664]{2,1,0:T(8,128)(2,1)S(1)}) custom-call(s32[4]{0:T(128)S(1)} %pad_add_fusion.idx, bf16[16,64,384]{2,1,0:T(8,128)(2,1)S(1)} %all-to-all-done.6.recv, bf16[256,768]{1,0:T(8,128)(2,1)} %get-tuple-element.166.xn, ...), custom_call_target="tpu_custom_call" | custom-call | flops 905969664 | bytes 9084944 | tf_op jit(solution)/shard_map/grad_qkv/pallas_call | solution.py:54
  282.0 5.4 %all-to-all-start.7 = ((bf16[8,48,1664]{2,1,0:T(8,128)(2,1)}), bf16[8,48,1664]{2,1,0:T(8,128)(2,1)S(1)}, u32[]{:S(2)}, u32[]{:S(2)}) async-start(bf16[8,48,1664]{2,1,0:T(8,128)(2,1)} %add.87), calls=%async_computation.7 | async-start | bytes 2555904 | tf_op jit(solution)/shard_map/all_to_all | solution.py:829
  288.7 5.5 %collective-permute-done.18.other = bf16[128,768]{1,0:T(8,128)(2,1)S(1)} collective-permute-done((bf16[128,768]{1,0:T(8,128)(2,1)S(1)}, bf16[128,768]{1,0:T(8,128)(2,1)S(1)}, u32[]{:S(2)}, u32[]{:S(2)}) %collective-permute-start.18) | collective-permute-done | bytes 196640 | tf_op jit(solution)/shard_map/ppermute | solution.py:631
  296.4 22.1 %all-to-all-done.7.recv = bf16[8,48,1664]{2,1,0:T(8,128)(2,1)S(1)} async-done(((bf16[8,48,1664]{2,1,0:T(8,128)(2,1)}), bf16[8,48,1664]{2,1,0:T(8,128)(2,1)S(1)}, u32[]{:S(2)}, u32[]{:S(2)}) %all-to-all-start.7) | async-done | bytes 1277984 | tf_op jit(solution)/shard_map/all_to_all | solution.py:829
  (176 shorter events, 93.9 us)
Async XLA Ops:
  7.2 62.8 %all-gather.2.cloned.1.call-start = ((), (), s32[]{:S(2)}) async-start(), calls=%async_computation.8 | async-start | bytes 2715648 | tf_op jit(solution)/shard_map/all_gather | solution.py:664
  18.6 28.1 %all-to-all-start = ((bf16[16,24,768]{2,1,0:T(8,128)(2,1)}), bf16[16,24,768]{2,1,0:T(8,128)(2,1)}, u32[]{:S(2)}, u32[]{:S(2)}) async-start(bf16[16,24,768]{2,1,0:T(8,128)(2,1)} %bitcast.20), calls=%async_computation | async-start | bytes 1179648 | tf_op jit(solution)/shard_map/all_to_all | solution.py:702
  27.0 43.0 %collective-permute-start = (bf16[128,768]{1,0:T(8,128)(2,1)S(1)}, bf16[128,768]{1,0:T(8,128)(2,1)S(1)}, u32[]{:S(2)}, u32[]{:S(2)}) collective-permute-start(bf16[128,768]{1,0:T(8,128)(2,1)S(1)} %bitcast.89), channel_id=1, source_target_pairs={{0,16},{16,0},{1,17},{17,1},{2,18},{18,2},{3,19},{19,3},{4,20},{20... | collective-permute-start | bytes 589832 | tf_op jit(solution)/shard_map/ppermute | solution.py:631
  46.7 19.7 %collective-permute-start.1 = (bf16[1152,256]{1,0:T(8,128)(2,1)}, bf16[1152,256]{1,0:T(8,128)(2,1)S(1)}, u32[]{:S(2)}, u32[]{:S(2)}) collective-permute-start(bf16[1152,256]{1,0:T(8,128)(2,1)} %get-tuple-element.102), channel_id=1, source_target_pairs={{0,2},{2,0},{4,6},{6,4},{8,10},{10,8},{12,14},{14,12},{1,3},{3,1},... | collective-permute-start | bytes 1769480 | tf_op jit(solution)/shard_map/ppermute | solution.py:657
  47.3 22.7 %collective-permute-start.2 = (bf16[1152,256]{1,0:T(8,128)(2,1)}, bf16[1152,256]{1,0:T(8,128)(2,1)}, u32[]{:S(2)}, u32[]{:S(2)}) collective-permute-start(bf16[1152,256]{1,0:T(8,128)(2,1)} %get-tuple-element.103), channel_id=1, source_target_pairs={{0,4},{2,6},{4,0},{6,2},{8,12},{10,14},{12,8},{14,10},{1,5},{3,7},... | collective-permute-start | bytes 1769480 | tf_op jit(solution)/shard_map/ppermute | solution.py:657
  73.5 34.2 %all-to-all-start.1 = ((bf16[16,64,384]{2,1,0:T(8,128)(2,1)}), bf16[16,64,384]{2,1,0:T(8,128)(2,1)S(1)}, u32[]{:S(2)}, u32[]{:S(2)}) async-start(bf16[16,64,384]{2,1,0:T(8,128)(2,1)} %get-tuple-element.105), calls=%async_computation.1 | async-start | bytes 1572864 | tf_op jit(solution)/shard_map/all_to_all | solution.py:735
  78.4 29.3 %collective-permute-start.3 = (bf16[1152,256]{1,0:T(8,128)(2,1)S(1)}, bf16[1152,256]{1,0:T(8,128)(2,1)S(1)}, u32[]{:S(2)}, u32[]{:S(2)}) collective-permute-start(bf16[1152,256]{1,0:T(8,128)(2,1)S(1)} %copy-done.27), channel_id=1, source_target_pairs={{0,6},{2,4},{4,2},{6,0},{8,14},{10,12},{12,10},{14,8},{1,7},{3,5},... | collective-permute-start | bytes 1769480 | tf_op jit(solution)/shard_map/ppermute | solution.py:657
  131.6 7.2 %collective-permute-start.4 = (bf16[128,768]{1,0:T(8,128)(2,1)S(1)}, bf16[128,768]{1,0:T(8,128)(2,1)S(1)}, u32[]{:S(2)}, u32[]{:S(2)}) collective-permute-start(bf16[128,768]{1,0:T(8,128)(2,1)S(1)} %get-tuple-element.110), channel_id=1, source_target_pairs={{0,16},{16,0},{1,17},{17,1},{2,18},{18,2},{3,19},{19,3},{4,20},{20... | collective-permute-start | bytes 589832 | tf_op jit(solution)/shard_map/ppermute | solution.py:631
  141.3 22.5 %all-to-all-start.3 = ((bf16[16,24,896]{2,1,0:T(8,128)(2,1)}), bf16[16,24,896]{2,1,0:T(8,128)(2,1)S(1)}, u32[]{:S(2)}, u32[]{:S(2)}) async-start(bf16[16,24,896]{2,1,0:T(8,128)(2,1)} %bitcast.33), calls=%async_computation.3 | async-start | bytes 1376256 | tf_op jit(solution)/shard_map/all_to_all | solution.py:702
  146.1 4.5 %collective-permute-start.6 = (bf16[1152,256]{1,0:T(8,128)(2,1)S(1)}, bf16[1152,256]{1,0:T(8,128)(2,1)S(1)}, u32[]{:S(2)}, u32[]{:S(2)}) collective-permute-start(bf16[1152,256]{1,0:T(8,128)(2,1)S(1)} %copy-done.32), channel_id=1, source_target_pairs={{0,1},{1,0},{2,3},{3,2},{4,5},{5,4},{6,7},{7,6},{8,9},{9,8},{10,11... | collective-permute-start | bytes 1769480 | tf_op jit(solution)/shard_map/ppermute | solution.py:634
  146.6 4.2 %collective-permute-start.7 = (bf16[1152,256]{1,0:T(8,128)(2,1)}, bf16[1152,256]{1,0:T(8,128)(2,1)S(1)}, u32[]{:S(2)}, u32[]{:S(2)}) collective-permute-start(bf16[1152,256]{1,0:T(8,128)(2,1)} %collective-permute-done.2.refs_2_), channel_id=1, source_target_pairs={{0,1},{1,0},{2,3},{3,2},{4,5},{5,4},{6,7},{7,6},{8,9},{9,8},{10,11... | collective-permute-start | bytes 1769480 | tf_op jit(solution)/shard_map/ppermute | solution.py:634
  146.6 5.6 %collective-permute-start.8 = (bf16[1152,256]{1,0:T(8,128)(2,1)S(1)}, bf16[1152,256]{1,0:T(8,128)(2,1)}, u32[]{:S(2)}, u32[]{:S(2)}) collective-permute-start(bf16[1152,256]{1,0:T(8,128)(2,1)S(1)} %collective-permute-done.3.refs_3_), channel_id=1, source_target_pairs={{0,1},{1,0},{2,3},{3,2},{4,5},{5,4},{6,7},{7,6},{8,9},{9,8},{10,11... | collective-permute-start | bytes 1769480 | tf_op jit(solution)/shard_map/ppermute | solution.py:634
  175.4 31.8 %all-to-all-start.4 = ((bf16[16,24,1536]{2,1,0:T(8,128)(2,1)}), bf16[16,24,1536]{2,1,0:T(8,128)(2,1)S(1)}, u32[]{:S(2)}, u32[]{:S(2)}) async-start(bf16[16,24,1536]{2,1,0:T(8,128)(2,1)} %bitcast.35), calls=%async_computation.4 | async-start | bytes 2359296 | tf_op jit(solution)/shard_map/all_to_all | solution.py:702
  179.8 3.2 collective-permute-start.11
  179.9 3.9 %collective-permute-start.12 = (bf16[1152,256]{1,0:T(8,128)(2,1)S(1)}, bf16[1152,256]{1,0:T(8,128)(2,1)S(1)}, u32[]{:S(2)}, u32[]{:S(2)}) collective-permute-start(bf16[1152,256]{1,0:T(8,128)(2,1)S(1)} %copy-done.35), channel_id=1, source_target_pairs={{0,1},{1,0},{2,3},{3,2},{4,5},{5,4},{6,7},{7,6},{8,9},{9,8},{10,11... | collective-permute-start | bytes 1769480 | tf_op jit(solution)/shard_map/ppermute | solution.py:634
  210.9 5.7 %collective-permute-start.13 = (bf16[128,768]{1,0:T(8,128)(2,1)S(1)}, bf16[128,768]{1,0:T(8,128)(2,1)S(1)}, u32[]{:S(2)}, u32[]{:S(2)}) collective-permute-start(bf16[128,768]{1,0:T(8,128)(2,1)S(1)} %get-tuple-element.148.mine), channel_id=1, source_target_pairs={{0,16},{16,0},{1,17},{17,1},{2,18},{18,2},{3,19},{19,3},{4,20},{20... | collective-permute-start | bytes 589832 | tf_op jit(solution)/shard_map/ppermute | solution.py:631
  212.4 15.5 %collective-permute-start.14 = (bf16[1152,256]{1,0:T(8,128)(2,1)}, bf16[1152,256]{1,0:T(8,128)(2,1)S(1)}, u32[]{:S(2)}, u32[]{:S(2)}) collective-permute-start(bf16[1152,256]{1,0:T(8,128)(2,1)} %get-tuple-element.152), channel_id=1, source_target_pairs={{0,2},{2,0},{4,6},{6,4},{8,10},{10,8},{12,14},{14,12},{1,3},{3,1},... | collective-permute-start | bytes 1769480 | tf_op jit(solution)/shard_map/ppermute | solution.py:657
  213.0 17.9 %collective-permute-start.15 = (bf16[1152,256]{1,0:T(8,128)(2,1)}, bf16[1152,256]{1,0:T(8,128)(2,1)S(1)}, u32[]{:S(2)}, u32[]{:S(2)}) collective-permute-start(bf16[1152,256]{1,0:T(8,128)(2,1)} %get-tuple-element.153), channel_id=1, source_target_pairs={{0,4},{2,6},{4,0},{6,2},{8,12},{10,14},{12,8},{14,10},{1,5},{3,7},... | collective-permute-start | bytes 1769480 | tf_op jit(solution)/shard_map/ppermute | solution.py:657
  214.4 27.9 %collective-permute-start.16 = (bf16[1152,256]{1,0:T(8,128)(2,1)S(1)}, bf16[1152,256]{1,0:T(8,128)(2,1)S(1)}, u32[]{:S(2)}, u32[]{:S(2)}) collective-permute-start(bf16[1152,256]{1,0:T(8,128)(2,1)S(1)} %copy-done.34), channel_id=1, source_target_pairs={{0,6},{2,4},{4,2},{6,0},{8,14},{10,12},{12,10},{14,8},{1,7},{3,5},... | collective-permute-start | bytes 1769480 | tf_op jit(solution)/shard_map/ppermute | solution.py:657
  219.4 25.1 %all-to-all-start.5 = ((bf16[16,64,128]{2,1,0:T(8,128)(2,1)}), bf16[16,64,128]{2,1,0:T(8,128)(2,1)S(1)}, u32[]{:S(2)}, u32[]{:S(2)}) async-start(bf16[16,64,128]{2,1,0:T(8,128)(2,1)} %get-tuple-element.150), calls=%async_computation.5 | async-start | bytes 524288 | tf_op jit(solution)/shard_map/all_to_all | solution.py:735
  251.5 22.3 %all-to-all-start.6 = ((bf16[16,64,384]{2,1,0:T(8,128)(2,1)}), bf16[16,64,384]{2,1,0:T(8,128)(2,1)S(1)}, u32[]{:S(2)}, u32[]{:S(2)}) async-start(bf16[16,64,384]{2,1,0:T(8,128)(2,1)} %bitcast.39), calls=%async_computation.6 | async-start | bytes 1572864 | tf_op jit(solution)/shard_map/all_to_all | solution.py:735
  282.0 36.5 %all-to-all-start.7 = ((bf16[8,48,1664]{2,1,0:T(8,128)(2,1)}), bf16[8,48,1664]{2,1,0:T(8,128)(2,1)S(1)}, u32[]{:S(2)}, u32[]{:S(2)}) async-start(bf16[8,48,1664]{2,1,0:T(8,128)(2,1)} %add.87), calls=%async_computation.7 | async-start | bytes 2555904 | tf_op jit(solution)/shard_map/all_to_all | solution.py:829
  287.4 6.8 %collective-permute-start.18 = (bf16[128,768]{1,0:T(8,128)(2,1)S(1)}, bf16[128,768]{1,0:T(8,128)(2,1)S(1)}, u32[]{:S(2)}, u32[]{:S(2)}) collective-permute-start(bf16[128,768]{1,0:T(8,128)(2,1)S(1)} %get-tuple-element.173), channel_id=1, source_target_pairs={{0,16},{16,0},{1,17},{17,1},{2,18},{18,2},{3,19},{19,3},{4,20},{20... | collective-permute-start | bytes 589832 | tf_op jit(solution)/shard_map/ppermute | solution.py:631
  319.4 3.8 %collective-permute-start.19 = (f32[48,128]{1,0:T(8,128)S(1)}, f32[48,128]{1,0:T(8,128)S(1)}, u32[]{:S(2)}, u32[]{:S(2)}) collective-permute-start(f32[48,128]{1,0:T(8,128)S(1)} %get-tuple-element.177.mine), channel_id=1, source_target_pairs={{0,16},{16,0},{1,17},{17,1},{2,18},{18,2},{3,19},{19,3},{4,20},{20... | collective-permute-start | bytes 73736 | tf_op jit(solution)/shard_map/ppermute | solution.py:631
  (46 other events, 350.2 us)
Sparse Core Ops, SparseCore 0:
  13.1 55.5 all-gather.1

commit v3 on v2

--- a/solution.py
+++ b/solution.py
@@ -3,6 +3,7 @@
 
 import jax
 import jax.numpy as jnp
+import numpy as np
 from jax import lax
 from jax.experimental import pallas as pl
 from jax.experimental.pallas import tpu as pltpu
@@ -20,6 +21,7 @@
 MM = (((1,), (0,)), ((), ()))
 C_CONST, C_VEC, C_GAIN1, C_GAIN2 = 12, 16, 18, 19
 RESID = 32
+S_HEAD, S_LEN, S_CORE, S_EXPERT, S_BLOCK, S_BIT, S_TABLE = 0, 1, 2, 3, 4, 5, 8
 
 
 def dot(a, b, dims=MM):
@@ -68,6 +70,32 @@
     return jax.ShapeDtypeStruct(shape, dtype)
 
 
+def unit_at(seq, pair):
+    ring = (seq >> 1) * 4 + (pair >> 1) * 2 + (seq & 1)
+    return ring * 2 + (pair & 1)
+
+
+def idle_units(n_blk, n_seq, pairs):
+    busy = {unit_at(q, p) for q in range(n_seq) for p in range(pairs)}
+    return [u for u in range(n_blk) if u not in busy]
+
+
+def halving_order(n):
+    bits = n.bit_length() - 1
+    return [sum(((k >> i) & 1) << (bits - 1 - i) for i in range(bits)) for k in range(n)]
+
+
+def gather_rows(dst, arrays, idx, base, rows):
+    j = base
+    for a in arrays:
+        for i in range(a.shape[0] // rows):
+            at = idx[j] * rows
+            if rows % 16 == 0:
+                at = pl.multiple_of(at, 16)
+            dst[pl.ds(at, rows), :] = a[i * rows : (i + 1) * rows, :]
+            j += 1
+
+
 def lower_lanes(shape):
     return (lax.broadcasted_iota(jnp.int32, shape, 1) & 63) < 32
 
@@ -76,40 +104,6 @@
     return jnp.where(
         lower_lanes(values.shape), -pltpu.roll(values, 96, 1), pltpu.roll(values, 32, 1)
     )
-
-
-def qkv_kernel(idx, mine, other, wq, wsmall, cos, sin, send, xn, small, xall):
-    h = idx[0]
-    rows = mine.shape[0]
-    xall[pl.ds(h * rows, rows), :] = mine[...]
-    xall[pl.ds((1 - h) * rows, rows), :] = other[...]
-    width = mine.shape[1]
-    small_t = jnp.transpose(wsmall[...].astype(F32))
-    small[...] = small_t[: small.shape[0]]
-    x = xall[...].astype(F32)
-    rstd = lax.rsqrt(jnp.mean(x * x, axis=-1, keepdims=True) + EPS)
-    normed = (x * rstd * small_t[C_GAIN1 : C_GAIN1 + 1]).astype(BF)
-    xn[...] = normed
-    part = wq.shape[1] // 3
-    pairs = part // 128
-    y = dot(normed, wq[...])
-    slots = cos.shape[0]
-    n_seq = xall.shape[0] // slots
-    c = jnp.concatenate([cos[...]] * n_seq, axis=0)
-    s = jnp.concatenate([sin[...]] * n_seq, axis=0)
-    for p in range(pairs):
-        for k in range(3):
-            piece = y[:, k * part + p * 128 : k * part + (p + 1) * 128]
-            if k < 2:
-                piece = piece * c + turned(piece) * s
-            if k == 0:
-                piece = piece * (1.0 / math.sqrt(HD))
-            piece = piece.astype(BF)
-            for q in range(n_seq):
-                send[p * n_seq + q, :, k * 128 : (k + 1) * 128] = piece[q * slots : (q + 1) * slots]
-    used = pairs * n_seq
-    if send.shape[0] > used:
-        send[used:] = jnp.zeros((send.shape[0] - used,) + send.shape[1:], BF)
 
 
 def head_mask(shape, which):
@@ -140,10 +134,38 @@
             fn(pl.multiple_of(i * block, block), total)
 
 
-def attend_kernel(idx, qkv, out, lse, vt):
+def attend_kernel(n_x, n_w, n_p, w_rows, p_rows, idx, *refs):
+    xs, ws, ps = refs[:n_x], refs[n_x : n_x + n_w], refs[n_x + n_w : n_x + n_w + n_p]
+    cos, sin, out, lse, xn, qkv, early, vt, wg = refs[n_x + n_w + n_p :]
     total = qkv.shape[0]
     block = 256
-    limit_len = idx[1]
+    slots = 64
+    limit_len = idx[S_LEN]
+    j = S_TABLE + sum(a.shape[0] // slots for a in xs)
+    gather_rows(wg, ws, idx, j, w_rows)
+    gather_rows(early, ps, idx, j + sum(a.shape[0] // w_rows for a in ws), p_rows)
+    columns = early[:, early.shape[1] - 128 :].astype(F32)
+    gain = jnp.transpose(columns)[C_GAIN1 : C_GAIN1 + 1]
+    j = S_TABLE
+    for a in xs:
+        for i in range(a.shape[0] // slots):
+            x = a[i * slots : (i + 1) * slots, :].astype(F32)
+            rstd = lax.rsqrt(jnp.mean(x * x, axis=-1, keepdims=True) + EPS)
+            at = pl.ds(pl.multiple_of(idx[j] * slots, slots), slots)
+            xn[at, :] = (x * rstd * gain).astype(BF)
+            j += 1
+
+    def project(start, _):
+        at = pl.ds(start, block)
+        y = dot(xn[at, :], wg[...])
+        c, s = cos[at, :], sin[at, :]
+        q, k = y[:, 0:128], y[:, 128:256]
+        q = (q * c + turned(q) * s) * (1.0 / math.sqrt(HD))
+        qkv[at, 0:128] = q.astype(BF)
+        qkv[at, 128:256] = (k * c + turned(k) * s).astype(BF)
+        qkv[at, 256:384] = y[:, 256:384].astype(BF)
+
+    each_block(total, block, project)
     vt[...] = jnp.transpose(qkv[:, 256:384])
 
     def step(start, n_keys):
@@ -162,10 +184,14 @@
     each_block(total, block, step)
 
 
+def unit_dw_kernel(xn, grad, dw):
+    dw[...] = dot(jnp.transpose(xn[...]), grad[...]).astype(BF)
+
+
 def attend_back_kernel(idx, qkv, dout, out, lse, cos, sin, grad, kt, dk, dv):
     total = qkv.shape[0]
     block = 256
-    limit_len = idx[1]
+    limit_len = idx[S_LEN]
     kt[...] = jnp.transpose(qkv[:, 128:256])
     dk[...] = jnp.zeros_like(dk)
     dv[...] = jnp.zeros_like(dv)
@@ -206,14 +232,15 @@
     each_block(total, block, finish)
 
 
-def out_kernel(idx, recv, wpack, mine, other, attn, full):
-    h = idx[0]
+def out_kernel(idx, recv, wos, mine, other, attn, full):
+    h = idx[S_HEAD]
     part = attn.shape[1]
-    n_seq = attn.shape[0] // recv.shape[1]
+    slots = recv.shape[1]
+    n_seq = attn.shape[0] // slots
     for p in range(part // 128):
-        rows = recv[p * n_seq : (p + 1) * n_seq].reshape(attn.shape[0], 128)
-        attn[:, p * 128 : (p + 1) * 128] = rows
-    full[...] = dot(attn[...], wpack[...], ANY2)
+        for q in range(n_seq):
+            attn[q * slots : (q + 1) * slots, p * 128 : (p + 1) * 128] = recv[unit_at(q, p)]
+    full[...] = dot(attn[...], wos[...], ANY2)
     rows = mine.shape[0]
     mine[...] = full[pl.ds(h * rows, rows), :]
     other[...] = full[pl.ds((1 - h) * rows, rows), :].astype(BF)
@@ -244,9 +271,10 @@
     return rstd, xhat, xhat * gain
 
 
-def route_kernel(tokens, mine, other, wpack, small, prev_logits, ints, slots, send, residual, aux):
+def route_kernel(tokens, mine, other, wpack, prev_logits, ints, slots, send, residual, aux, small):
     res = tokens[...].astype(F32) + mine[...] + other[...].astype(F32)
     residual[...] = res
+    small[...] = jnp.transpose(wpack[...].astype(F32))[: small.shape[0]]
     _, _, normed = norm_two(res, small[C_GAIN2 : C_GAIN2 + 1])
     low = normed.astype(BF)
     logits = dot(low, wpack[...]) + prev_logits[...]
@@ -468,86 +496,94 @@
     grad_low[...] = grad.astype(BF)
 
 
-def grad_vec_kernel(idx, mine, other, attn, wpack, send, dw, both):
-    h = idx[0]
+def grad_vec_kernel(idx, mine, other, attn, wos, sums, resid, send, keep, give, both, pay):
+    h = idx[S_HEAD]
     rows = mine.shape[0]
     both[pl.ds(h * rows, rows), :] = mine[...]
     both[pl.ds((1 - h) * rows, rows), :] = other[...]
     part = attn.shape[1]
     g = both[...]
-    gv = dot(g, wpack[...]).astype(BF)
+    gv = dot(g, wos[...]).astype(BF)
     slots = send.shape[1]
     n_seq = g.shape[0] // slots
     for p in range(part // 128):
-        for s in range(n_seq):
-            send[p * n_seq + s] = gv[s * slots : (s + 1) * slots, p * 128 : (p + 1) * 128]
-    used = part // 128 * n_seq
-    if send.shape[0] > used:
-        send[used:] = jnp.zeros((send.shape[0] - used,) + send.shape[1:], BF)
-    dw[...] = dot(jnp.transpose(g), attn[...])
-
-
-def grad_qkv_kernel(idx, recv, xn, mine_tok, other_tok, wpack, sums, resid, dw_out, mine, other, keep, give,
-                    both, full, pay, xall):
-    h, c = idx[0], idx[2]
+        for q in range(n_seq):
+            send[unit_at(q, p)] = gv[q * slots : (q + 1) * slots, p * 128 : (p + 1) * 128]
+    for u in idle_units(send.shape[0], n_seq, part // 128):
+        send[u] = jnp.zeros(send.shape[1:], BF)
+    dw = dot(jnp.transpose(g), attn[...])
+    table = jnp.concatenate([sums[...], jnp.zeros((128 - sums.shape[0], sums.shape[1]), F32)], axis=0)
+    columns = jnp.transpose(table)
+    n, owned, _ = pay.shape
+    block = pltpu.roll(resid[:owned, :], RESID, 1)
+    for i in range(n):
+        at = i * owned
+        pay[i, :, :part] = dw[at : at + owned]
+        pay[i, :, part:] = columns[at : at + owned] + block
+    for k, offset in enumerate(halving_order(n)):
+        value = pay[idx[S_BLOCK] ^ offset]
+        if k < n // 2:
+            keep[k] = value
+        else:
+            give[k - n // 2] = value.astype(BF)
+
+
+def halve_kernel(mine, came, keep, give):
+    half = keep.shape[0]
+    keep[...] = mine[:half] + came[:half].astype(F32)
+    give[...] = (mine[half:] + came[half:].astype(F32)).astype(BF)
+
+
+def last_add_kernel(mine, came, dw, table):
+    total = mine[0] + came[0].astype(F32)
+    dw[...] = total[:, : dw.shape[1]]
+    table[...] = total[:, dw.shape[1] :]
+
+
+def grad_qkv_kernel(n_w, rows_here, base, idx, recv, *refs):
+    ws = refs[:n_w]
+    mine, other, both, full, wall = refs[n_w:]
+    h = idx[S_HEAD]
     part = both.shape[1] // 3
-    n_seq = both.shape[0] // recv.shape[1]
+    slots = recv.shape[1]
+    n_seq = both.shape[0] // slots
+    gather_rows(wall, ws, idx, base, rows_here)
     for p in range(part // 128):
-        rows = recv[p * n_seq : (p + 1) * n_seq].reshape(both.shape[0], 384)
-        for k in range(3):
-            at = k * part + p * 128
-            both[:, at : at + 128] = rows[:, k * 128 : (k + 1) * 128]
-    g = both[...]
-    gn = dot(g, wpack[...], ANY2)
-    full[...] = gn
+        for q in range(n_seq):
+            unit = recv[unit_at(q, p)]
+            for k in range(3):
+                at = k * part + p * 128
+                both[q * slots : (q + 1) * slots, at : at + 128] = unit[:, k * 128 : (k + 1) * 128]
+    full[...] = dot(both[...], wall[...], ANY2)
     rows = mine.shape[0]
     mine[...] = full[pl.ds(h * rows, rows), :]
     other[...] = full[pl.ds((1 - h) * rows, rows), :].astype(BF)
-    xall[pl.ds(h * rows, rows), :] = mine_tok[...]
-    xall[pl.ds((1 - h) * rows, rows), :] = other_tok[...]
-    x = xall[...].astype(F32)
-    rstd = lax.rsqrt(jnp.mean(x * x, axis=-1, keepdims=True) + EPS)
-    gain_row = jnp.sum(gn * (x * rstd), axis=0, keepdims=True)
-    row = lax.broadcasted_iota(jnp.int32, (sums.shape[0], 1), 0)
-    table = jnp.where(row == C_GAIN1, gain_row, sums[...])
-    table = jnp.concatenate([table, jnp.zeros((128 - table.shape[0], table.shape[1]), F32)], axis=0)
-    columns = jnp.transpose(table)
-    dw = dot(jnp.transpose(xn[...]), g)
-    half, _, owned, _ = pay.shape
-    block = pltpu.roll(resid[:owned, :], RESID, 1)
-    for i in range(half):
-        for j in range(2):
-            at = (2 * i + j) * owned
-            pay[i, j, :, : 3 * part] = dw[at : at + owned]
-            pay[i, j, :, 3 * part : 4 * part] = dw_out[at : at + owned, :]
-            pay[i, j, :, 4 * part :] = columns[at : at + owned] + block
-    for i in range(half):
-        keep[i] = pay[i, c]
-        give[i] = pay[i, 1 - c].astype(BF)
-
-
-def add_kernel(a, b, out):
-    out[...] = (a[...] + b[...].astype(F32)).astype(BF)
-
-
-def total_kernel(recv, dw, dw_out, small):
-    total = recv[0].astype(F32)
-    for i in range(1, recv.shape[0]):
-        total = total + recv[i].astype(F32)
+
+
+def total_kernel(recv, w, gain, dw, gain_row):
     part = dw.shape[2]
-    for k in range(3):
-        dw[k] = total[:, k * part : (k + 1) * part]
-    dw_out[...] = total[:, 3 * part : 4 * part]
-    small[...] = total[:, 4 * part :]
-
-
-def small_kernel(n_all, mine, other, gain1, gain2, router, const, vec, resid):
+    owned = dw.shape[1]
+    column = jnp.transpose(jnp.broadcast_to(gain[...].astype(F32), (8, owned)))[:, 0:1]
+    rowsum = jnp.zeros((owned, 1), F32)
+    for p in range(part // 128):
+        total = recv[unit_at(0, p)].astype(F32)
+        for q in range(1, 4):
+            total = total + recv[unit_at(q, p)].astype(F32)
+        for k in range(3):
+            piece = total[:, k * 128 : (k + 1) * 128]
+            at = slice(p * 128, (p + 1) * 128)
+            rowsum = rowsum + jnp.sum(piece * w[k, :, at].astype(F32), axis=1, keepdims=True)
+            dw[k, :, at] = piece
+    rowsum = rowsum / column
+    gain_row[...] = jnp.transpose(jnp.broadcast_to(rowsum, (owned, 128)))[: gain_row.shape[0]]
+
+
+def small_kernel(n_all, mine, other, gain2, router, const, vec, resid):
     total = mine[...] + other[...]
     rows = jnp.transpose(total)
     router[...] = rows[:n_all]
     const[...] = rows[C_CONST:C_VEC]
     vec[...] = rows[C_VEC : C_VEC + 2]
-    gain1[...] = rows[C_GAIN1 : C_GAIN1 + 1]
     gain2[...] = rows[C_GAIN2 : C_GAIN2 + 1]
     resid[...] = total[:n_all, RESID : RESID + n_all]
 
@@ -564,7 +600,7 @@
     per = strips * 2 * e_loc
     for q in range(e_loc):
 
-        @pl.when(idx[3] == q)
+        @pl.when(idx[S_EXPERT] == q)
         def _():
             for d in range(e_loc):
                 e = q ^ d
@@ -579,14 +615,27 @@
                         gdown[pl.ds(start, 128, stride=per), :] = rows
 
 
-def pack_kernel(w_qkv, w_out, router, const, vec, gain1, gain2, out):
+def pack_kernel(idx, w_qkv, w_out, router, const, vec, gain1, gain2, keep, swap, give, early, late, pairs):
     part = w_out.shape[1]
+    owned = w_out.shape[0]
+    rows = [r[...].astype(F32) for r in (router, const, vec, gain1, gain2)]
+    rows.append(jnp.zeros((128 - 20, owned), F32))
+    columns = jnp.transpose(jnp.concatenate(rows, axis=0))
+    early[:, :part] = w_out[...]
+    early[:, part:] = columns.astype(BF)
     for k in range(3):
-        out[:, k * part : (k + 1) * part] = w_qkv[k]
-    out[:, 3 * part : 4 * part] = w_out[...]
-    rows = [r[...].astype(F32) for r in (router, const, vec, gain1, gain2)]
-    rows.append(jnp.zeros((128 - 20, out.shape[0]), F32))
-    out[:, 4 * part :] = jnp.transpose(jnp.concatenate(rows, axis=0)).astype(BF)
+        late[:, k * part : (k + 1) * part] = w_qkv[k]
+        for p in range(4):
+            if p < part // 128:
+                pairs[p, :, k * 128 : (k + 1) * 128] = w_qkv[k, :, p * 128 : (p + 1) * 128]
+            else:
+                pairs[p, :, k * 128 : (k + 1) * 128] = jnp.zeros((owned, 128), BF)
+    near, away = 2 * idx[S_BIT], 2 * (1 - idx[S_BIT])
+    core = idx[S_CORE]
+    keep[...] = pairs[near + core]
+    swap[...] = pairs[away + core]
+    give[:owned, :] = pairs[near + 1 - core]
+    give[owned:, :] = pairs[away + 1 - core]
 
 
 def final_kernel(tokens, mine, other, grad_res, small, grad):
@@ -656,22 +705,80 @@
     def hop(x, d):
         return lax.ppermute(x, "ring", [(i, i ^ d) for i in range(ring)]) if d else x
 
-    (packed,) = call(
-        pack_kernel, [sds((rows_here, 4 * part + 128), BF)],
-        [jnp.transpose(w_qkv, (1, 0, 2)), w_out, jnp.transpose(w_router), jnp.transpose(w_const),
-         jnp.transpose(const_vec), gain_attn[None, :], gain_ffn[None, :]],
-        name="pack")
-    wpack = lax.all_gather(packed, blk, axis=0, tiled=True)
+    bit = [(ring_at >> i) & 1 for i in range(3)]
+    more = [1 << i for i in range(3, ring.bit_length() - 1)]
+    both_axes = ("head", "ring")
+
+    def to_head(same):
+        pairs = []
+        for i in range(heads):
+            for r in range(ring):
+                third = (r >> 2) & 1
+                target = third if same else 1 - third
+                pairs.append((i * ring + r, target * ring + ((r & ~4) | (i << 2))))
+        return pairs
+
+    def xor_blocks(ring_base, offsets):
+        ring_off = np.array([d for d, _ in offsets], np.int32)
+        core_off = np.array([k for _, k in offsets], np.int32)
+        return (ring_base ^ ring_off) * 2 + (core ^ core_off)
+
+    seq_base = (ring_at & ~4) | (h << 2)
+    x_off = [(0, 0), (1, 0), (4, 0), (5, 0)]
+    for d in more:
+        x_off = x_off + [(r ^ d, k) for r, k in x_off]
+    x_off = x_off + [(r ^ 2, k) for r, k in x_off]
+    x_off = x_off + [(r, 1) for r, _ in x_off]
+    w_off = [(0, 0), (0, 1), (2, 0), (2, 1)]
+    w_off = w_off + [(r ^ 4, k) for r, k in w_off]
+    w_off = w_off + [(r ^ 1, k) for r, k in w_off]
+    p_off = [(0, 0)]
+    for d in (4, 2, 1):
+        p_off = p_off + [(r ^ d, 0) for r, _ in p_off]
+    p_off = p_off + [(r, 1) for r, _ in p_off]
+    direct = ring == 8
+    seq = 2 * bit[2] + bit[0]
+    seq_len = lax.dynamic_index_in_dim(lengths, seq, 0, keepdims=False)
+    scalars = [jnp.stack([h, seq_len, core, q, b, bit[1], h * 0, h * 0]), xor_blocks(seq_base, x_off)]
+    w_table = S_TABLE + len(x_off)
+    if direct:
+        scalars += [xor_blocks(ring_at, w_off), xor_blocks(ring_at, p_off)]
+        p_table = w_table + len(w_off)
+    else:
+        scalars += [jnp.zeros((8,), jnp.int32)]
+        p_table = w_table
+    idx = jnp.concatenate(scalars)
+
     flat_tokens = tokens.reshape(tok, width)
-    other_tokens = across(flat_tokens)
-
-    strips = width // (2 * unit)
-    bundle = jnp.concatenate(
-        [jnp.transpose(w_in, (1, 0, 2, 3)).reshape(e_loc, width, 2 * unit),
-         jnp.transpose(w_down.reshape(unit, e_loc, strips, 2 * unit), (1, 2, 0, 3)).reshape(
-             e_loc, strips * unit, 2 * unit)], axis=1)
-
-    shares = [lax.dynamic_index_in_dim(bundle, q ^ d, 0, keepdims=False) for d in range(e_loc)]
+    near_rows = lax.dynamic_index_in_dim(tokens, bit[0], 0, keepdims=False)
+    away_rows = lax.dynamic_index_in_dim(tokens, 1 - bit[0], 0, keepdims=False)
+    w_phys = jnp.transpose(w_qkv, (1, 0, 2))
+    gain_row_in = gain_attn[None, :]
+    keep_w, swap_w, give_w, early, late = call(
+        pack_kernel,
+        [sds((rows_here, part), BF), sds((rows_here, part), BF), sds((2 * rows_here, part), BF),
+         sds((rows_here, part + 128), BF), sds((rows_here, 3 * part), BF)],
+        [idx, w_phys, w_out, jnp.transpose(w_router), jnp.transpose(w_const),
+         jnp.transpose(const_vec), gain_row_in, gain_ffn[None, :]], smem=1,
+        scratch=[pltpu.VMEM((4, rows_here, part), BF)], name="pack", far_in=range(1, 8))
+
+    def spread_to(x, d):
+        return jnp.concatenate([x, hop(x, d)], axis=0)
+
+    def gathered(x):
+        return [lax.all_gather(x, blk, axis=0, tiled=True)]
+
+    p_rows = rows_here if direct else width
+    w_rows = rows_here if direct else width
+    two_blocks = jnp.concatenate([near_rows, hop(away_rows, 1)], axis=0)
+    if direct:
+        came_w = partner(give_w)
+        early = spread_to(early, 4)
+        two_blocks, came_w, early, routes, pair_order, cotangent = barrier(
+            (two_blocks, came_w, early, routes, pair_order, cotangent))
+        swapped = [hop(swap_w, 2), hop(came_w[rows_here:], 2)]
+        early = spread_to(early, 2)
+    x_parts = [lax.ppermute(two_blocks, both_axes, to_head(same)) for same in (True, False)]
 
     positions = b * slot_dev + jnp.arange(slot_dev, dtype=jnp.int32)
     own_len = lax.dynamic_slice_in_dim(lengths, h * seq_dev, seq_dev)
@@ -701,62 +808,93 @@
         flat = rows.reshape(heads * ring * capacity, rows.shape[-1])
         return lax.all_to_all(flat, ("head", "ring"), 0, 0, tiled=True)
 
+    if direct:
+        x_parts, swapped, early, send_g, ints, slot_rows, w_in, w_down = barrier(
+            (x_parts, swapped, early, send_g, ints, slot_rows, w_in, w_down))
+    for d in more:
+        x_parts = x_parts + [hop(a, d) for a in x_parts]
+    x_parts = x_parts + [hop(a, 2) for a in x_parts]
+    if direct:
+        first = jnp.concatenate([keep_w, came_w[:rows_here], *swapped], axis=0)
+        w_parts = [first, hop(first, 4)]
+        early = spread_to(early, 1)
     g_rows = to_experts(send_g)
-    g_rows, shares = barrier((g_rows, shares))
-    pieces = [hop(shares[d], d) for d in range(e_loc)]
+
+    strips = width // (2 * unit)
+    bundle = jnp.concatenate(
+        [jnp.transpose(w_in, (1, 0, 2, 3)).reshape(e_loc, width, 2 * unit),
+         jnp.transpose(w_down.reshape(unit, e_loc, strips, 2 * unit), (1, 2, 0, 3)).reshape(
+             e_loc, strips * unit, 2 * unit)], axis=1)
+    shares = [lax.dynamic_index_in_dim(bundle, q ^ d, 0, keepdims=False) for d in range(e_loc)]
 
     frequency = 10000.0 ** (-(2.0 * jnp.arange(HD // 2, dtype=F32)) / HD)
     angles = jnp.arange(n_slots, dtype=jnp.int32).astype(F32)[:, None] * frequency[None, :]
     cos_all = jnp.concatenate([jnp.cos(angles)] * 4, axis=1)
     sin_all = jnp.concatenate([jnp.sin(angles)] * 4, axis=1)
-    cos_here = lax.dynamic_slice_in_dim(cos_all, b * slot_dev, slot_dev)
-    sin_here = lax.dynamic_slice_in_dim(sin_all, b * slot_dev, slot_dev)
-    idx = jnp.stack([h, lax.dynamic_index_in_dim(lengths, b % n_seq, 0, keepdims=False), core, q])
     prev = previous_layer_logits.reshape(tok, n_all)
     prev_wide = jnp.pad(prev, ((0, 0), (0, 128 - n_all)))
     prev_logits = jnp.pad(
         jnp.dot(prev, w_residual, precision=lax.Precision.HIGHEST), ((0, 0), (0, 128 - n_all)))
-    (wpack, g_rows, pieces[:-1], prev_wide, prev_logits, cos_all, sin_all, ints, slot_rows) = barrier(
-        (wpack, g_rows, pieces[:-1], prev_wide, prev_logits, cos_all, sin_all, ints, slot_rows))
-
-    w_qkv_all = Columns(wpack, 3 * part, 0)
-    w_out_all = Columns(wpack, part, 3 * part)
-    w_small_all = Columns(wpack, 128, 4 * part)
-
-    send_qkv, xn, small = call(
-        qkv_kernel,
-        [sds((n_blk, slot_dev, 384), BF), sds((n_seq * slot_dev, width), BF), sds((24, width), F32)],
-        [idx, flat_tokens, other_tokens, w_qkv_all, w_small_all, cos_here, sin_here], smem=1,
-        scratch=[pltpu.VMEM((n_seq * slot_dev, width), BF)],
-        flops=2 * n_seq * slot_dev * width * 3 * part, name="qkv", far_in=(3, 4), far_out=(1, 2))
+    if direct:
+        x_parts, w_parts, early, shares, prev_wide, prev_logits, cos_all, sin_all = barrier(
+            (x_parts, w_parts, early, shares, prev_wide, prev_logits, cos_all, sin_all))
+        w_parts = w_parts + [hop(a, 1) for a in w_parts]
+        early_parts = [early, partner(early)]
+    else:
+        wide_w = jnp.pad(w_qkv, ((0, 0), (0, 0), (0, 512 - part))).reshape(rows_here, 3, 4, 128)
+        wide_w = jnp.transpose(wide_w, (0, 2, 1, 3)).reshape(rows_here, -1)
+        (whole_w,) = gathered(wide_w)
+        w_parts = [lax.dynamic_slice_in_dim(whole_w, (2 * bit[1] + core) * part, part, 1)]
+        early_parts = gathered(early)
+    x_parts = x_parts + [partner(a) for a in x_parts]
+    x_parts, w_parts, early_parts, g_rows, shares, late = barrier(
+        (x_parts, w_parts, early_parts, g_rows, shares, late))
+    pieces = [hop(shares[d], d) for d in range(e_loc)]
+    if direct:
+        late = spread_to(late, 4)
+
+    attn_unit, lse, xn, qkv, early_all = call(
+        functools.partial(
+            attend_kernel, len(x_parts), len(w_parts), len(early_parts), w_rows, p_rows),
+        [sds((n_slots, 128), BF), sds((8, n_slots), F32), sds((n_slots, width), BF),
+         sds((n_slots, 384), BF), sds((width, part + 128), BF)],
+        [idx, *x_parts, *w_parts, *early_parts, cos_all, sin_all], smem=1,
+        scratch=[pltpu.VMEM((128, n_slots), BF), pltpu.VMEM((width, 384), BF)],
+        flops=2 * n_slots * n_slots * 512 + 2 * n_slots * width * 384, name="attend",
+        far_in=range(1, 3 + len(x_parts) + len(w_parts) + len(early_parts)),
+        far_out=(0, 1, 2, 3, 4))
+    attn_unit, late = barrier((attn_unit, late))
 
     def exchange(x):
-        flat = x.reshape(n_blk * slot_dev, x.shape[-1])
+        flat = x.reshape(n_blk * (x.size // x.shape[-1] // n_blk), x.shape[-1])
         return lax.all_to_all(flat, blk, 0, 0, tiled=True)
 
-    qkv = exchange(send_qkv)
-    qkv, pieces[-1] = barrier((qkv, pieces[-1]))
-    attn_unit, lse = call(
-        attend_kernel, [sds((n_slots, 128), BF), sds((8, n_slots), F32)], [idx, qkv], smem=1,
-        scratch=[pltpu.VMEM((128, n_slots), BF)], flops=2 * n_slots * n_slots * 512, name="attend", far_in=(1,), far_out=(0, 1))
     attn_recv = exchange(attn_unit).reshape(n_blk, slot_dev, 128)
+    attn_recv, pieces = barrier((attn_recv, pieces))
     pieces = pieces + [partner(p) for p in pieces]
+    w_out_all = Columns(early_all, part, 0)
     mine, other, attn_low = call(
         out_kernel,
         [sds((tok, width), F32), sds((tok, width), BF), sds((n_seq * slot_dev, part), BF)],
-        [idx, attn_recv, w_out_all], smem=1, scratch=[pltpu.VMEM((n_seq * slot_dev, width), F32)],
+        [idx, attn_recv, w_out_all], smem=1,
+        scratch=[pltpu.VMEM((n_seq * slot_dev, width), F32)],
         flops=2 * n_seq * slot_dev * width * part, name="out", far_in=(2,), far_out=(2,))
-    send_x, residual, aux = call(
+    w_small_all = Columns(early_all, 128, part)
+    send_x, residual, aux, small = call(
         route_kernel,
-        [sds((heads * n_share, per_send, width + 128), BF), sds((tok, width), F32), sds((tok, 128), F32)],
-        [flat_tokens, mine, across(other), w_small_all, small, prev_logits, ints, slot_rows],
-        flops=tok * width * 1000, name="route", far_in=(3, 4, 5), far_out=(1, 2))
+        [sds((heads * n_share, per_send, width + 128), BF), sds((tok, width), F32),
+         sds((tok, 128), F32), sds((24, width), F32)],
+        [flat_tokens, mine, across(other), w_small_all, prev_logits, ints, slot_rows],
+        flops=tok * width * 1000, name="route", far_in=(3, 4, 5), far_out=(1, 2, 3))
     x_rows = to_experts(send_x)
-    x_rows, pieces = barrier((x_rows, pieces))
+    x_rows, pieces, late = barrier((x_rows, pieces, late))
+    if direct:
+        late = spread_to(late, 2)
     group = max(1, 128 // unit)
     if group > 1:
         pieces = [join(pieces[i : i + group]) for i in range(0, len(pieces), group)]
     back_rows, *grad_pieces = experts(x_rows, g_rows, pieces)
+    back_rows, late = barrier((back_rows, late))
     back_recv = to_experts(back_rows)
 
     if group > 1:
@@ -777,20 +915,43 @@
         name="combine", far_in=(1, 2, 3, 4, 5, 6, 7), far_out=(0, 1, 3, 4))
 
     came = [hop(added[d], d) for d in range(e_loc)]
-    send_gv, dw_out = call(
-        grad_vec_kernel, [sds((n_blk, slot_dev, 128), BF), sds((width, part), F32)],
-        [idx, grad_low, across(grad_low), attn_low, w_out_all], smem=1,
-        scratch=[pltpu.VMEM((n_seq * slot_dev, width), BF)],
-        flops=4 * n_seq * slot_dev * width * part, name="grad_vec", far_in=(3, 4), far_out=(1,))
+    pay = (n_blk // 2, rows_here, part + 128)
+    send_gv, keep, give = call(
+        grad_vec_kernel,
+        [sds((n_blk, slot_dev, 128), BF), sds(pay, F32), sds(pay, BF)],
+        [idx, grad_low, across(grad_low), attn_low, w_out_all, sums, resid], smem=1,
+        scratch=[pltpu.VMEM((n_seq * slot_dev, width), BF),
+                 pltpu.VMEM((n_blk, rows_here, part + 128), F32)],
+        flops=4 * n_seq * slot_dev * width * part, name="grad_vec", far_in=(3, 4), far_out=(1, 2))
     dout = exchange(send_gv)
-    dout, came = barrier((dout, came))
+    came_sum = partner(give)
+    dout, came, came_sum, late = barrier((dout, came, came_sum, late))
+    if direct:
+        late = spread_to(late, 1)
+
+    def halve(keep, came_sum, d):
+        half = (keep.shape[0] // 2,) + keep.shape[1:]
+        keep, give = call(
+            halve_kernel, [sds(half, F32), sds(half, BF)], [keep, came_sum], name="halve")
+        return keep, hop(give, d)
+
+    steps = [1 << i for i in range(ring.bit_length() - 1)]
+    keep, came_sum = halve(keep, came_sum, steps[0])
     (grad_unit,) = call(
         attend_back_kernel, [sds((n_slots, 384), BF)],
         [idx, qkv, dout, attn_unit, lse, cos_all, sin_all], smem=1,
         scratch=[pltpu.VMEM((128, n_slots), BF), pltpu.VMEM((n_slots, 128), F32),
                  pltpu.VMEM((n_slots, 128), F32)],
         flops=5 * n_slots * n_slots * 256, name="attend_back", far_in=(1, 3, 4, 5, 6), far_out=())
+    grad_unit, came_sum = barrier((grad_unit, came_sum))
     grad_recv = exchange(grad_unit).reshape(n_blk, slot_dev, 384)
+    late_parts = [late, partner(late)] if direct else gathered(late)
+    (unit_dw,) = call(
+        unit_dw_kernel, [sds((width, 384), BF)], [xn, grad_unit],
+        flops=2 * n_slots * width * 384, name="unit_dw", far_in=(0,), room=20)
+
+    for d in steps[1:]:
+        keep, came_sum = halve(keep, came_sum, d)
     def by_source(parts):
         chosen = []
         for e in range(e_loc):
@@ -813,38 +974,38 @@
         down_sum = by_source([p[width:].reshape(strips, unit, 2 * unit) for p in came])
         down_sum = jnp.transpose(jnp.stack(down_sum, axis=0), (2, 0, 1, 3))
         down_sum = down_sum.reshape(unit, e_loc, width)
-    grad_recv, in_sum, down_sum = barrier((grad_recv, in_sum, down_sum))
-    pay = (ring, rows_here, 4 * part + 128)
-    gn_mine, gn_other, keep, give = call(
-        grad_qkv_kernel,
-        [sds((tok, width), F32), sds((tok, width), BF), sds(pay, F32), sds(pay, BF)],
-        [idx, grad_recv, xn, flat_tokens, other_tokens, w_qkv_all, sums, resid, dw_out], smem=1,
+    grad_recv, unit_dw, in_sum, down_sum, came_sum = barrier(
+        (grad_recv, unit_dw, in_sum, down_sum, came_sum))
+    dw_recv = exchange(unit_dw).reshape(n_blk, rows_here, 384)
+    out_sum, table = call(
+        last_add_kernel, [sds((rows_here, part), F32), sds((rows_here, 128), F32)],
+        [keep, came_sum], name="last_add")
+    gain2_sum, router_sum, const_sum, vec_sum, resid_sum = call(
+        functools.partial(small_kernel, n_all),
+        [sds((1, rows_here), F32), sds((n_all, rows_here), F32), sds((4, rows_here), F32),
+         sds((2, rows_here), F32), sds((n_all, n_all), F32)],
+        [table, across(table)], name="small")
+
+    gn_mine, gn_other = call(
+        functools.partial(grad_qkv_kernel, len(late_parts), p_rows, p_table),
+        [sds((tok, width), F32), sds((tok, width), BF)], [idx, grad_recv, *late_parts], smem=1,
         scratch=[pltpu.VMEM((n_seq * slot_dev, 3 * part), BF),
-                 pltpu.VMEM((n_seq * slot_dev, width), F32),
-                 pltpu.VMEM((ring, 2, rows_here, 4 * part + 128), F32),
-                 pltpu.VMEM((n_seq * slot_dev, width), BF)],
-        flops=4 * n_seq * slot_dev * width * 3 * part, name="grad_qkv", far_in=(2, 3, 4, 5, 6, 7, 8), far_out=(0,))
-    gn_came = across(gn_other)
-    (pair_sum,) = call(add_kernel, [sds(pay, BF)], [keep, partner(give)], name="add")
-    ring_recv = lax.all_to_all(pair_sum, "ring", 0, 0, tiled=True)
+                 pltpu.VMEM((n_seq * slot_dev, width), F32), pltpu.VMEM((width, 3 * part), BF)],
+        flops=2 * n_seq * slot_dev * width * 3 * part, name="grad_qkv", far_in=(2, 3), far_out=(0,))
     (grad_tokens,) = call(
         final_kernel, [sds((tok, width), F32)],
-        [flat_tokens, gn_mine, gn_came, grad_res, small], name="final", far_in=(0, 1, 3, 4), far_out=(0,))
-    ring_recv, grad_tokens = barrier((ring_recv, grad_tokens))
-    qkv_sum, out_sum, small_sum = call(
-        total_kernel,
-        [sds((3, rows_here, part), F32), sds((rows_here, part), F32), sds((rows_here, 128), F32)],
-        [ring_recv], name="total")
-    gain1_sum, gain2_sum, router_sum, const_sum, vec_sum, resid_sum = call(
-        functools.partial(small_kernel, n_all),
-        [sds((1, rows_here), F32), sds((1, rows_here), F32), sds((n_all, rows_here), F32),
-         sds((4, rows_here), F32), sds((2, rows_here), F32), sds((n_all, n_all), F32)],
-        [small_sum, across(small_sum)], name="small")
+        [flat_tokens, gn_mine, across(gn_other), grad_res, small], name="final",
+        far_in=(0, 1, 3, 4), far_out=(0,))
+    dw_recv, grad_tokens, gain2_sum = barrier((dw_recv, grad_tokens, gain2_sum))
+    qkv_sum, gain1_part = call(
+        total_kernel, [sds((3, rows_here, part), F32), sds((8, rows_here), F32)],
+        [dw_recv, w_phys, gain_row_in], name="total", far_in=(1, 2))
+    gain1_sum = gain1_part[0] + across(gain1_part)[0]
 
     return (
         output.reshape(tokens.shape),
         grad_tokens.reshape(tokens.shape),
-        gain1_sum.reshape(rows_here),
+        gain1_sum,
         jnp.transpose(qkv_sum, (1, 0, 2)),
         out_sum,
         gain2_sum.reshape(rows_here),

time: 332 us -> 301 us (0.907); the launches traced: 331 us -> 296 us
  waiting for transfers between devices: 159 us -> 122 us
  starting transfers between devices: 53.3 us -> 80.7 us
  blocking collectives: 15 us -> 0 us
  between operations: 14.5 us -> 1.73 us
  Pallas kernels: 58.7 us -> 62.1 us
    ppermute x6 -> x23, starting transfers between devices: 8.01 us -> 36.2 us  [hop(): lax.ppermute(x, 'ring', [(i, i ^ d) for i in range(ring)])]
    all_to_all x1 -> x0, waiting for transfers between devices: 22.1 us -> none  [per_device(): ring_recv = lax.all_to_all(pair_sum, 'ring', 0, 0, tiled=True)]
    all_to_all x1 -> x0, blocking collectives: 15 us -> none  [exchange(): return lax.all_to_all(flat, blk, 0, 0, tiled=True)]
    all_to_all x3 -> x4, waiting for transfers between devices: 14.2 us -> 5.17 us  [exchange(): return lax.all_to_all(flat, blk, 0, 0, tiled=True)]
    ppermute x0 -> x2, waiting for transfers between devices: none -> 7.85 us  [per_device(): lax.ppermute(two_blocks, both_axes, to_head(same))]
    all_to_all x3, waiting for transfers between devices: 39.7 us -> 32.2 us  [to_experts(): return lax.all_to_all(flat, ('head', 'ring'), 0, 0, tiled=True)]
    ppermute x6 -> x23, waiting for transfers between devices: 61.5 us -> 55.1 us  [hop(): lax.ppermute(x, 'ring', [(i, i ^ d) for i in range(ring)])]
    unnamed x90 -> x76, local copies, waits for them, and re-layouts: 13.8 us -> 7.43 us
  transfers between devices with their start and end apart: 28 -> 53, of which waited for: 24 -> 31; matrix products, arithmetic and copies ran while one was open for 6% -> 8% of each run, Pallas kernels for 5% -> 18%
where the time goes in v3:
time: 301 us; the launch traced here: 296 us
  waiting for transfers between devices  122 us (41%)
  starting transfers between devices  80.7 us (27%)
  Pallas kernels  62.1 us (21%)
  local copies, waits for them, and re-layouts  22.2 us (7%)
  other arithmetic  6.77 us (2%)
    ppermute x23, waiting for transfers between devices, hop(): lax.ppermute(x, 'ring', [(i, i ^ d) for i in range(ring)])  55.1 us
    pallas_call x19, Pallas kernels, call(): pl.pallas_call(kernel, grid=(1,), out_shape=shapes, in_specs=[sm] * smem...  50.5 us
    ppermute x23, starting transfers between devices, hop(): lax.ppermute(x, 'ring', [(i, i ^ d) for i in range(ring)])  36.2 us
    all_to_all x3, waiting for transfers between devices, to_experts(): return lax.all_to_all(flat, ('head', 'ring'), 0, 0, tiled=True)  32.2 us
    all_to_all x3, starting transfers between devices, to_experts(): return lax.all_to_all(flat, ('head', 'ring'), 0, 0, tiled=True)  16.3 us
    all_to_all x4, starting transfers between devices, exchange(): return lax.all_to_all(flat, blk, 0, 0, tiled=True)  16.1 us
    pallas_call x1, Pallas kernels, experts(): pl.pallas_call(functools.partial(expert_kernel, n, steps), grid=(steps,),...  11.6 us
    ppermute x5, waiting for transfers between devices, across(): return lax.ppermute(x, 'head', swap)  11.5 us
  transfers between devices with their start and end apart: 53, of which 31 were waited for; matrix products, arithmetic and copies ran while one was open for 8% of the time, Pallas kernels for 18%

profile of v3, /device:TPU:0, one launch (start us, length us, event | category | flops | bytes accessed | tf_op | source)
XLA Modules:
  0.0 295.7 jit_solution(10609989410105886392)
XLA Ops:
  25.5 7.8 %collective-permute-done.4.refs_1_ = bf16[128,768]{1,0:T(8,128)(2,1)S(1)} collective-permute-done((bf16[128,768]{1,0:T(8,128)(2,1)S(1)}, bf16[128,768]{1,0:T(8,128)(2,1)S(1)}, u32[]{:S(2)}, u32[]{:S(2)}) %collective-permute-start.4) | collective-permute-done | bytes 196640 | tf_op jit(solution)/shard_map/ppermute | solution.py:781
  33.3 7.3 %all-to-all-start = ((bf16[16,24,768]{2,1,0:T(8,128)(2,1)}), bf16[16,24,768]{2,1,0:T(8,128)(2,1)S(1)}, u32[]{:S(2)}, u32[]{:S(2)}) async-start(bf16[16,24,768]{2,1,0:T(8,128)(2,1)} %bitcast.33), calls=%async_computation | async-start | bytes 1179648 | tf_op jit(solution)/shard_map/all_to_all | solution.py:809
  57.6 5.6 %collective-permute-done.10.refs_9_ = bf16[192,384]{1,0:T(8,128)(2,1)} collective-permute-done((bf16[192,384]{1,0:T(8,128)(2,1)S(1)}, bf16[192,384]{1,0:T(8,128)(2,1)}, u32[]{:S(2)}, u32[]{:S(2)}) %collective-permute-start.10) | collective-permute-done | bytes 147488 | tf_op jit(solution)/shard_map/ppermute | solution.py:706
  67.2 4.1 %collective-permute-done.16.refs_10_ = bf16[192,384]{1,0:T(8,128)(2,1)S(1)} collective-permute-done((bf16[192,384]{1,0:T(8,128)(2,1)S(1)}, bf16[192,384]{1,0:T(8,128)(2,1)S(1)}, u32[]{:S(2)}, u32[]{:S(2)}) %collective-permute-start.16) | collective-permute-done | bytes 147488 | tf_op jit(solution)/shard_map/ppermute | solution.py:706
  81.5 9.6 %attend.1 = (bf16[1024,128]{1,0:T(8,128)(2,1)}, f32[8,1024]{1,0:T(8,128)}, bf16[1024,768]{1,0:T(8,128)(2,1)}, bf16[1024,384]{1,0:T(8,128)(2,1)}, bf16[768,512]{1,0:T(8,128)(2,1)}) custom-call(s32[56]{0:T(128)S(1)} %concatenate.51.idx, bf16[128,768]{1,0:T(8,128)(2,1)} %collective-permute-done.3.refs_0_, bf16[128,768]{1,0:T(8,128)(2,1)} %copy-done.29, ...), custom_call_target="tpu_custom_call" | custom-call | flops 1677721600 | bytes 7438560 | tf_op jit(solution)/shard_map/attend/pallas_call | solution.py:56
  91.2 3.7 %all-to-all-start.1 = ((bf16[16,64,128]{2,1,0:T(8,128)(2,1)}), bf16[16,64,128]{2,1,0:T(8,128)(2,1)S(1)}, u32[]{:S(2)}, u32[]{:S(2)}) async-start(bf16[16,64,128]{2,1,0:T(8,128)(2,1)} %bitcast.111), calls=%async_computation.1 | async-start | bytes 524288 | tf_op jit(solution)/shard_map/all_to_all | solution.py:870
  96.5 16.5 %collective-permute-done.22.refs_3_ = bf16[1152,256]{1,0:T(8,128)(2,1)} collective-permute-done((bf16[1152,256]{1,0:T(8,128)(2,1)}, bf16[1152,256]{1,0:T(8,128)(2,1)}, u32[]{:S(2)}, u32[]{:S(2)}) %collective-permute-start.22) | collective-permute-done | bytes 589856 | tf_op jit(solution)/shard_map/ppermute | solution.py:706
  117.1 4.8 %collective-permute-done.23.other = bf16[128,768]{1,0:T(8,128)(2,1)S(1)} collective-permute-done((bf16[128,768]{1,0:T(8,128)(2,1)S(1)}, bf16[128,768]{1,0:T(8,128)(2,1)S(1)}, u32[]{:S(2)}, u32[]{:S(2)}) %collective-permute-start.23) | collective-permute-done | bytes 196640 | tf_op jit(solution)/shard_map/ppermute | solution.py:680
  124.5 5.1 %all-to-all-start.2 = ((bf16[16,24,896]{2,1,0:T(8,128)(2,1)}), bf16[16,24,896]{2,1,0:T(8,128)(2,1)S(1)}, u32[]{:S(2)}, u32[]{:S(2)}) async-start(bf16[16,24,896]{2,1,0:T(8,128)(2,1)} %bitcast.36), calls=%async_computation.2 | async-start | bytes 1376256 | tf_op jit(solution)/shard_map/all_to_all | solution.py:809
  134.4 13.4 %all-to-all-done.2 = bf16[16,24,896]{2,1,0:T(8,128)(2,1)S(1)} async-done(((bf16[16,24,896]{2,1,0:T(8,128)(2,1)}), bf16[16,24,896]{2,1,0:T(8,128)(2,1)S(1)}, u32[]{:S(2)}, u32[]{:S(2)}) %all-to-all-start.2) | async-done | bytes 688160 | tf_op jit(solution)/shard_map/all_to_all | solution.py:809
  148.9 11.6 %experts.1 = (bf16[384,1536]{1,0:T(8,128)(2,1)}, bf16[1152,256]{1,0:T(8,128)(2,1)}, bf16[1152,256]{1,0:T(8,128)(2,1)}, bf16[1152,256]{1,0:T(8,128)(2,1)}, bf16[1...) custom-call(bf16[384,896]{1,0:T(8,128)(2,1)S(1)} %bitcast.98, ...), custom_call_target="tpu_custom_call" | custom-call | flops 5435817984 | bytes 11796480 | tf_op jit(solution)/shard_map/experts/pallas_call | solution.py:388
  160.5 3.9 %all-to-all-start.3 = ((bf16[16,24,1536]{2,1,0:T(8,128)(2,1)}), bf16[16,24,1536]{2,1,0:T(8,128)(2,1)S(1)}, u32[]{:S(2)}, u32[]{:S(2)}) async-start(bf16[16,24,1536]{2,1,0:T(8,128)(2,1)} %bitcast.38), calls=%async_computation.3 | async-start | bytes 2359296 | tf_op jit(solution)/shard_map/all_to_all | solution.py:809
  169.9 3.9 %pair_add.1 = (bf16[1152,256]{1,0:T(8,128)(2,1)}, bf16[1152,256]{1,0:T(8,128)(2,1)}, bf16[1152,256]{1,0:T(8,128)(2,1)}, bf16[1152,256]{1,0:T(8,128)(2,1)}) custom-call(bf16[1152,256]{1,0:T(8,128)(2,1)} %get-tuple-element.240.refs_0_, bf16[1152,256]{1,0:T(8,128)(2,1)} %get-tuple-element.241.refs_1_, bf16[1152,256]{1,0:T(8,128)(2,1)} %get-tuple-element.242.refs_2_, ...), custom_call_target="tpu_custom_call" | custom-call | bytes 7077888 | tf_op jit(solution)/shard_map/pair_add/pallas_call | solution.py:56
  173.8 18.7 %all-to-all-done.3 = bf16[16,24,1536]{2,1,0:T(8,128)(2,1)S(1)} async-done(((bf16[16,24,1536]{2,1,0:T(8,128)(2,1)}), bf16[16,24,1536]{2,1,0:T(8,128)(2,1)S(1)}, u32[]{:S(2)}, u32[]{:S(2)}) %all-to-all-start.3) | async-done | bytes 1179680 | tf_op jit(solution)/shard_map/all_to_all | solution.py:809
  192.5 3.7 %combine.1 = (f32[128,768]{1,0:T(8,128)}, f32[128,768]{1,0:T(8,128)}, bf16[128,768]{1,0:T(8,128)(2,1)S(1)}, f32[24,768]{1,0:T(8,128)}, f32[128,128]{1,0:T(8,128)}) custom-call(bf16[4,96,1536]{2,1,0:T(8,128)(2,1)S(1)} %bitcast.93, f32[128,768]{1,0:T(8,128)} %get-tuple-element.253.residual, f32[128,768]{1,0:T(8,128)} %bitcast.96, ...), custom_call_target="tpu_custom_call" | custom-call | flops 196608000 | bytes 3493888 | tf_op jit(solution)/shard_map/combine/pallas_call | solution.py:56
  206.4 3.8 %all-to-all-start.4 = ((bf16[16,64,128]{2,1,0:T(8,128)(2,1)}), bf16[16,64,128]{2,1,0:T(8,128)(2,1)S(1)}, u32[]{:S(2)}, u32[]{:S(2)}) async-start(bf16[16,64,128]{2,1,0:T(8,128)(2,1)} %get-tuple-element.263), calls=%async_computation.4 | async-start | bytes 524288 | tf_op jit(solution)/shard_map/all_to_all | solution.py:870
  215.6 11.7 %collective-permute-done.36.refs_3_ = bf16[1152,256]{1,0:T(8,128)(2,1)S(1)} collective-permute-done((bf16[1152,256]{1,0:T(8,128)(2,1)}, bf16[1152,256]{1,0:T(8,128)(2,1)S(1)}, u32[]{:S(2)}, u32[]{:S(2)}) %collective-permute-start.36) | collective-permute-done | bytes 589856 | tf_op jit(solution)/shard_map/ppermute | solution.py:706
  232.0 6.9 %attend_back.1.grad = bf16[1024,384]{1,0:T(8,128)(2,1)} custom-call(s32[56]{0:T(128)S(1)} %concatenate.51.idx, bf16[1024,384]{1,0:T(8,128)(2,1)} %get-tuple-element.258.qkv, bf16[1024,128]{1,0:T(8,128)(2,1)S(1)} %bitcast.99, bf16[1024,128]{1,0:T(8,128)(2,1)} %get-tuple-element.209.out, f32[8,1024]{1,0:T(8,128)} %get-tuple-element.271.lse, ...), custom_call_target="tpu_custom_call" | custom-call | flops 1342177280 | bytes 3178720 | tf_op jit(solution)/shard_map/attend_back/pallas_call | solution.py:56
  238.9 3.9 %all-to-all-start.5 = ((bf16[16,64,384]{2,1,0:T(8,128)(2,1)}), bf16[16,64,384]{2,1,0:T(8,128)(2,1)S(1)}, u32[]{:S(2)}, u32[]{:S(2)}) async-start(bf16[16,64,384]{2,1,0:T(8,128)(2,1)} %bitcast.42), calls=%async_computation.5 | async-start | bytes 1572864 | tf_op jit(solution)/shard_map/all_to_all | solution.py:870
  247.1 5.0 %place.1 = (f32[6144,128]{1,0:T(8,128)}, f32[3072,128]{1,0:T(8,128)}) custom-call(s32[56]{0:T(128)S(1)} %concatenate.51.idx, bf16[1152,256]{1,0:T(8,128)(2,1)} %get-tuple-element.277.refs_0_, bf16[1152,256]{1,0:T(8,128)(2,1)} %copy-done.12, bf16[1152,256]{1,0:T(8,128)(2,1)} %copy-done.13, bf16[1152,256]{1,0:T(8,128)(2,1)} %copy-done.14), custom_call_target="tpu_custom_call" | custom-call | bytes 7078112 | tf_op jit(solution)/shard_map/place/pallas_call | solution.py:56
  253.9 4.8 %collective-permute-done.39.came = bf16[2,48,512]{2,1,0:T(8,128)(2,1)S(1)} collective-permute-done((bf16[2,48,512]{2,1,0:T(8,128)(2,1)S(1)}, bf16[2,48,512]{2,1,0:T(8,128)(2,1)S(1)}, u32[]{:S(2)}, u32[]{:S(2)}) %collective-permute-start.39) | collective-permute-done | bytes 98336 | tf_op jit(solution)/shard_map/ppermute | solution.py:706
  258.7 4.6 %collective-permute-start.40 = (bf16[1,48,512]{2,1,0:T(8,128)(2,1)S(1)}, bf16[1,48,512]{2,1,0:T(8,128)(2,1)S(1)}, u32[]{:S(2)}, u32[]{:S(2)}) collective-permute-start(bf16[1,48,512]{2,1,0:T(8,128)(2,1)S(1)} %get-tuple-element.287), channel_id=1, source_target_pairs={{0,8},{2,10},{4,12},{6,14},{8,0},{10,2},{12,4},{14,6},{1,9},{3,11}... | collective-permute-start | bytes 147464 | tf_op jit(solution)/shard_map/ppermute | solution.py:706
  269.2 4.8 %all-to-all-start.6 = ((bf16[16,48,384]{2,1,0:T(8,128)(2,1)}), bf16[16,48,384]{2,1,0:T(8,128)(2,1)S(1)}, u32[]{:S(2)}, u32[]{:S(2)}) async-start(bf16[16,48,384]{2,1,0:T(8,128)(2,1)} %bitcast.47), calls=%async_computation.6 | async-start | bytes 1179648 | tf_op jit(solution)/shard_map/all_to_all | solution.py:870
  279.7 5.1 %collective-permute-done.44.other = f32[48,128]{1,0:T(8,128)S(1)} collective-permute-done((f32[48,128]{1,0:T(8,128)S(1)}, f32[48,128]{1,0:T(8,128)S(1)}, u32[]{:S(2)}, u32[]{:S(2)}) %collective-permute-start.44) | collective-permute-done | bytes 24608 | tf_op jit(solution)/shard_map/ppermute | solution.py:680
  (227 shorter events, 123.7 us)
Async XLA Ops:
  1.7 14.5 %collective-permute-start = (bf16[64,768]{1,0:T(8,128)(2,1)S(1)}, bf16[64,768]{1,0:T(8,128)(2,1)S(1)}, u32[]{:S(2)}, u32[]{:S(2)}) collective-permute-start(bf16[64,768]{1,0:T(8,128)(2,1)S(1)} %get-tuple-element.365), channel_id=1, source_target_pairs={{0,2},{2,0},{4,6},{6,4},{8,10},{10,8},{12,14},{14,12},{1,3},{3,1},... | collective-permute-start | bytes 294920 | tf_op jit(solution)/shard_map/ppermute | solution.py:706
  8.5 17.0 %collective-permute-start.5 = (bf16[48,384]{1,0:T(8,128)(2,1)S(1)}, bf16[48,384]{1,0:T(8,128)(2,1)S(1)}, u32[]{:S(2)}, u32[]{:S(2)}) collective-permute-start(bf16[48,384]{1,0:T(8,128)(2,1)S(1)} %get-tuple-element.164), channel_id=1, source_target_pairs={{0,4},{2,6},{4,0},{6,2},{8,12},{10,14},{12,8},{14,10},{1,5},{3,7},... | collective-permute-start | bytes 110600 | tf_op jit(solution)/shard_map/ppermute | solution.py:706
  16.7 16.6 %collective-permute-start.4 = (bf16[128,768]{1,0:T(8,128)(2,1)S(1)}, bf16[128,768]{1,0:T(8,128)(2,1)S(1)}, u32[]{:S(2)}, u32[]{:S(2)}) collective-permute-start(bf16[128,768]{1,0:T(8,128)(2,1)S(1)} %pad_maximum_fusion.5), channel_id=1, source_target_pairs={{0,16},{2,18},{4,20},{6,22},{8,0},{10,2},{12,4},{14,6},{16,24},{18... | collective-permute-start | bytes 589832 | tf_op jit(solution)/shard_map/ppermute | solution.py:781
  18.3 15.0 %collective-permute-start.3 = (bf16[128,768]{1,0:T(8,128)(2,1)S(1)}, bf16[128,768]{1,0:T(8,128)(2,1)}, u32[]{:S(2)}, u32[]{:S(2)}) collective-permute-start(bf16[128,768]{1,0:T(8,128)(2,1)S(1)} %pad_maximum_fusion.5), channel_id=1, source_target_pairs={{0,0},{2,2},{4,4},{6,6},{8,16},{10,18},{12,20},{14,22},{16,8},{18,... | collective-permute-start | bytes 589832 | tf_op jit(solution)/shard_map/ppermute | solution.py:781
  33.3 42.4 %all-to-all-start = ((bf16[16,24,768]{2,1,0:T(8,128)(2,1)}), bf16[16,24,768]{2,1,0:T(8,128)(2,1)S(1)}, u32[]{:S(2)}, u32[]{:S(2)}) async-start(bf16[16,24,768]{2,1,0:T(8,128)(2,1)} %bitcast.33), calls=%async_computation | async-start | bytes 1179648 | tf_op jit(solution)/shard_map/all_to_all | solution.py:809
  44.0 19.1 %collective-permute-start.10 = (bf16[192,384]{1,0:T(8,128)(2,1)S(1)}, bf16[192,384]{1,0:T(8,128)(2,1)}, u32[]{:S(2)}, u32[]{:S(2)}) collective-permute-start(bf16[192,384]{1,0:T(8,128)(2,1)S(1)} %pad_maximum_fusion.7.refs_8_), channel_id=1, source_target_pairs={{0,8},{2,10},{4,12},{6,14},{8,0},{10,2},{12,4},{14,6},{1,9},{3,11}... | collective-permute-start | bytes 442376 | tf_op jit(solution)/shard_map/ppermute | solution.py:706
  47.0 16.1 %collective-permute-start.8 = (bf16[128,768]{1,0:T(8,128)(2,1)}, bf16[128,768]{1,0:T(8,128)(2,1)}, u32[]{:S(2)}, u32[]{:S(2)}) collective-permute-start(bf16[128,768]{1,0:T(8,128)(2,1)} %collective-permute-done.3.refs_0_), channel_id=1, source_target_pairs={{0,4},{2,6},{4,0},{6,2},{8,12},{10,14},{12,8},{14,10},{1,5},{3,7},... | collective-permute-start | bytes 589832 | tf_op jit(solution)/shard_map/ppermute | solution.py:706
  48.5 16.2 %collective-permute-start.9 = (bf16[128,768]{1,0:T(8,128)(2,1)S(1)}, bf16[128,768]{1,0:T(8,128)(2,1)}, u32[]{:S(2)}, u32[]{:S(2)}) collective-permute-start(bf16[128,768]{1,0:T(8,128)(2,1)S(1)} %collective-permute-done.4.refs_1_), channel_id=1, source_target_pairs={{0,4},{2,6},{4,0},{6,2},{8,12},{10,14},{12,8},{14,10},{1,5},{3,7},... | collective-permute-start | bytes 589832 | tf_op jit(solution)/shard_map/ppermute | solution.py:706
  75.8 15.4 %collective-permute-start.19 = (bf16[48,1152]{1,0:T(8,128)(2,1)S(1)}, bf16[48,1152]{1,0:T(8,128)(2,1)S(1)}, u32[]{:S(2)}, u32[]{:S(2)}) collective-permute-start(bf16[48,1152]{1,0:T(8,128)(2,1)S(1)} %get-tuple-element.208), channel_id=1, source_target_pairs={{0,8},{2,10},{4,12},{6,14},{8,0},{10,2},{12,4},{14,6},{1,9},{3,11}... | collective-permute-start | bytes 331784 | tf_op jit(solution)/shard_map/ppermute | solution.py:706
  78.0 16.9 %collective-permute-start.20 = (bf16[1152,256]{1,0:T(8,128)(2,1)}, bf16[1152,256]{1,0:T(8,128)(2,1)}, u32[]{:S(2)}, u32[]{:S(2)}) collective-permute-start(bf16[1152,256]{1,0:T(8,128)(2,1)} %get-tuple-element.211), channel_id=1, source_target_pairs={{0,2},{2,0},{4,6},{6,4},{8,10},{10,8},{12,14},{14,12},{1,3},{3,1},... | collective-permute-start | bytes 1769480 | tf_op jit(solution)/shard_map/ppermute | solution.py:706
  79.4 17.1 %collective-permute-start.21 = (bf16[1152,256]{1,0:T(8,128)(2,1)}, bf16[1152,256]{1,0:T(8,128)(2,1)}, u32[]{:S(2)}, u32[]{:S(2)}) collective-permute-start(bf16[1152,256]{1,0:T(8,128)(2,1)} %get-tuple-element.212), channel_id=1, source_target_pairs={{0,4},{2,6},{4,0},{6,2},{8,12},{10,14},{12,8},{14,10},{1,5},{3,7},... | collective-permute-start | bytes 1769480 | tf_op jit(solution)/shard_map/ppermute | solution.py:706
  79.9 33.1 %collective-permute-start.22 = (bf16[1152,256]{1,0:T(8,128)(2,1)}, bf16[1152,256]{1,0:T(8,128)(2,1)}, u32[]{:S(2)}, u32[]{:S(2)}) collective-permute-start(bf16[1152,256]{1,0:T(8,128)(2,1)} %get-tuple-element.213), channel_id=1, source_target_pairs={{0,6},{2,4},{4,2},{6,0},{8,14},{10,12},{12,10},{14,8},{1,7},{3,5},... | collective-permute-start | bytes 1769480 | tf_op jit(solution)/shard_map/ppermute | solution.py:706
  91.2 21.9 %all-to-all-start.1 = ((bf16[16,64,128]{2,1,0:T(8,128)(2,1)}), bf16[16,64,128]{2,1,0:T(8,128)(2,1)S(1)}, u32[]{:S(2)}, u32[]{:S(2)}) async-start(bf16[16,64,128]{2,1,0:T(8,128)(2,1)} %bitcast.111), calls=%async_computation.1 | async-start | bytes 524288 | tf_op jit(solution)/shard_map/all_to_all | solution.py:870
  124.5 23.4 %all-to-all-start.2 = ((bf16[16,24,896]{2,1,0:T(8,128)(2,1)}), bf16[16,24,896]{2,1,0:T(8,128)(2,1)S(1)}, u32[]{:S(2)}, u32[]{:S(2)}) async-start(bf16[16,24,896]{2,1,0:T(8,128)(2,1)} %bitcast.36), calls=%async_computation.2 | async-start | bytes 1376256 | tf_op jit(solution)/shard_map/all_to_all | solution.py:809
  147.8 12.7 %collective-permute-start.28 = (bf16[96,1152]{1,0:T(8,128)(2,1)S(1)}, bf16[96,1152]{1,0:T(8,128)(2,1)S(1)}, u32[]{:S(2)}, u32[]{:S(2)}) collective-permute-start(bf16[96,1152]{1,0:T(8,128)(2,1)S(1)} %pad_maximum_fusion.4), channel_id=1, source_target_pairs={{0,4},{2,6},{4,0},{6,2},{8,12},{10,14},{12,8},{14,10},{1,5},{3,7},... | collective-permute-start | bytes 663560 | tf_op jit(solution)/shard_map/ppermute | solution.py:706
  160.5 31.9 %all-to-all-start.3 = ((bf16[16,24,1536]{2,1,0:T(8,128)(2,1)}), bf16[16,24,1536]{2,1,0:T(8,128)(2,1)S(1)}, u32[]{:S(2)}, u32[]{:S(2)}) async-start(bf16[16,24,1536]{2,1,0:T(8,128)(2,1)} %bitcast.38), calls=%async_computation.3 | async-start | bytes 2359296 | tf_op jit(solution)/shard_map/all_to_all | solution.py:809
  197.7 14.8 %collective-permute-start.34 = (bf16[1152,256]{1,0:T(8,128)(2,1)}, bf16[1152,256]{1,0:T(8,128)(2,1)S(1)}, u32[]{:S(2)}, u32[]{:S(2)}) collective-permute-start(bf16[1152,256]{1,0:T(8,128)(2,1)} %get-tuple-element.265), channel_id=1, source_target_pairs={{0,2},{2,0},{4,6},{6,4},{8,10},{10,8},{12,14},{14,12},{1,3},{3,1},... | collective-permute-start | bytes 1769480 | tf_op jit(solution)/shard_map/ppermute | solution.py:706
  198.2 17.4 %collective-permute-start.35 = (bf16[1152,256]{1,0:T(8,128)(2,1)}, bf16[1152,256]{1,0:T(8,128)(2,1)S(1)}, u32[]{:S(2)}, u32[]{:S(2)}) collective-permute-start(bf16[1152,256]{1,0:T(8,128)(2,1)} %get-tuple-element.266), channel_id=1, source_target_pairs={{0,4},{2,6},{4,0},{6,2},{8,12},{10,14},{12,8},{14,10},{1,5},{3,7},... | collective-permute-start | bytes 1769480 | tf_op jit(solution)/shard_map/ppermute | solution.py:706
  199.6 27.8 %collective-permute-start.36 = (bf16[1152,256]{1,0:T(8,128)(2,1)}, bf16[1152,256]{1,0:T(8,128)(2,1)S(1)}, u32[]{:S(2)}, u32[]{:S(2)}) collective-permute-start(bf16[1152,256]{1,0:T(8,128)(2,1)} %get-tuple-element.267), channel_id=1, source_target_pairs={{0,6},{2,4},{4,2},{6,0},{8,14},{10,12},{12,10},{14,8},{1,7},{3,5},... | collective-permute-start | bytes 1769480 | tf_op jit(solution)/shard_map/ppermute | solution.py:706
  206.4 24.2 %all-to-all-start.4 = ((bf16[16,64,128]{2,1,0:T(8,128)(2,1)}), bf16[16,64,128]{2,1,0:T(8,128)(2,1)S(1)}, u32[]{:S(2)}, u32[]{:S(2)}) async-start(bf16[16,64,128]{2,1,0:T(8,128)(2,1)} %get-tuple-element.263), calls=%async_computation.4 | async-start | bytes 524288 | tf_op jit(solution)/shard_map/all_to_all | solution.py:870
  238.9 30.3 %all-to-all-start.5 = ((bf16[16,64,384]{2,1,0:T(8,128)(2,1)}), bf16[16,64,384]{2,1,0:T(8,128)(2,1)S(1)}, u32[]{:S(2)}, u32[]{:S(2)}) async-start(bf16[16,64,384]{2,1,0:T(8,128)(2,1)} %bitcast.42), calls=%async_computation.5 | async-start | bytes 1572864 | tf_op jit(solution)/shard_map/all_to_all | solution.py:870
  242.8 21.1 %collective-permute-start.41 = (bf16[192,1152]{1,0:T(8,128)(2,1)S(1)}, bf16[192,1152]{1,0:T(8,128)(2,1)}, u32[]{:S(2)}, u32[]{:S(2)}) collective-permute-start(bf16[192,1152]{1,0:T(8,128)(2,1)S(1)} %pad_maximum_fusion.2), channel_id=1, source_target_pairs={{0,2},{2,0},{4,6},{6,4},{8,10},{10,8},{12,14},{14,12},{1,3},{3,1},... | collective-permute-start | bytes 1327112 | tf_op jit(solution)/shard_map/ppermute | solution.py:706
  244.8 13.9 %collective-permute-start.39 = (bf16[2,48,512]{2,1,0:T(8,128)(2,1)S(1)}, bf16[2,48,512]{2,1,0:T(8,128)(2,1)S(1)}, u32[]{:S(2)}, u32[]{:S(2)}) collective-permute-start(bf16[2,48,512]{2,1,0:T(8,128)(2,1)S(1)} %get-tuple-element.286), channel_id=1, source_target_pairs={{0,4},{2,6},{4,0},{6,2},{8,12},{10,14},{12,8},{14,10},{1,5},{3,7},... | collective-permute-start | bytes 294920 | tf_op jit(solution)/shard_map/ppermute | solution.py:706
  269.2 20.3 %all-to-all-start.6 = ((bf16[16,48,384]{2,1,0:T(8,128)(2,1)}), bf16[16,48,384]{2,1,0:T(8,128)(2,1)S(1)}, u32[]{:S(2)}, u32[]{:S(2)}) async-start(bf16[16,48,384]{2,1,0:T(8,128)(2,1)} %bitcast.47), calls=%async_computation.6 | async-start | bytes 1179648 | tf_op jit(solution)/shard_map/all_to_all | solution.py:870
  (65 other events, 642.6 us)
